TPU v7x, 512 devices: a whole 4x8x8 slice. The times are simulated.
512 devices in a mesh: lon: 8 (over y_lo, core), lat: 64 (over x, y_hi, z).
Axes of the slice: x: 4, y: 8 (y_hi: 2, y_lo: 4; y = y_hi * 4 + y_lo), z: 8, core: 2. Of those that a mesh axis runs over, the one named last changes fastest.
Arguments:
- ocean_state: bfloat16 [1, 384, 512, 256], P(None, 'lat', 'lon'), may hold values from -6 to 6
- land_sea: int32 [1, 384, 512], P(None, 'lat', 'lon'), may hold values 0 or 1
- cotangent: bfloat16 [1, 384, 512, 256], P(None, 'lat', 'lon'), may hold values from -6 to 6
- dw_kernel: float32 [7, 7, 256], replicated, may hold values from -0.875 to 0.875
- dw_bias: float32 [256], replicated, may hold values from -3 to 3
- ln_gain: float32 [256], replicated, may hold values from 0.1 to 1.9
- ln_bias: float32 [256], replicated, may hold values from -2 to 2
- w_in: bfloat16 [256, 1024], replicated, may hold values from -0.375 to 0.375
- b_in: float32 [1024], replicated, may hold values from -2 to 2
- w_out: bfloat16 [1024, 256], replicated, may hold values from -0.1875 to 0.1875
- b_out: float32 [256], replicated, may hold values from -2 to 2
- layer_scale: float32 [256], replicated, may hold values from 0.3 to 1.5
Outputs:
- output: bfloat16 [1, 384, 512, 256], P(None, 'lat', 'lon')
- grad_state: bfloat16 [1, 384, 512, 256], P(None, 'lat', 'lon')
- grad_kernel: float32 [7, 7, 256], replicated
- grad_dw_bias: float32 [256], replicated
- grad_ln_gain: float32 [256], replicated
- grad_ln_bias: float32 [256], replicated
- grad_w_in: float32 [256, 1024], replicated
- grad_b_in: float32 [1024], replicated
- grad_w_out: float32 [1024, 256], replicated
- grad_b_out: float32 [256], replicated
- grad_scale: float32 [256], replicated
All inputs are finite; a program needn't handle non-finite values. No bound on the sum of `land_sea` on one device may be relied on, other than what follows from the above.
Results may differ from a plain program's by a relative error of at most 0.0085.
Values may be sent and summed in bfloat16 or wider, within the bound.
No kernel may reach another device: no remote copies, remote signals or barrier semaphores. Data moves between devices by JAX's collectives and lax.ppermute only.
A program may use at most 64 MiB of HBM per device.

v0:
```python
import jax
import jax.numpy as jnp
from jax import lax
from jax.sharding import PartitionSpec as P


def extended(array, sides, width, wrap):
    for axis, dim in sides:
        size, length = (lax.axis_size(axis), array.shape[dim])
        up = [(i, (i + 1) % size) for i in range(size if wrap else size - 1)]
        down = [(j, i) for i, j in up]
        last = lax.slice_in_dim(array, length - width, length, axis=dim)
        leading = lax.slice_in_dim(array, 0, width, axis=dim)
        before = lax.ppermute(last, axis, up)
        after = lax.ppermute(leading, axis, down)
        array = jnp.concatenate([before, array, after], axis=dim)
    return array


def depthwise(padded, kernel, num_rows, num_cols):
    summed = jnp.zeros((padded.shape[0], num_rows, num_cols, padded.shape[3]), jnp.float32)
    for row_off in range(7):
        for col_off in range(7):
            summed = (
                summed
                + padded[:, row_off : row_off + num_rows, col_off : col_off + num_cols, :].astype(
                    jnp.float32
                )
                * kernel[row_off, col_off]
            )
    return summed


def transposed(padded, kernel, num_rows, num_cols):
    summed = jnp.zeros((padded.shape[0], num_rows, num_cols, padded.shape[3]), jnp.float32)
    for row_off in range(7):
        for col_off in range(7):
            summed = (
                summed
                + padded[
                    :, 6 - row_off : 6 - row_off + num_rows, 6 - col_off : 6 - col_off + num_cols, :
                ].astype(jnp.float32)
                * kernel[row_off, col_off]
            )
    return summed


def kernel_terms(padded, grad_depth, num_rows, num_cols):
    grad_float = grad_depth.astype(jnp.float32)
    rows_out = []
    for row_off in range(7):
        cols_out = []
        for col_off in range(7):
            window = padded[
                :, row_off : row_off + num_rows, col_off : col_off + num_cols, :
            ].astype(jnp.float32)
            cols_out.append(jnp.sum(window * grad_float, axis=(0, 1, 2)))
        rows_out.append(jnp.stack(cols_out))
    return jnp.stack(rows_out)


def forward_tokens(depth_out, ln_gain, ln_bias, w_in, b_in, w_out, b_out):
    center = depth_out - jnp.mean(depth_out, axis=-1, keepdims=True)
    inv_std = lax.rsqrt(jnp.mean(center * center, axis=-1, keepdims=True) + 1e-06)
    norm_hat = center * inv_std
    normed = (norm_hat * ln_gain + ln_bias).astype(jnp.bfloat16)
    pre_act = jnp.dot(normed, w_in, preferred_element_type=jnp.float32) + b_in
    activated = jax.nn.gelu(pre_act, approximate=True).astype(jnp.bfloat16)
    branch = jnp.dot(activated, w_out, preferred_element_type=jnp.float32) + b_out
    return (norm_hat, inv_std, normed, pre_act, activated, branch)


def backward_tokens(masked, norm_hat, inv_std, pre_act, ln_gain, w_in, w_out, layer_scale):
    grad_branch = (masked * layer_scale).astype(jnp.bfloat16)
    grad_act = lax.dot_general(
        grad_branch, w_out, (((1,), (1,)), ((), ())), preferred_element_type=jnp.float32
    )
    unused, pull_back = jax.vjp(lambda v: jax.nn.gelu(v, approximate=True), pre_act)
    grad_pre = pull_back(grad_act)[0].astype(jnp.bfloat16)
    grad_norm = lax.dot_general(
        grad_pre, w_in, (((1,), (1,)), ((), ())), preferred_element_type=jnp.float32
    )
    scaled = grad_norm * ln_gain
    grad_depth = (
        inv_std
        * (
            scaled
            - jnp.mean(scaled, axis=-1, keepdims=True)
            - norm_hat * jnp.mean(scaled * norm_hat, axis=-1, keepdims=True)
        )
    ).astype(jnp.bfloat16)
    return (grad_branch, grad_pre, grad_norm, grad_depth)


def weight_terms(masked, branch, grad_branch, activated, normed, grad_pre, grad_norm, norm_hat):
    dims = (((0,), (0,)), ((), ()))
    grad_w_in = lax.dot_general(normed, grad_pre, dims, preferred_element_type=jnp.float32)
    grad_w_out = lax.dot_general(activated, grad_branch, dims, preferred_element_type=jnp.float32)
    return (
        grad_w_in,
        grad_w_out,
        jnp.sum(grad_pre.astype(jnp.float32), axis=0),
        jnp.sum(grad_branch.astype(jnp.float32), axis=0),
        jnp.sum(masked * branch, axis=0),
        jnp.sum(grad_norm * norm_hat, axis=0),
        jnp.sum(grad_norm, axis=0),
    )


def local(
    ocean_state,
    land_sea,
    cotangent,
    dw_kernel,
    dw_bias,
    ln_gain,
    ln_bias,
    w_in,
    b_in,
    w_out,
    b_out,
    layer_scale,
):
    num_batch, num_rows, num_cols, channels = ocean_state.shape
    mask_float = land_sea.astype(jnp.float32)[..., None]
    lon_ext = extended(ocean_state, (("lon", 2),), 3, True)
    padded = extended(lon_ext, (("lat", 1),), 3, False)
    depth_out = depthwise(padded, dw_kernel, num_rows, num_cols) + dw_bias
    masked = (mask_float * cotangent.astype(jnp.float32)).reshape(-1, channels)
    norm_hat, inv_std, normed, pre_act, activated, branch = forward_tokens(
        depth_out.reshape(-1, channels), ln_gain, ln_bias, w_in, b_in, w_out, b_out
    )
    grad_branch, grad_pre, grad_norm, grad_flat = backward_tokens(
        masked, norm_hat, inv_std, pre_act, ln_gain, w_in, w_out, layer_scale
    )
    grad_terms = weight_terms(
        masked, branch, grad_branch, activated, normed, grad_pre, grad_norm, norm_hat
    )
    grad_depth = grad_flat.reshape(num_batch, num_rows, num_cols, channels)
    grad_ext = extended(grad_depth, (("lon", 2),), 3, True)
    grad_pad = extended(grad_ext, (("lat", 1),), 3, False)
    branch_own = branch.reshape(num_batch, num_rows, num_cols, channels)
    output = (ocean_state.astype(jnp.float32) + mask_float * layer_scale * branch_own).astype(
        jnp.bfloat16
    )
    grad_state = (
        cotangent.astype(jnp.float32) + transposed(grad_pad, dw_kernel, num_rows, num_cols)
    ).astype(jnp.bfloat16)
    kernel_part = kernel_terms(padded, grad_depth, num_rows, num_cols)
    bias_part = jnp.sum(grad_depth.astype(jnp.float32), axis=(0, 1, 2))
    grad_w_in, grad_w_out, grad_b_in, grad_b_out, grad_scale, grad_ln_gain, grad_ln_bias = (
        grad_terms
    )
    reduced = lax.psum(
        (
            grad_w_in,
            grad_w_out,
            grad_b_in,
            grad_b_out,
            grad_scale,
            grad_ln_gain,
            grad_ln_bias,
            kernel_part,
            bias_part,
        ),
        ("lon", "lat"),
    )
    (
        grad_w_in,
        grad_w_out,
        grad_b_in,
        grad_b_out,
        grad_scale,
        grad_ln_gain,
        grad_ln_bias,
        kernel_part,
        bias_part,
    ) = reduced
    all_cells = num_batch * num_rows * num_cols * lax.axis_size("lon") * lax.axis_size("lat")
    factor = 1.0 / jnp.sqrt(jnp.float32(all_cells))
    return (
        output,
        grad_state,
        kernel_part * factor,
        bias_part * factor,
        grad_ln_gain * factor,
        grad_ln_bias * factor,
        grad_w_in * factor,
        grad_b_in * factor,
        grad_w_out * factor,
        grad_b_out * factor,
        grad_scale * factor,
    )


def solution(mesh):
    in_specs = (
        P(None, "lat", "lon", None),
        P(None, "lat", "lon"),
        P(None, "lat", "lon", None),
        P(),
        P(),
        P(),
        P(),
        P(),
        P(),
        P(),
        P(),
        P(),
    )
    out_specs = (
        P(None, "lat", "lon", None),
        P(None, "lat", "lon", None),
        P(),
        P(),
        P(),
        P(),
        P(),
        P(),
        P(),
        P(),
        P(),
    )
    return jax.shard_map(local, mesh=mesh, in_specs=in_specs, out_specs=out_specs, check_vma=False)
```

profile of v0, /device:TPU:1, one launch (start us, length us, event | category | flops | bytes accessed | tf_op | source)
XLA Modules:
  0.0 450.9 jit_solution(3544239886626899903)
XLA Ops:
  7.3 0.8 fusion.147
  8.1 8.8 %collective-permute-start.1 = (bf16[1,6,3,256]{3,2,1,0:T(4,128)(2,1)S(1)}, bf16[1,6,3,256]{3,2,1,0:T(4,128)(2,1)S(1)}, u32[]{:S(2)}, u32[]{:S(2)}) collective-permute-start(bf16[1,6,3,256]{3,2,1,0:T(4,128)(2,1)S(1)} %get-tuple-element.102), channel_id=1, source_target_pairs={{64,0},{128,64},{192,128},{256,192},{320,256},{384,320},{448,384},... | collective-permute-start | bytes 27656 | tf_op jit(solution)/shard_map/ppermute | solution.py:15
  16.9 1.9 collective-permute-start
  18.8 0.9 fusion.150
  19.8 1.0 fusion.148
  20.8 1.0 fusion.149
  21.8 0.9 constant_dynamic-update-slice_fusion.1
  22.7 0.7 convert_element_type.400
  23.4 1.0 pad_maximum_fusion.2
  24.5 1.3 collective-permute-start.2
  25.8 1.3 collective-permute-start.3
  27.5 3.8 collective-permute-done.3
  31.4 3.2 fusion.142
  35.7 0.6 convolution_add_fusion.1
  36.6 0.9 convert_reduce_fusion.1
  37.6 1.3 convert_reduce_fusion
  39.7 0.8 fusion.102
  40.5 0.8 fusion.130
  41.2 1.4 fusion.151
  42.7 1.7 fusion.141
  44.4 3.6 collective-permute-start.4
  48.0 2.6 collective-permute-start.5
  50.6 0.7 fusion.129
  51.6 111.9 %all-reduce = (f32[7,7,256]{2,1,0:T(8,128)S(1)}, f32[256]{0:T(256)S(1)}, f32[256]{0:T(256)S(1)}, f32[256]{0:T(256)S(1)}, f32[1024]{0:T(1024)S(1)}, /*index=5*/f32[256]{0:T(256)S(1)}, f32[256]{0:T(256)S(1)}) all-reduce(f32[7,7,256]{2,1,0:T(8,128)S(1)} %constant_dynamic-update-slice_fusion.2, ...), channel_id=1, replica_groups=mesh['lon'=8,'lat'=64] {'lon','lat'}, use_global_device_ids=true, to_apply=%region_53.0 | all-reduce | flops 14848 | bytes 118784 | tf_op jit(solution)/shard_map/psum | solution.py:154
  163.5 0.6 broadcast_multiply_fusion.2
  167.1 1.3 collective-permute-start.6
  168.4 4.0 collective-permute-start.7
  173.0 1.2 collective-permute-done.7
  174.3 3.8 fusion.55
  178.0 262.5 %all-reduce.4.cloned.1.call-done = (f32[256,1024]{1,0:T(8,128)}, f32[1024,256]{1,0:T(8,128)}) async-done(((f32[256,1024]{1,0:T(8,128)}, f32[1024,256]{1,0:T(8,128)}), (f32[256,1024]{1,0:T(8,128)}, f32[1024,256]{1,0:T(8,128)})) %all-reduce.4.cloned.1.call-update) | async-done | bytes 2097168 | tf_op jit(solution)/shard_map/psum | solution.py:154
  440.5 2.4 broadcast_multiply_fusion.1
  443.0 1.1 broadcast_multiply_fusion
  (69 shorter events, 6.7 us)
Async XLA Ops:
  7.2 28.0 %copy-start = (bf16[256,1024]{1,0:T(8,128)(2,1)S(1)}, bf16[256,1024]{1,0:T(8,128)(2,1)}, u32[]{:S(2)}) copy-start(bf16[256,1024]{1,0:T(8,128)(2,1)} %param.19) | copy-start | bytes 1572868
  7.2 24.1 %copy-start.1 = (bf16[1,6,64,256]{3,2,1,0:T(8,128)(2,1)S(1)}, bf16[1,6,64,256]{3,2,1,0:T(8,128)(2,1)}, u32[]{:S(2)}) copy-start(bf16[1,6,64,256]{3,2,1,0:T(8,128)(2,1)} %param.12) | copy-start | bytes 589828
  7.2 24.1 %copy-start.8 = (f32[256]{0:T(256)S(1)}, f32[256]{0:T(256)}, u32[]{:S(2)}) copy-start(f32[256]{0:T(256)} %param.16) | copy-start | bytes 3076
  7.2 433.3 %all-reduce.4.cloned.1.call-start = ((), (), s32[]{:S(2)}) async-start(), calls=%async_computation | async-start | bytes 4194304 | tf_op jit(solution)/shard_map/psum | solution.py:154
  8.1 15.3 %collective-permute-start.1 = (bf16[1,6,3,256]{3,2,1,0:T(4,128)(2,1)S(1)}, bf16[1,6,3,256]{3,2,1,0:T(4,128)(2,1)S(1)}, u32[]{:S(2)}, u32[]{:S(2)}) collective-permute-start(bf16[1,6,3,256]{3,2,1,0:T(4,128)(2,1)S(1)} %get-tuple-element.102), channel_id=1, source_target_pairs={{64,0},{128,64},{192,128},{256,192},{320,256},{384,320},{448,384},... | collective-permute-start | bytes 27656 | tf_op jit(solution)/shard_map/ppermute | solution.py:15
  16.9 6.5 %collective-permute-start = (bf16[1,6,3,256]{3,2,1,0:T(4,128)(2,1)S(1)}, bf16[1,6,3,256]{3,2,1,0:T(4,128)(2,1)S(1)}, u32[]{:S(2)}, u32[]{:S(2)}) collective-permute-start(bf16[1,6,3,256]{3,2,1,0:T(4,128)(2,1)S(1)} %get-tuple-element.101), channel_id=1, source_target_pairs={{0,64},{64,128},{128,192},{192,256},{256,320},{320,384},{384,448},... | collective-permute-start | bytes 27656 | tf_op jit(solution)/shard_map/ppermute | solution.py:14
  24.5 3.0 collective-permute-start.2
  25.8 5.5 %collective-permute-start.3 = (bf16[1,3,70,256]{3,2,1,0:T(8,128)(2,1)S(1)}, bf16[1,3,70,256]{3,2,1,0:T(8,128)(2,1)S(1)}, u32[]{:S(2)}, u32[]{:S(2)}) collective-permute-start(bf16[1,3,70,256]{3,2,1,0:T(8,128)(2,1)S(1)} %get-tuple-element.96), channel_id=1, source_target_pairs={{1,0},{2,1},{3,2},{4,3},{5,4},{6,5},{7,6},{8,7},{9,8},{10,9},{11,1... | collective-permute-start | bytes 322568 | tf_op jit(solution)/shard_map/ppermute | solution.py:15
  31.4 3.6 copy-start.5
  31.4 3.6 copy-start.7
  31.4 3.8 copy-start.4
  34.6 1.0 copy-start.9
  34.6 1.0 copy-start.10
  35.7 0.9 copy-start.3
  35.7 0.9 copy-start.6
  44.4 122.7 %collective-permute-start.4 = (bf16[1,6,3,256]{3,2,1,0:T(4,128)(2,1)S(1)}, bf16[1,6,3,256]{3,2,1,0:T(4,128)(2,1)S(1)}, u32[]{:S(2)}, u32[]{:S(2)}) collective-permute-start(bf16[1,6,3,256]{3,2,1,0:T(4,128)(2,1)S(1)} %get-tuple-element.100), channel_id=1, source_target_pairs={{0,64},{64,128},{128,192},{192,256},{256,320},{320,384},{384,448},... | collective-permute-start | bytes 27656 | tf_op jit(solution)/shard_map/ppermute | solution.py:14
  48.0 119.0 %collective-permute-start.5 = (bf16[1,6,3,256]{3,2,1,0:T(4,128)(2,1)S(1)}, bf16[1,6,3,256]{3,2,1,0:T(4,128)(2,1)S(1)}, u32[]{:S(2)}, u32[]{:S(2)}) collective-permute-start(bf16[1,6,3,256]{3,2,1,0:T(4,128)(2,1)S(1)} %get-tuple-element.99), channel_id=1, source_target_pairs={{64,0},{128,64},{192,128},{256,192},{320,256},{384,320},{448,384},... | collective-permute-start | bytes 27656 | tf_op jit(solution)/shard_map/ppermute | solution.py:15
  167.1 5.9 %collective-permute-start.6 = (bf16[1,3,70,256]{3,2,1,0:T(8,128)(2,1)S(1)}, bf16[1,3,70,256]{3,2,1,0:T(8,128)(2,1)S(1)}, u32[]{:S(2)}, u32[]{:S(2)}) collective-permute-start(bf16[1,3,70,256]{3,2,1,0:T(8,128)(2,1)S(1)} %get-tuple-element.91), channel_id=1, source_target_pairs={{1,0},{2,1},{3,2},{4,3},{5,4},{6,5},{7,6},{8,7},{9,8},{10,9},{11,1... | collective-permute-start | bytes 322568 | tf_op jit(solution)/shard_map/ppermute | solution.py:15
  168.4 5.7 %collective-permute-start.7 = (bf16[1,3,70,256]{3,2,1,0:T(8,128)(2,1)S(1)}, bf16[1,3,70,256]{3,2,1,0:T(8,128)(2,1)S(1)}, u32[]{:S(2)}, u32[]{:S(2)}) collective-permute-start(bf16[1,3,70,256]{3,2,1,0:T(8,128)(2,1)S(1)} %get-tuple-element.92), channel_id=1, source_target_pairs={{0,1},{1,2},{2,3},{3,4},{4,5},{5,6},{6,7},{7,8},{8,9},{9,10},{10,1... | collective-permute-start | bytes 322568 | tf_op jit(solution)/shard_map/ppermute | solution.py:14
  440.5 2.4 copy-start.2
Sparse Core Ops, SparseCore 0:
  167.1 273.3 all-reduce.3
where the time goes:
time: 452 us; the launch traced here: 451 us
  waiting for transfers between devices  268 us (59%)
  blocking collectives  112 us (25%)
  starting transfers between devices  24.9 us (6%)
  other arithmetic  20.3 us (4%)
  between operations  14.4 us (3%)
  matrix products  5.94 us (1%)
  local copies, waits for them, and re-layouts  5.65 us (1%)
    psum x1, waiting for transfers between devices, local(): lax.psum((grad_w_in, grad_w_out, grad_b_in, grad_b_out, grad_scale, grad_...  262 us
    psum x1, blocking collectives, local(): lax.psum((grad_w_in, grad_w_out, grad_b_in, grad_b_out, grad_scale, grad_...  112 us
    ppermute x4, starting transfers between devices, extended(): after = lax.ppermute(leading, axis, down)  14 us
    ppermute x4, starting transfers between devices, extended(): before = lax.ppermute(last, axis, up)  10.9 us
  transfers between devices with their start and end apart: 9, of which 4 were waited for; matrix products, arithmetic and copies ran while one was open for 3% of the time, Pallas kernels for 0%

commit v1 on v0

--- a/solution.py
+++ b/solution.py
@@ -1,7 +1,26 @@
 import jax
 import jax.numpy as jnp
+import numpy as np
 from jax import lax
-from jax.sharding import PartitionSpec as P
+from jax.sharding import Mesh, PartitionSpec as P
+
+LON = ("y_lo", "core")
+LAT = ("x", "y_hi", "z")
+FAR = ("x", "y_hi", "y_lo", "z")
+
+
+def whole_sum(chunks):
+    far = lax.axis_size(FAR)
+    pair = chunks.astype(jnp.bfloat16).reshape(2, far * 5, 256)
+    pair = lax.all_to_all(pair, "core", 0, 0)
+    value = (pair[0].astype(jnp.float32) + pair[1].astype(jnp.float32)).astype(jnp.bfloat16)
+    value = lax.all_to_all(value.reshape(far, 2, 640), FAR, 0, 0)
+    value = jnp.sum(value.astype(jnp.float32), axis=0).astype(jnp.bfloat16)
+    value = lax.all_to_all(jnp.broadcast_to(value[None], (far, 2, 640)), FAR, 0, 0)
+    mine = value.reshape(far, 5, 256)
+    other = lax.ppermute(mine, "core", [(0, 1), (1, 0)])
+    is_first = lax.axis_index("core") == 0
+    return jnp.where(is_first, mine, other), jnp.where(is_first, other, mine)
 
 
 def extended(array, sides, width, wrap):
@@ -123,8 +142,8 @@
 ):
     num_batch, num_rows, num_cols, channels = ocean_state.shape
     mask_float = land_sea.astype(jnp.float32)[..., None]
-    lon_ext = extended(ocean_state, (("lon", 2),), 3, True)
-    padded = extended(lon_ext, (("lat", 1),), 3, False)
+    lon_ext = extended(ocean_state, ((LON, 2),), 3, True)
+    padded = extended(lon_ext, ((LAT, 1),), 3, False)
     depth_out = depthwise(padded, dw_kernel, num_rows, num_cols) + dw_bias
     masked = (mask_float * cotangent.astype(jnp.float32)).reshape(-1, channels)
     norm_hat, inv_std, normed, pre_act, activated, branch = forward_tokens(
@@ -137,8 +156,8 @@
         masked, branch, grad_branch, activated, normed, grad_pre, grad_norm, norm_hat
     )
     grad_depth = grad_flat.reshape(num_batch, num_rows, num_cols, channels)
-    grad_ext = extended(grad_depth, (("lon", 2),), 3, True)
-    grad_pad = extended(grad_ext, (("lat", 1),), 3, False)
+    grad_ext = extended(grad_depth, ((LON, 2),), 3, True)
+    grad_pad = extended(grad_ext, ((LAT, 1),), 3, False)
     branch_own = branch.reshape(num_batch, num_rows, num_cols, channels)
     output = (ocean_state.astype(jnp.float32) + mask_float * layer_scale * branch_own).astype(
         jnp.bfloat16
@@ -151,53 +170,57 @@
     grad_w_in, grad_w_out, grad_b_in, grad_b_out, grad_scale, grad_ln_gain, grad_ln_bias = (
         grad_terms
     )
-    reduced = lax.psum(
-        (
-            grad_w_in,
-            grad_w_out,
-            grad_b_in,
-            grad_b_out,
-            grad_scale,
-            grad_ln_gain,
-            grad_ln_bias,
-            kernel_part,
-            bias_part,
-        ),
-        ("lon", "lat"),
-    )
-    (
-        grad_w_in,
-        grad_w_out,
-        grad_b_in,
-        grad_b_out,
-        grad_scale,
-        grad_ln_gain,
-        grad_ln_bias,
-        kernel_part,
-        bias_part,
-    ) = reduced
-    all_cells = num_batch * num_rows * num_cols * lax.axis_size("lon") * lax.axis_size("lat")
+    all_cells = num_batch * num_rows * num_cols * lax.axis_size(LON) * lax.axis_size(LAT)
     factor = 1.0 / jnp.sqrt(jnp.float32(all_cells))
+    hidden = w_in.shape[1]
+    blocks = hidden // channels
+    smalls = (
+        kernel_part.reshape(-1, channels),
+        grad_b_in.reshape(-1, channels),
+        bias_part[None],
+        grad_ln_gain[None],
+        grad_ln_bias[None],
+        grad_b_out[None],
+        grad_scale[None],
+    )
+    parts = [grad_w_in[:, k * channels : (k + 1) * channels] for k in range(blocks)]
+    big_terms = jnp.concatenate(parts + [grad_w_out]).reshape(-1, 4, channels)
+    small_terms = jnp.concatenate(smalls)
+    spare = big_terms.shape[0] - small_terms.shape[0]
+    small_terms = jnp.pad(small_terms, ((0, spare), (0, 0)))[:, None]
+    first, second = whole_sum(jnp.concatenate([big_terms, small_terms], axis=1))
+    total = first[:, :4].reshape(hidden, channels).astype(jnp.float32) * factor
+    grad_w_in = jnp.concatenate(
+        [total[k * channels : (k + 1) * channels] for k in range(blocks)], axis=1
+    )
+    grad_w_out = second[:, :4].reshape(hidden, channels).astype(jnp.float32) * factor
+    total = first[:, 4].astype(jnp.float32) * factor
+    kernel_part = total[:49].reshape(7, 7, channels)
+    at = 49
+    grad_b_in = total[at : at + blocks].reshape(hidden)
+    at += blocks
     return (
         output,
         grad_state,
-        kernel_part * factor,
-        bias_part * factor,
-        grad_ln_gain * factor,
-        grad_ln_bias * factor,
-        grad_w_in * factor,
-        grad_b_in * factor,
-        grad_w_out * factor,
-        grad_b_out * factor,
-        grad_scale * factor,
+        kernel_part,
+        total[at],
+        total[at + 1],
+        total[at + 2],
+        grad_w_in,
+        grad_b_in,
+        grad_w_out,
+        total[at + 3],
+        total[at + 4],
     )
 
 
 def solution(mesh):
+    devices = mesh.devices.reshape(4, 2, 4, 2, 8)
+    mesh = Mesh(devices, ("y_lo", "core", "x", "y_hi", "z"))
     in_specs = (
-        P(None, "lat", "lon", None),
-        P(None, "lat", "lon"),
-        P(None, "lat", "lon", None),
+        P(None, LAT, LON, None),
+        P(None, LAT, LON),
+        P(None, LAT, LON, None),
         P(),
         P(),
         P(),
@@ -209,8 +232,8 @@
         P(),
     )
     out_specs = (
-        P(None, "lat", "lon", None),
-        P(None, "lat", "lon", None),
+        P(None, LAT, LON, None),
+        P(None, LAT, LON, None),
         P(),
         P(),
         P(),

time: 452 us -> 185 us (0.41)
  the two profiles are of different devices: /device:TPU:1 before, /device:TPU:7 now
where the time goes in v1:
time: 185 us; the launch traced here: 184 us
  starting transfers between devices  55.2 us (30%)
  blocking collectives  42.4 us (23%)
  local copies, waits for them, and re-layouts  28.5 us (15%)
  waiting for transfers between devices  25.7 us (14%)
  other arithmetic  22.1 us (12%)
  matrix products  7.3 us (4%)
  between operations  3.32 us (2%)
    all_to_all x1, blocking collectives, whole_sum(): value = lax.all_to_all(value.reshape(far, 2, 640), FAR, 0, 0)  36.6 us
    ppermute x4, starting transfers between devices, extended(): after = lax.ppermute(leading, axis, down)  26.8 us
    ppermute x4, starting transfers between devices, extended(): before = lax.ppermute(last, axis, up)  13.8 us
    ppermute x4, waiting for transfers between devices, extended(): after = lax.ppermute(leading, axis, down)  13.1 us
    ppermute x4, waiting for transfers between devices, extended(): before = lax.ppermute(last, axis, up)  12.6 us
    all_to_all x1, starting transfers between devices, whole_sum(): lax.all_to_all(jnp.broadcast_to(value[None], (far, 2, 640)), FAR, 0, 0)  12 us
    slice x9, local copies, waits for them, and re-layouts, local(): total[k * channels:(k + 1) * channels]  7.03 us
    all_to_all x1, blocking collectives, whole_sum(): pair = lax.all_to_all(pair, 'core', 0, 0)  5.73 us
  transfers between devices with their start and end apart: 10, of which 6 were waited for; matrix products, arithmetic and copies ran while one was open for 6% of the time, Pallas kernels for 0%

profile of v1, /device:TPU:7, one launch (start us, length us, event | category | flops | bytes accessed | tf_op | source)
XLA Modules:
  0.0 184.4 jit_solution(17241710076899631731)
XLA Ops:
  1.5 2.6 %collective-permute-start.1 = (bf16[1,6,3,256]{3,2,1,0:T(4,128)(2,1)S(1)}, bf16[1,6,3,256]{3,2,1,0:T(4,128)(2,1)S(1)}, u32[]{:S(2)}, u32[]{:S(2)}) collective-permute-start(bf16[1,6,3,256]{3,2,1,0:T(4,128)(2,1)S(1)} %get-tuple-element.111), channel_id=1, source_target_pairs={{64,0},{128,64},{192,128},{256,192},{320,256},{384,320},{448,384},... | collective-permute-start | bytes 27656 | tf_op jit(solution)/shard_map/ppermute | solution.py:34
  4.1 3.1 %collective-permute-start = (bf16[1,6,3,256]{3,2,1,0:T(4,128)(2,1)S(1)}, bf16[1,6,3,256]{3,2,1,0:T(4,128)(2,1)S(1)}, u32[]{:S(2)}, u32[]{:S(2)}) collective-permute-start(bf16[1,6,3,256]{3,2,1,0:T(4,128)(2,1)S(1)} %get-tuple-element.110), channel_id=1, source_target_pairs={{0,64},{64,128},{128,192},{192,256},{256,320},{320,384},{384,448},... | collective-permute-start | bytes 27656 | tf_op jit(solution)/shard_map/ppermute | solution.py:33
  9.4 1.6 fusion.152
  15.4 4.0 %collective-permute-start.2 = (bf16[1,3,70,256]{3,2,1,0:T(8,128)(2,1)S(1)}, bf16[1,3,70,256]{3,2,1,0:T(8,128)(2,1)S(1)}, u32[]{:S(2)}, u32[]{:S(2)}) collective-permute-start(bf16[1,3,70,256]{3,2,1,0:T(8,128)(2,1)S(1)} %get-tuple-element.106), channel_id=1, source_target_pairs={{0,1},{1,2},{2,3},{3,4},{4,5},{5,6},{6,7},{7,8},{8,9},{9,10},{10,1... | collective-permute-start | bytes 322568 | tf_op jit(solution)/shard_map/ppermute | solution.py:33
  19.4 14.0 %collective-permute-start.3 = (bf16[1,3,70,256]{3,2,1,0:T(8,128)(2,1)S(1)}, bf16[1,3,70,256]{3,2,1,0:T(8,128)(2,1)S(1)}, u32[]{:S(2)}, u32[]{:S(2)}) collective-permute-start(bf16[1,3,70,256]{3,2,1,0:T(8,128)(2,1)S(1)} %get-tuple-element.107), channel_id=1, source_target_pairs={{1,0},{2,1},{3,2},{4,3},{5,4},{6,5},{7,6},{8,7},{9,8},{10,9},{11,1... | collective-permute-start | bytes 322568 | tf_op jit(solution)/shard_map/ppermute | solution.py:34
  33.5 2.1 %collective-permute-done.2 = bf16[1,3,70,256]{3,2,1,0:T(8,128)(2,1)S(1)} collective-permute-done((bf16[1,3,70,256]{3,2,1,0:T(8,128)(2,1)S(1)}, bf16[1,3,70,256]{3,2,1,0:T(8,128)(2,1)S(1)}, u32[]{:S(2)}, u32[]{:S(2)}) %collective-permute-start.2) | collective-permute-done | bytes 107552 | tf_op jit(solution)/shard_map/ppermute | solution.py:33
  35.5 3.0 %collective-permute-done.3 = bf16[1,3,70,256]{3,2,1,0:T(8,128)(2,1)S(1)} collective-permute-done((bf16[1,3,70,256]{3,2,1,0:T(8,128)(2,1)S(1)}, bf16[1,3,70,256]{3,2,1,0:T(8,128)(2,1)S(1)}, u32[]{:S(2)}, u32[]{:S(2)}) %collective-permute-start.3) | collective-permute-done | bytes 107552 | tf_op jit(solution)/shard_map/ppermute | solution.py:34
  38.7 3.9 %fusion.144 = (f32[6,64]{1,0:T(8,128)S(1)}, f32[1,6,64,256]{3,2,1,0:T(8,128)S(1)}) fusion(f32[256]{0:T(256)S(1)} %copy-done.92, f32[256]{0:T(256)S(1)} %bitcast.138, bf16[1,9,70,256]{3,2,1,0:T(8,128)(2,1)S(1)} %get-tuple-element.105, f32[256]{0:T(256)S(1)} %bitcast.140, f32[256]{0:T(256)S(1)} %bitcast.144, f32[256]{0:T(256)S(1)} %bitcast.146, ...), kind=kLoop, calls=%fused_computation.316 | loop fusion | flops 15433344 | bytes 9499136 | tf_op jit(solution)/shard_map/reduce_sum | solution.py:82
  46.7 1.9 %fusion.154 = (bf16[1024]{0:T(1024)(128)(2,1)}, bf16[384,1024]{1,0:T(8,128)(2,1)S(1)}) fusion(f32[384,1024]{1,0:T(8,128)S(1)} %convolution_add_fusion, bf16[384,256]{1,0:T(8,128)(2,1)S(1)} %get-tuple-element.99, bf16[1024,256]{1,0:T(8,128)(2,1)S(1)} %copy-done.128), kind=kOutput, calls=%fused_computation.325 | convolution fusion | flops 209583104 | bytes 3082240 | tf_op jit(solution)/shard_map/dot_general | solution.py:94
  50.5 1.4 fusion.103
  51.8 1.4 fusion.131
  59.3 2.9 %fusion.7 = bf16[2048,256]{1,0:T(8,128)(2,1)} fusion(bf16[2048,256]{1,0:T(8,128)(2,1)} %slice_dynamic-update-slice_fusion, bf16[384,256]{1,0:T(8,128)(2,1)S(1)} %get-tuple-element.99, f32[384,1024]{1,0:T(8,128)} %copy-done.5), kind=kOutput, calls=%fused_computation.65 | convolution fusion | flops 205127680 | bytes 2293760 | tf_op jit(solution)/shard_map/dot_general | solution.py:117
  62.2 2.1 %reshape.342 = bf16[512,4,256]{2,1,0:T(4,128)(2,1)} reshape(bf16[2048,256]{1,0:T(8,128)(2,1)} %fusion.7) | data formatting | bytes 2097152 | tf_op jit(solution)/shard_map/reshape | solution.py:187
  64.3 2.2 %pad_maximum_fusion = bf16[512,5,256]{2,1,0:T(8,128)(2,1)S(1)} fusion(bf16[512,1,256]{2,1,0:T(2,128)(2,1)S(1)} %copy.33, bf16[512,4,256]{2,1,0:T(4,128)(2,1)} %reshape.342), kind=kLoop, calls=%fused_computation.52 | loop fusion | flops 2621440 | bytes 2621440 | tf_op jit(solution)/shard_map/concatenate | solution.py:191
  66.6 1.4 convert_element_type.548
  68.0 5.7 %all_to_all.15 = bf16[2,1280,256]{2,1,0:T(8,128)(2,1)S(1)} all-to-all(bf16[2,1280,256]{2,1,0:T(8,128)(2,1)} %convert_element_type.548), channel_id=1, replica_groups=mesh['y_lo'=4,'core'=2,'x'=4,'y_hi'=2,'z'=8] {'core'}, dimensions={0} | all-to-all | bytes 2621440 | tf_op jit(solution)/shard_map/all_to_all | solution.py:15
  74.3 36.6 %all_to_all.16 = bf16[256,2,640]{2,1,0:T(2,128)(2,1)S(1)} all-to-all(bf16[256,2,640]{2,1,0:T(2,128)(2,1)S(1)} %convert_element_type.552), channel_id=1, replica_groups=mesh['y_lo'=4,'core'=2,'x'=4,'y_hi'=2,'z'=8] {'x','y_hi','y_lo','z'}, dimensions={0} | all-to-all | bytes 1310720 | tf_op jit(solution)/shard_map/all_to_all | solution.py:17
  111.6 1.2 broadcast_in_dim.49
  112.7 12.0 %all-to-all-start.2 = ((bf16[256,2,640]{2,1,0:T(2,128)(2,1)}), bf16[256,2,640]{2,1,0:T(2,128)(2,1)S(1)}, u32[]{:S(2)}, u32[]{:S(2)}) async-start(bf16[256,2,640]{2,1,0:T(2,128)(2,1)} %broadcast_in_dim.49), calls=%async_computation.2 | async-start | bytes 1310720 | tf_op jit(solution)/shard_map/all_to_all | solution.py:19
  124.7 4.8 %collective-permute-start.4 = (bf16[1,6,3,256]{3,2,1,0:T(4,128)(2,1)S(1)}, bf16[1,6,3,256]{3,2,1,0:T(4,128)(2,1)S(1)}, u32[]{:S(2)}, u32[]{:S(2)}) collective-permute-start(bf16[1,6,3,256]{3,2,1,0:T(4,128)(2,1)S(1)} %get-tuple-element.109), channel_id=1, source_target_pairs={{0,64},{64,128},{128,192},{192,256},{256,320},{320,384},{384,448},... | collective-permute-start | bytes 27656 | tf_op jit(solution)/shard_map/ppermute | solution.py:33
  129.9 1.9 %collective-permute-start.5 = (bf16[1,6,3,256]{3,2,1,0:T(4,128)(2,1)S(1)}, bf16[1,6,3,256]{3,2,1,0:T(4,128)(2,1)S(1)}, u32[]{:S(2)}, u32[]{:S(2)}) collective-permute-start(bf16[1,6,3,256]{3,2,1,0:T(4,128)(2,1)S(1)} %get-tuple-element.108), channel_id=1, source_target_pairs={{64,0},{128,64},{192,128},{256,192},{320,256},{384,320},{448,384},... | collective-permute-start | bytes 27656 | tf_op jit(solution)/shard_map/ppermute | solution.py:34
  132.1 7.7 %collective-permute-done.5 = bf16[1,6,3,256]{3,2,1,0:T(4,128)(2,1)S(1)} collective-permute-done((bf16[1,6,3,256]{3,2,1,0:T(4,128)(2,1)S(1)}, bf16[1,6,3,256]{3,2,1,0:T(4,128)(2,1)S(1)}, u32[]{:S(2)}, u32[]{:S(2)}) %collective-permute-start.5) | collective-permute-done | bytes 9248 | tf_op jit(solution)/shard_map/ppermute | solution.py:34
  139.9 8.3 %collective-permute-start.6 = (bf16[1,3,70,256]{3,2,1,0:T(8,128)(2,1)S(1)}, bf16[1,3,70,256]{3,2,1,0:T(8,128)(2,1)S(1)}, u32[]{:S(2)}, u32[]{:S(2)}) collective-permute-start(bf16[1,3,70,256]{3,2,1,0:T(8,128)(2,1)S(1)} %get-tuple-element.102), channel_id=1, source_target_pairs={{1,0},{2,1},{3,2},{4,3},{5,4},{6,5},{7,6},{8,7},{9,8},{10,9},{11,1... | collective-permute-start | bytes 322568 | tf_op jit(solution)/shard_map/ppermute | solution.py:34
  148.3 1.9 %collective-permute-start.7 = (bf16[1,3,70,256]{3,2,1,0:T(8,128)(2,1)S(1)}, bf16[1,3,70,256]{3,2,1,0:T(8,128)(2,1)S(1)}, u32[]{:S(2)}, u32[]{:S(2)}) collective-permute-start(bf16[1,3,70,256]{3,2,1,0:T(8,128)(2,1)S(1)} %get-tuple-element.103), channel_id=1, source_target_pairs={{0,1},{1,2},{2,3},{3,4},{4,5},{5,6},{6,7},{7,8},{8,9},{9,10},{10,1... | collective-permute-start | bytes 322568 | tf_op jit(solution)/shard_map/ppermute | solution.py:33
  150.2 2.4 %collective-permute-done.6 = bf16[1,3,70,256]{3,2,1,0:T(8,128)(2,1)S(1)} collective-permute-done((bf16[1,3,70,256]{3,2,1,0:T(8,128)(2,1)S(1)}, bf16[1,3,70,256]{3,2,1,0:T(8,128)(2,1)S(1)}, u32[]{:S(2)}, u32[]{:S(2)}) %collective-permute-start.6) | collective-permute-done | bytes 107552 | tf_op jit(solution)/shard_map/ppermute | solution.py:34
  152.6 10.2 %collective-permute-done.7 = bf16[1,3,70,256]{3,2,1,0:T(8,128)(2,1)S(1)} collective-permute-done((bf16[1,3,70,256]{3,2,1,0:T(8,128)(2,1)S(1)}, bf16[1,3,70,256]{3,2,1,0:T(8,128)(2,1)S(1)}, u32[]{:S(2)}, u32[]{:S(2)}) %collective-permute-start.7) | collective-permute-done | bytes 107552 | tf_op jit(solution)/shard_map/ppermute | solution.py:33
  164.0 2.6 %collective-permute-start.8 = (bf16[256,5,256]{0,2,1:T(8,128)(2,1)S(1)}, bf16[256,5,256]{0,2,1:T(8,128)(2,1)S(1)}, u32[]{:S(2)}, u32[]{:S(2)}) collective-permute-start(bf16[256,5,256]{0,2,1:T(8,128)(2,1)S(1)} %bitcast.113), channel_id=1, source_target_pairs={{0,64},{64,0},{1,65},{65,1},{2,66},{66,2},{3,67},{67,3},{4,68},{68... | collective-permute-start | bytes 1966088 | tf_op jit(solution)/shard_map/ppermute | solution.py:21
  167.0 4.6 %fusion.56 = bf16[1,6,64,256]{3,2,1,0:T(8,128)(2,1)} fusion(bf16[1,6,64,256]{3,2,1,0:T(8,128)(2,1)S(1)} %copy-done.4, bf16[1,6,64,256]{3,2,1,0:T(8,128)(2,1)S(1)} %bitcast.112, bf16[1,6,3,256]{3,2,1,0:T(4,128)(2,1)S(1)} %collective-permute-done.4, bf16[1,6,3,256]{3,2,1,0:T(4,128)(2,1)S(1)} %collective-permute-done.5, ...), kind=kLoop, calls=%fused_computation.172 | loop fusion | flops 16416768 | bytes 8915968 | tf_op jit(solution)/shard_map/convert_element_type | solution.py:167
  173.6 1.6 fusion.146
  175.2 1.3 copy.39
  177.4 1.2 copy.38
  182.0 1.3 mul.1388
  (399 shorter events, 28.1 us)
Async XLA Ops:
  0.6 42.9 %copy-start = (bf16[256,1024]{1,0:T(8,128)(2,1)S(1)}, bf16[256,1024]{1,0:T(8,128)(2,1)}, u32[]{:S(2)}) copy-start(bf16[256,1024]{1,0:T(8,128)(2,1)} %param.19) | copy-start | bytes 1572868
  0.7 37.9 %copy-start.1 = (bf16[1,6,64,256]{3,2,1,0:T(8,128)(2,1)S(1)}, bf16[1,6,64,256]{3,2,1,0:T(8,128)(2,1)}, u32[]{:S(2)}) copy-start(bf16[1,6,64,256]{3,2,1,0:T(8,128)(2,1)} %param.12) | copy-start | bytes 589828
  0.7 38.0 %copy-start.92 = (f32[256]{0:T(256)S(1)}, f32[256]{0:T(256)}, u32[]{:S(2)}) copy-start(f32[256]{0:T(256)} %param.16) | copy-start | bytes 3076
  1.5 12.9 %collective-permute-start.1 = (bf16[1,6,3,256]{3,2,1,0:T(4,128)(2,1)S(1)}, bf16[1,6,3,256]{3,2,1,0:T(4,128)(2,1)S(1)}, u32[]{:S(2)}, u32[]{:S(2)}) collective-permute-start(bf16[1,6,3,256]{3,2,1,0:T(4,128)(2,1)S(1)} %get-tuple-element.111), channel_id=1, source_target_pairs={{64,0},{128,64},{192,128},{256,192},{320,256},{384,320},{448,384},... | collective-permute-start | bytes 27656 | tf_op jit(solution)/shard_map/ppermute | solution.py:34
  4.1 10.3 %collective-permute-start = (bf16[1,6,3,256]{3,2,1,0:T(4,128)(2,1)S(1)}, bf16[1,6,3,256]{3,2,1,0:T(4,128)(2,1)S(1)}, u32[]{:S(2)}, u32[]{:S(2)}) collective-permute-start(bf16[1,6,3,256]{3,2,1,0:T(4,128)(2,1)S(1)} %get-tuple-element.110), channel_id=1, source_target_pairs={{0,64},{64,128},{128,192},{192,256},{256,320},{320,384},{384,448},... | collective-permute-start | bytes 27656 | tf_op jit(solution)/shard_map/ppermute | solution.py:33
  15.4 20.1 %collective-permute-start.2 = (bf16[1,3,70,256]{3,2,1,0:T(8,128)(2,1)S(1)}, bf16[1,3,70,256]{3,2,1,0:T(8,128)(2,1)S(1)}, u32[]{:S(2)}, u32[]{:S(2)}) collective-permute-start(bf16[1,3,70,256]{3,2,1,0:T(8,128)(2,1)S(1)} %get-tuple-element.106), channel_id=1, source_target_pairs={{0,1},{1,2},{2,3},{3,4},{4,5},{5,6},{6,7},{7,8},{8,9},{9,10},{10,1... | collective-permute-start | bytes 322568 | tf_op jit(solution)/shard_map/ppermute | solution.py:33
  19.4 19.1 %collective-permute-start.3 = (bf16[1,3,70,256]{3,2,1,0:T(8,128)(2,1)S(1)}, bf16[1,3,70,256]{3,2,1,0:T(8,128)(2,1)S(1)}, u32[]{:S(2)}, u32[]{:S(2)}) collective-permute-start(bf16[1,3,70,256]{3,2,1,0:T(8,128)(2,1)S(1)} %get-tuple-element.107), channel_id=1, source_target_pairs={{1,0},{2,1},{3,2},{4,3},{5,4},{6,5},{7,6},{8,7},{9,8},{10,9},{11,1... | collective-permute-start | bytes 322568 | tf_op jit(solution)/shard_map/ppermute | solution.py:34
  112.7 50.1 %all-to-all-start.2 = ((bf16[256,2,640]{2,1,0:T(2,128)(2,1)}), bf16[256,2,640]{2,1,0:T(2,128)(2,1)S(1)}, u32[]{:S(2)}, u32[]{:S(2)}) async-start(bf16[256,2,640]{2,1,0:T(2,128)(2,1)} %broadcast_in_dim.49), calls=%async_computation.2 | async-start | bytes 1310720 | tf_op jit(solution)/shard_map/all_to_all | solution.py:19
  124.7 7.4 %collective-permute-start.4 = (bf16[1,6,3,256]{3,2,1,0:T(4,128)(2,1)S(1)}, bf16[1,6,3,256]{3,2,1,0:T(4,128)(2,1)S(1)}, u32[]{:S(2)}, u32[]{:S(2)}) collective-permute-start(bf16[1,6,3,256]{3,2,1,0:T(4,128)(2,1)S(1)} %get-tuple-element.109), channel_id=1, source_target_pairs={{0,64},{64,128},{128,192},{192,256},{256,320},{320,384},{384,448},... | collective-permute-start | bytes 27656 | tf_op jit(solution)/shard_map/ppermute | solution.py:33
  129.5 37.1 %copy-start.11 = (f32[1,1,256]{2,1,0:T(1,128)S(1)}, f32[1,1,256]{2,1,0:T(1,128)}, u32[]{:S(2)}) copy-start(f32[1,1,256]{2,1,0:T(1,128)} %copy-done.10) | copy-start | bytes 3076
  129.5 37.1 %copy-start.13 = (f32[1,1,256]{2,1,0:T(1,128)S(1)}, f32[1,1,256]{2,1,0:T(1,128)}, u32[]{:S(2)}) copy-start(f32[1,1,256]{2,1,0:T(1,128)} %copy-done.12) | copy-start | bytes 3076
  129.5 37.1 %copy-start.15 = (f32[1,1,256]{2,1,0:T(1,128)S(1)}, f32[1,1,256]{2,1,0:T(1,128)}, u32[]{:S(2)}) copy-start(f32[1,1,256]{2,1,0:T(1,128)} %copy-done.14) | copy-start | bytes 3076
  129.6 37.1 %copy-start.17 = (f32[1,1,256]{2,1,0:T(1,128)S(1)}, f32[1,1,256]{2,1,0:T(1,128)}, u32[]{:S(2)}) copy-start(f32[1,1,256]{2,1,0:T(1,128)} %copy-done.16) | copy-start | bytes 3076
  129.6 37.1 %copy-start.19 = (f32[1,1,256]{2,1,0:T(1,128)S(1)}, f32[1,1,256]{2,1,0:T(1,128)}, u32[]{:S(2)}) copy-start(f32[1,1,256]{2,1,0:T(1,128)} %copy-done.18) | copy-start | bytes 3076
  129.6 37.1 %copy-start.21 = (f32[1,1,256]{2,1,0:T(1,128)S(1)}, f32[1,1,256]{2,1,0:T(1,128)}, u32[]{:S(2)}) copy-start(f32[1,1,256]{2,1,0:T(1,128)} %copy-done.20) | copy-start | bytes 3076
  129.6 37.1 %copy-start.23 = (f32[1,1,256]{2,1,0:T(1,128)S(1)}, f32[1,1,256]{2,1,0:T(1,128)}, u32[]{:S(2)}) copy-start(f32[1,1,256]{2,1,0:T(1,128)} %copy-done.22) | copy-start | bytes 3076
  129.6 37.1 %copy-start.25 = (f32[1,1,256]{2,1,0:T(1,128)S(1)}, f32[1,1,256]{2,1,0:T(1,128)}, u32[]{:S(2)}) copy-start(f32[1,1,256]{2,1,0:T(1,128)} %copy-done.24) | copy-start | bytes 3076
  129.6 37.1 %copy-start.27 = (f32[1,1,256]{2,1,0:T(1,128)S(1)}, f32[1,1,256]{2,1,0:T(1,128)}, u32[]{:S(2)}) copy-start(f32[1,1,256]{2,1,0:T(1,128)} %copy-done.26) | copy-start | bytes 3076
  129.6 37.1 %copy-start.29 = (f32[1,1,256]{2,1,0:T(1,128)S(1)}, f32[1,1,256]{2,1,0:T(1,128)}, u32[]{:S(2)}) copy-start(f32[1,1,256]{2,1,0:T(1,128)} %copy-done.28) | copy-start | bytes 3076
  129.6 37.1 %copy-start.31 = (f32[1,1,256]{2,1,0:T(1,128)S(1)}, f32[1,1,256]{2,1,0:T(1,128)}, u32[]{:S(2)}) copy-start(f32[1,1,256]{2,1,0:T(1,128)} %copy-done.30) | copy-start | bytes 3076
  129.6 37.1 %copy-start.33 = (f32[1,1,256]{2,1,0:T(1,128)S(1)}, f32[1,1,256]{2,1,0:T(1,128)}, u32[]{:S(2)}) copy-start(f32[1,1,256]{2,1,0:T(1,128)} %copy-done.32) | copy-start | bytes 3076
  129.6 37.1 %copy-start.35 = (f32[1,1,256]{2,1,0:T(1,128)S(1)}, f32[1,1,256]{2,1,0:T(1,128)}, u32[]{:S(2)}) copy-start(f32[1,1,256]{2,1,0:T(1,128)} %copy-done.34) | copy-start | bytes 3076
  129.7 37.1 %copy-start.37 = (f32[1,1,256]{2,1,0:T(1,128)S(1)}, f32[1,1,256]{2,1,0:T(1,128)}, u32[]{:S(2)}) copy-start(f32[1,1,256]{2,1,0:T(1,128)} %copy-done.36) | copy-start | bytes 3076
  129.7 37.1 %copy-start.39 = (f32[1,1,256]{2,1,0:T(1,128)S(1)}, f32[1,1,256]{2,1,0:T(1,128)}, u32[]{:S(2)}) copy-start(f32[1,1,256]{2,1,0:T(1,128)} %copy-done.38) | copy-start | bytes 3076
  129.7 37.1 %copy-start.41 = (f32[1,1,256]{2,1,0:T(1,128)S(1)}, f32[1,1,256]{2,1,0:T(1,128)}, u32[]{:S(2)}) copy-start(f32[1,1,256]{2,1,0:T(1,128)} %copy-done.40) | copy-start | bytes 3076
  129.7 37.1 %copy-start.43 = (f32[1,1,256]{2,1,0:T(1,128)S(1)}, f32[1,1,256]{2,1,0:T(1,128)}, u32[]{:S(2)}) copy-start(f32[1,1,256]{2,1,0:T(1,128)} %copy-done.42) | copy-start | bytes 3076
  129.7 37.1 %copy-start.45 = (f32[1,1,256]{2,1,0:T(1,128)S(1)}, f32[1,1,256]{2,1,0:T(1,128)}, u32[]{:S(2)}) copy-start(f32[1,1,256]{2,1,0:T(1,128)} %copy-done.44) | copy-start | bytes 3076
  129.7 37.1 %copy-start.47 = (f32[1,1,256]{2,1,0:T(1,128)S(1)}, f32[1,1,256]{2,1,0:T(1,128)}, u32[]{:S(2)}) copy-start(f32[1,1,256]{2,1,0:T(1,128)} %copy-done.46) | copy-start | bytes 3076
  129.9 9.9 %collective-permute-start.5 = (bf16[1,6,3,256]{3,2,1,0:T(4,128)(2,1)S(1)}, bf16[1,6,3,256]{3,2,1,0:T(4,128)(2,1)S(1)}, u32[]{:S(2)}, u32[]{:S(2)}) collective-permute-start(bf16[1,6,3,256]{3,2,1,0:T(4,128)(2,1)S(1)} %get-tuple-element.108), channel_id=1, source_target_pairs={{64,0},{128,64},{192,128},{256,192},{320,256},{384,320},{448,384},... | collective-permute-start | bytes 27656 | tf_op jit(solution)/shard_map/ppermute | solution.py:34
  139.9 12.6 %collective-permute-start.6 = (bf16[1,3,70,256]{3,2,1,0:T(8,128)(2,1)S(1)}, bf16[1,3,70,256]{3,2,1,0:T(8,128)(2,1)S(1)}, u32[]{:S(2)}, u32[]{:S(2)}) collective-permute-start(bf16[1,3,70,256]{3,2,1,0:T(8,128)(2,1)S(1)} %get-tuple-element.102), channel_id=1, source_target_pairs={{1,0},{2,1},{3,2},{4,3},{5,4},{6,5},{7,6},{8,7},{9,8},{10,9},{11,1... | collective-permute-start | bytes 322568 | tf_op jit(solution)/shard_map/ppermute | solution.py:34
  148.3 14.5 %collective-permute-start.7 = (bf16[1,3,70,256]{3,2,1,0:T(8,128)(2,1)S(1)}, bf16[1,3,70,256]{3,2,1,0:T(8,128)(2,1)S(1)}, u32[]{:S(2)}, u32[]{:S(2)}) collective-permute-start(bf16[1,3,70,256]{3,2,1,0:T(8,128)(2,1)S(1)} %get-tuple-element.103), channel_id=1, source_target_pairs={{0,1},{1,2},{2,3},{3,4},{4,5},{5,6},{6,7},{7,8},{8,9},{9,10},{10,1... | collective-permute-start | bytes 322568 | tf_op jit(solution)/shard_map/ppermute | solution.py:33
  164.0 7.5 %collective-permute-start.8 = (bf16[256,5,256]{0,2,1:T(8,128)(2,1)S(1)}, bf16[256,5,256]{0,2,1:T(8,128)(2,1)S(1)}, u32[]{:S(2)}, u32[]{:S(2)}) collective-permute-start(bf16[256,5,256]{0,2,1:T(8,128)(2,1)S(1)} %bitcast.113), channel_id=1, source_target_pairs={{0,64},{64,0},{1,65},{65,1},{2,66},{66,2},{3,67},{67,3},{4,68},{68... | collective-permute-start | bytes 1966088 | tf_op jit(solution)/shard_map/ppermute | solution.py:21
  (110 other events, 2089.6 us)

commit v2 on v0

v2 whole, which is shorter than its diff:
```python
import functools
import math

import jax
import jax.numpy as jnp
from jax import lax
from jax.experimental import pallas as pl
from jax.experimental.pallas import tpu as pltpu
from jax.sharding import Mesh, PartitionSpec as P

LON = ("y_lo", "core")
LAT = ("x", "y_hi", "z")
FAR = ("x", "y_hi", "y_lo", "z")
LANES = 128
VMEM_BYTES = 44 << 20
F32 = jnp.float32
BF16 = jnp.bfloat16


def dot(a, b, ca, cb):
    return lax.dot_general(a, b, (((ca,), (cb,)), ((), ())), preferred_element_type=F32)


def fill_padded(pad_ref, own_ref, up_ref, down_ref, left_ref, right_ref, top_ref, low_ref):
    rows, cols, _ = own_ref.shape
    for t in range(2):
        ln = slice(t * LANES, (t + 1) * LANES)
        pad_ref[t, 0:3, 8 : 8 + cols] = up_ref[:, :, ln].astype(F32)
        pad_ref[t, 3 : 3 + rows, 8 : 8 + cols] = own_ref[:, :, ln].astype(F32)
        pad_ref[t, 3 + rows : 6 + rows, 8 : 8 + cols] = down_ref[:, :, ln].astype(F32)
        pad_ref[t, 3 : 3 + rows, 5:8] = left_ref[:, :, ln].astype(F32)
        pad_ref[t, 3 : 3 + rows, 8 + cols : 11 + cols] = right_ref[:, :, ln].astype(F32)
        pad_ref[t, 0:3, 5:8] = top_ref[:, 0:3, ln].astype(F32)
        pad_ref[t, 0:3, 8 + cols : 11 + cols] = top_ref[:, 3:6, ln].astype(F32)
        pad_ref[t, 3 + rows : 6 + rows, 5:8] = low_ref[:, 0:3, ln].astype(F32)
        pad_ref[t, 3 + rows : 6 + rows, 8 + cols : 11 + cols] = low_ref[:, 3:6, ln].astype(F32)


def convolve(pad_ref, k_ref, out_ref, rows, cols, flip):
    blocks = cols // 8

    def step(n, carry):
        t = n // blocks
        at = pl.multiple_of((n % blocks) * 8, 8)
        acc = [jnp.zeros((8, LANES), F32) for _ in range(rows)]
        for j in range(7):
            window = [pad_ref[t, r, pl.ds(at + 5 + j, 8), :] for r in range(rows + 6)]
            for i in range(7):
                tap = (6 - i) * 7 + 6 - j if flip else i * 7 + j
                weight = k_ref[t, tap : tap + 1, :]
                for p in range(rows):
                    acc[p] = acc[p] + window[p + i] * weight
        for p in range(rows):
            out_ref[t, p, pl.ds(at, 8), :] = acc[p]
        return carry

    lax.fori_loop(0, 2 * blocks, step, 0)


def kernel_sums(pad_ref, grad_ref, out_ref, rows, cols):
    def step(n, carry):
        t, j = n // 7, n % 7
        acc = [jnp.zeros((8, LANES), F32) for _ in range(7)]
        for b in range(cols // 8):
            window = [pad_ref[t, r, pl.ds(b * 8 + 5 + j, 8), :] for r in range(rows + 6)]
            grad = [grad_ref[t, p, b * 8 : b * 8 + 8, :] for p in range(rows)]
            for i in range(7):
                for p in range(rows):
                    acc[i] = acc[i] + window[p + i] * grad[p]
        for i in range(7):
            out_ref[t, j, i] = acc[i]
        return carry

    lax.fori_loop(0, 14, step, 0)


def block_kernel(
    own_ref, up_ref, down_ref, left_ref, right_ref, top_ref, low_ref, mask_ref, masked_ref, k_ref, dw_bias_ref,
    gain_ref, bias_ref, w_in_ref, b_in_ref, w_out_ref, b_out_ref, scale_ref,
    out_ref, grad_ref, big_ref, small_ref,
    pad_ref, depth_ref, terms_ref,
):
    rows, cols, channels = own_ref.shape
    cells = rows * cols
    hidden = w_in_ref.shape[1]
    halves = channels // LANES
    fill_padded(pad_ref, own_ref, up_ref, down_ref, left_ref, right_ref, top_ref, low_ref)
    convolve(pad_ref, k_ref, depth_ref, rows, cols, False)
    depth = jnp.concatenate([depth_ref[t].reshape(cells, LANES) for t in range(2)], axis=1)
    depth = depth + dw_bias_ref[...]
    center = depth - jnp.mean(depth, axis=-1, keepdims=True)
    inv_std = lax.rsqrt(jnp.mean(center * center, axis=-1, keepdims=True) + 1e-6)
    norm_hat = center * inv_std
    normed = (norm_hat * gain_ref[...] + bias_ref[...]).astype(BF16)
    masked = masked_ref[...].astype(F32)
    grad_branch = (masked * scale_ref[...]).astype(BF16)
    branch = jnp.zeros((cells, channels), F32)
    grad_norm = jnp.zeros((cells, channels), F32)
    root = math.sqrt(2.0 / math.pi)
    b_in_sums = []
    width = channels
    for h in range(hidden // width):
        at = slice(h * width, (h + 1) * width)
        w_in = w_in_ref[:, at]
        w_out = w_out_ref[at, :]
        pre = dot(normed, w_in, 1, 0) + b_in_ref[:, at]
        square = pre * pre
        bent = jnp.tanh(root * pre * (1.0 + 0.044715 * square))
        half = 0.5 * (1.0 + bent)
        act = (pre * half).astype(BF16)
        slope = half + (0.5 * root) * pre * (1.0 - bent * bent) * (1.0 + (3 * 0.044715) * square)
        grad_pre = (dot(grad_branch, w_out, 1, 1) * slope).astype(BF16)
        branch = branch + dot(act, w_out, 1, 0)
        grad_norm = grad_norm + dot(grad_pre, w_in, 1, 1)
        g_in = dot(normed, grad_pre, 0, 0).astype(BF16)
        g_out = dot(act, grad_branch, 0, 0).astype(BF16)
        for t in range(width // LANES):
            base = (h * (width // LANES) + t) * channels
            big_ref[base : base + channels, :] = g_in[:, t * LANES : (t + 1) * LANES]
        for t in range(halves):
            base = hidden * halves + t * hidden + h * width
            big_ref[base : base + width, :] = g_out[:, t * LANES : (t + 1) * LANES]
        b_in_sums.append(jnp.sum(grad_pre.astype(F32), axis=0, keepdims=True))
    branch = branch + b_out_ref[...]
    mask = mask_ref[...].astype(F32)
    own = own_ref[...].reshape(cells, channels).astype(F32)
    out_ref[...] = (own + mask * scale_ref[...] * branch).astype(BF16).reshape(rows, cols, channels)
    scaled = grad_norm * gain_ref[...]
    mean_u = jnp.mean(scaled, axis=-1, keepdims=True)
    mean_un = jnp.mean(scaled * norm_hat, axis=-1, keepdims=True)
    grad_depth = (inv_std * (scaled - mean_u - norm_hat * mean_un)).astype(BF16)
    grad_ref[...] = grad_depth.reshape(rows, cols, channels)
    grad_float = grad_depth.astype(F32)
    for t in range(2):
        depth_ref[t] = grad_float[:, t * LANES : (t + 1) * LANES].reshape(rows, cols, LANES)
    kernel_sums(pad_ref, depth_ref, terms_ref, rows, cols)
    singles = b_in_sums + [
        jnp.sum(grad_float, axis=0, keepdims=True),
        jnp.sum(grad_norm * norm_hat, axis=0, keepdims=True),
        jnp.sum(grad_norm, axis=0, keepdims=True),
        jnp.sum(grad_branch.astype(F32), axis=0, keepdims=True),
        jnp.sum(masked * branch, axis=0, keepdims=True),
    ]
    for t in range(2):
        ln = slice(t * LANES, (t + 1) * LANES)
        small_ref[t, 0:49, :] = jnp.sum(terms_ref[t].reshape(49, 8, LANES), axis=1)
        for n, single in enumerate(singles):
            small_ref[t, 49 + n : 50 + n, :] = single[:, ln]
        small_ref[t, 49 + len(singles) :, :] = jnp.zeros((64 - 49 - len(singles), LANES), F32)


def state_kernel(
    own_ref, up_ref, down_ref, left_ref, right_ref, top_ref, low_ref, cot_ref, k_ref, out_ref, pad_ref, sum_ref
):
    rows, cols, _ = own_ref.shape
    fill_padded(pad_ref, own_ref, up_ref, down_ref, left_ref, right_ref, top_ref, low_ref)
    convolve(pad_ref, k_ref, sum_ref, rows, cols, True)
    for t in range(2):
        ln = slice(t * LANES, (t + 1) * LANES)
        out_ref[:, :, ln] = (cot_ref[:, :, ln].astype(F32) + sum_ref[t]).astype(BF16)


def unpack_kernel(factor, core_ref, mine_ref, other_ref, w_in_ref, w_out_ref):
    channels, hidden = w_in_ref.shape

    def write(first_ref, second_ref):
        for t in range(hidden // LANES):
            part = first_ref[t * channels : (t + 1) * channels, :]
            w_in_ref[:, t * LANES : (t + 1) * LANES] = part.astype(F32) * factor
        for t in range(channels // LANES):
            part = second_ref[t * hidden : (t + 1) * hidden, :]
            w_out_ref[:, t * LANES : (t + 1) * LANES] = part.astype(F32) * factor

    @pl.when(core_ref[0] == 0)
    def _():
        write(mine_ref, other_ref)

    @pl.when(core_ref[0] != 0)
    def _():
        write(other_ref, mine_ref)


def shifts(axis, wrap):
    size = lax.axis_size(axis)
    up = [(i, (i + 1) % size) for i in range(size if wrap else size - 1)]
    return up, [(j, i) for i, j in up]


def halo_sides(field):
    rows, cols, _ = field.shape
    lat_up, lat_down = shifts(LAT, False)
    lon_up, lon_down = shifts(LON, True)
    up = lax.ppermute(field[rows - 3 :], LAT, lat_up)
    down = lax.ppermute(field[:3], LAT, lat_down)
    left = lax.ppermute(field[:, cols - 3 :], LON, lon_up)
    right = lax.ppermute(field[:, :3], LON, lon_down)
    return up, down, left, right


def halo_corners(left, right):
    rows = left.shape[0]
    lat_up, lat_down = shifts(LAT, False)
    sides = jnp.concatenate([left, right], axis=1)
    top = lax.ppermute(sides[rows - 3 :], LAT, lat_up)
    low = lax.ppermute(sides[:3], LAT, lat_down)
    return top, low


def local(
    ocean_state, land_sea, cotangent, dw_kernel, dw_bias, ln_gain, ln_bias, w_in, b_in, w_out, b_out, layer_scale
):
    _, rows, cols, channels = ocean_state.shape
    cells = rows * cols
    hidden = w_in.shape[1]
    far = lax.axis_size(FAR)
    core = lax.axis_index("core")
    own = ocean_state[0]
    cot = cotangent[0]
    up, down, left, right = halo_sides(own)
    top, low = halo_corners(left, right)
    mask = jnp.broadcast_to(land_sea[0].astype(BF16)[..., None], cot.shape)
    masked = mask * cot
    taps = dw_kernel.reshape(49, 2, LANES).transpose(1, 0, 2)
    pad = pltpu.VMEM((2, rows + 6, cols + 16, LANES), F32)
    plane = pltpu.VMEM((2, rows, cols, LANES), F32)
    params = pltpu.CompilerParams(vmem_limit_bytes=VMEM_BYTES)
    output, grad_depth, big, small = pl.pallas_call(
        block_kernel,
        out_shape=(
            jax.ShapeDtypeStruct((rows, cols, channels), BF16),
            jax.ShapeDtypeStruct((rows, cols, channels), BF16),
            jax.ShapeDtypeStruct((4 * hidden, LANES), BF16),
            jax.ShapeDtypeStruct((2, 64, LANES), F32),
        ),
        scratch_shapes=[pad, plane, pltpu.VMEM((2, 7, 7, 8, LANES), F32)],
        compiler_params=params,
        cost_estimate=pl.CostEstimate(flops=1300000000, transcendentals=400000, bytes_accessed=6000000),
        name="block",
    )(
        own, up, down, left, right, top, low, mask.reshape(cells, channels), masked.reshape(cells, channels), taps,
        dw_bias[None], ln_gain[None], ln_bias[None], w_in, b_in[None], w_out, b_out[None], layer_scale[None],
    )
    sides = halo_sides(grad_depth)
    small_rows = small.transpose(1, 0, 2).astype(BF16)
    small_rows = jnp.pad(small_rows, ((0, 2 * far - 64), (0, 0), (0, 0)))[:, None]
    chunks = jnp.concatenate([big.reshape(2 * far, 4, 2, LANES), small_rows], axis=1)
    pair = lax.all_to_all(chunks.reshape(2, far, 5, 2, LANES), "core", 0, 0)
    value = (pair[0].astype(F32) + pair[1].astype(F32)).astype(BF16)
    value = lax.all_to_all(value, FAR, 0, 0)
    value = jnp.sum(value.astype(F32), axis=0).astype(BF16)
    value, sides = lax.optimization_barrier((value, sides))
    value = lax.all_to_all(jnp.broadcast_to(value[None], (far, 5, 2, LANES)), FAR, 0, 0)
    g_up, g_down, g_left, g_right = sides
    g_top, g_low = halo_corners(g_left, g_right)
    grad_state = pl.pallas_call(
        state_kernel,
        out_shape=jax.ShapeDtypeStruct((rows, cols, channels), BF16),
        scratch_shapes=[pad, plane],
        compiler_params=params,
        cost_estimate=pl.CostEstimate(flops=10000000, transcendentals=0, bytes_accessed=3000000),
        name="state",
    )(grad_depth, g_up, g_down, g_left, g_right, g_top, g_low, cot, taps)
    value, grad_state = lax.optimization_barrier((value, grad_state))
    other = lax.ppermute(value, "core", [(0, 1), (1, 0)])
    total_cells = cells * lax.axis_size(LON) * lax.axis_size(LAT)
    factor = 1.0 / math.sqrt(total_cells)
    grad_w_in, grad_w_out = pl.pallas_call(
        functools.partial(unpack_kernel, factor),
        out_shape=(
            jax.ShapeDtypeStruct((channels, hidden), F32),
            jax.ShapeDtypeStruct((hidden, channels), F32),
        ),
        in_specs=[
            pl.BlockSpec(memory_space=pltpu.SMEM),
            pl.BlockSpec(memory_space=pltpu.VMEM),
            pl.BlockSpec(memory_space=pltpu.VMEM),
        ],
        compiler_params=params,
        name="unpack",
    )(
        core.astype(jnp.int32).reshape(1),
        value[:, :4].reshape(2 * hidden, LANES),
        other[:, :4].reshape(2 * hidden, LANES),
    )
    small_sum = jnp.where(core == 0, value[:64, 4], other[:64, 4]).astype(F32) * factor
    small_sum = small_sum.reshape(64, channels)
    blocks = hidden // channels
    singles = 49 + blocks
    grad_kernel = small_sum[:49].reshape(7, 7, channels).transpose(1, 0, 2)
    return (
        output[None],
        grad_state[None],
        grad_kernel,
        small_sum[singles],
        small_sum[singles + 1],
        small_sum[singles + 2],
        grad_w_in,
        small_sum[49:singles].reshape(hidden),
        grad_w_out,
        small_sum[singles + 3],
        small_sum[singles + 4],
    )


def solution(mesh):
    mesh = Mesh(mesh.devices.reshape(4, 2, 4, 2, 8), ("y_lo", "core", "x", "y_hi", "z"))
    field = P(None, LAT, LON, None)
    in_specs = (field, P(None, LAT, LON), field) + (P(),) * 9
    out_specs = (field, field) + (P(),) * 9
    return jax.shard_map(local, mesh=mesh, in_specs=in_specs, out_specs=out_specs, check_vma=False)
```

time: 452 us -> 147 us (0.33)
  the two profiles are of different devices: /device:TPU:1 before, /device:TPU:7 now
where the time goes in v2:
time: 147 us; the launch traced here: 146 us
  starting transfers between devices  91.2 us (62%)
  waiting for transfers between devices  23.6 us (16%)
  Pallas kernels  11.5 us (8%)
  local copies, waits for them, and re-layouts  7.03 us (5%)
  blocking collectives  5.84 us (4%)
  other arithmetic  5.72 us (4%)
    ppermute x2, starting transfers between devices, halo_sides(): down = lax.ppermute(field[:3], LAT, lat_down)  25.3 us
    ppermute x2, starting transfers between devices, halo_corners(): low = lax.ppermute(sides[:3], LAT, lat_down)  19.5 us
    ppermute x2, waiting for transfers between devices, halo_corners(): top = lax.ppermute(sides[rows - 3:], LAT, lat_up)  17.5 us
    all_to_all x1, starting transfers between devices, local(): lax.all_to_all(jnp.broadcast_to(value[None], (far, 5, 2, LANES)), FAR, 0, 0)  11.4 us
    all_to_all x1, starting transfers between devices, local(): value = lax.all_to_all(value, FAR, 0, 0)  8.71 us
    pallas_call x1, Pallas kernels, local(): pl.pallas_call(block_kernel, out_shape=(jax.ShapeDtypeStruct((rows, cols,...  7.22 us
    ppermute x1, starting transfers between devices, local(): other = lax.ppermute(value, 'core', [(0, 1), (1, 0)])  7.09 us
    ppermute x2, starting transfers between devices, halo_sides(): left = lax.ppermute(field[:, cols - 3:], LON, lon_up)  5.85 us
  transfers between devices with their start and end apart: 15, of which 5 were waited for; matrix products, arithmetic and copies ran while one was open for 3% of the time, Pallas kernels for 2%

profile of v2, /device:TPU:7, one launch (start us, length us, event | category | flops | bytes accessed | tf_op | source)
XLA Modules:
  0.0 146.0 jit_solution(7914448782746829995)
XLA Ops:
  0.7 0.9 fusion.5
  1.6 2.6 %collective-permute-start.3 = (bf16[6,3,256]{2,1,0:T(4,128)(2,1)S(1)}, bf16[6,3,256]{2,1,0:T(4,128)(2,1)S(1)}, u32[]{:S(2)}, u32[]{:S(2)}) collective-permute-start(bf16[6,3,256]{2,1,0:T(4,128)(2,1)S(1)} %get-tuple-element.63), channel_id=1, source_target_pairs={{64,0},{128,64},{192,128},{256,192},{320,256},{384,320},{448,384},... | collective-permute-start | bytes 27656 | tf_op jit(solution)/shard_map/ppermute | solution.py:196
  4.2 3.1 %collective-permute-start.2 = (bf16[6,3,256]{2,1,0:T(4,128)(2,1)S(1)}, bf16[6,3,256]{2,1,0:T(4,128)(2,1)S(1)}, u32[]{:S(2)}, u32[]{:S(2)}) collective-permute-start(bf16[6,3,256]{2,1,0:T(4,128)(2,1)S(1)} %get-tuple-element.64), channel_id=1, source_target_pairs={{0,64},{64,128},{128,192},{192,256},{256,320},{320,384},{384,448},... | collective-permute-start | bytes 27656 | tf_op jit(solution)/shard_map/ppermute | solution.py:195
  7.3 1.0 slice_bitcast_fusion
  8.3 16.1 %collective-permute-start.1 = (bf16[3,64,256]{2,1,0:T(8,128)(2,1)S(1)}, bf16[3,64,256]{2,1,0:T(8,128)(2,1)S(1)}, u32[]{:S(2)}, u32[]{:S(2)}) collective-permute-start(bf16[3,64,256]{2,1,0:T(8,128)(2,1)S(1)} %get-tuple-element.65), channel_id=1, source_target_pairs={{1,0},{2,1},{3,2},{4,3},{5,4},{6,5},{7,6},{8,7},{9,8},{10,9},{11,1... | collective-permute-start | bytes 294920 | tf_op jit(solution)/shard_map/ppermute | solution.py:194
  24.4 1.9 %collective-permute-start = (bf16[3,64,256]{2,1,0:T(8,128)(2,1)S(1)}, bf16[3,64,256]{2,1,0:T(8,128)(2,1)S(1)}, u32[]{:S(2)}, u32[]{:S(2)}) collective-permute-start(bf16[3,64,256]{2,1,0:T(8,128)(2,1)S(1)} %get-tuple-element.66), channel_id=1, source_target_pairs={{0,1},{1,2},{2,3},{3,4},{4,5},{5,6},{6,7},{7,8},{8,9},{9,10},{10,1... | collective-permute-start | bytes 294920 | tf_op jit(solution)/shard_map/ppermute | solution.py:193
  26.3 0.7 convert_reduce_fusion
  27.1 10.3 %collective-permute-start.5 = (bf16[3,6,256]{2,1,0:T(8,128)(2,1)S(1)}, bf16[3,6,256]{2,1,0:T(8,128)(2,1)S(1)}, u32[]{:S(2)}, u32[]{:S(2)}) collective-permute-start(bf16[3,6,256]{2,1,0:T(8,128)(2,1)S(1)} %get-tuple-element.74), channel_id=1, source_target_pairs={{1,0},{2,1},{3,2},{4,3},{5,4},{6,5},{7,6},{8,7},{9,8},{10,9},{11,1... | collective-permute-start | bytes 27656 | tf_op jit(solution)/shard_map/ppermute | solution.py:205
  37.4 1.9 %collective-permute-start.4 = (bf16[3,6,256]{2,1,0:T(8,128)(2,1)S(1)}, bf16[3,6,256]{2,1,0:T(8,128)(2,1)S(1)}, u32[]{:S(2)}, u32[]{:S(2)}) collective-permute-start(bf16[3,6,256]{2,1,0:T(8,128)(2,1)S(1)} %get-tuple-element.75), channel_id=1, source_target_pairs={{0,1},{1,2},{2,3},{3,4},{4,5},{5,6},{6,7},{7,8},{8,9},{9,10},{10,1... | collective-permute-start | bytes 27656 | tf_op jit(solution)/shard_map/ppermute | solution.py:204
  39.3 1.0 bitcast_multiply_fusion.masked_ref
  40.4 0.8 reshape.100
  41.2 7.5 %collective-permute-done.4.top_ref = bf16[3,6,256]{2,1,0:T(8,128)(2,1)S(1)} collective-permute-done((bf16[3,6,256]{2,1,0:T(8,128)(2,1)S(1)}, bf16[3,6,256]{2,1,0:T(8,128)(2,1)S(1)}, u32[]{:S(2)}, u32[]{:S(2)}) %collective-permute-start.4) | collective-permute-done | bytes 9248 | tf_op jit(solution)/shard_map/ppermute | solution.py:204
  49.0 7.2 %block.1 = (bf16[6,64,256]{2,1,0:T(8,128)(2,1)}, bf16[6,64,256]{2,1,0:T(8,128)(2,1)S(1)}, bf16[4096,128]{1,0:T(8,128)(2,1)S(1)}, f32[2,64,128]{2,1,0:T(8,128)S(1)}) custom-call(bf16[6,64,256]{2,1,0:T(8,128)(2,1)S(1)} %bitcast.45, bf16[3,64,256]{2,1,0:T(8,128)(2,1)S(1)} %collective-permute-done.up_ref, ...), custom_call_target="tpu_custom_call" | custom-call | flops 1300000000 | bytes 6000000 | tf_op jit(solution)/shard_map/block/pallas_call | solution.py:227
  56.5 1.8 %pad_maximum_fusion = bf16[2,256,5,2,128]{4,3,2,1,0:T(2,128)(2,1)S(1)} fusion(bf16[2,256,1,2,128]{4,3,2,1,0:T(2,128)(2,1)S(1)} %copy.30, bf16[2,256,4,2,128]{4,3,2,1,0:T(2,128)(2,1)S(1)} %bitcast.42), kind=kLoop, calls=%fused_computation | loop fusion | flops 655360 | bytes 2621440 | tf_op jit(solution)/shard_map/concatenate | solution.py:246
  58.3 5.8 %all_to_all.15 = bf16[2,256,5,2,128]{4,3,2,1,0:T(2,128)(2,1)S(1)} all-to-all(bf16[2,256,5,2,128]{4,3,2,1,0:T(2,128)(2,1)S(1)} %pad_maximum_fusion), channel_id=1, replica_groups=mesh['y_lo'=4,'core'=2,'x'=4,'y_hi'=2,'z'=8] {'core'}, dimensions={0} | all-to-all | bytes 2621440 | tf_op jit(solution)/shard_map/all_to_all | solution.py:247
  64.1 1.5 %fusion = bf16[256,5,2,128]{3,2,1,0:T(2,128)(2,1)} fusion(bf16[2,256,5,2,128]{4,3,2,1,0:T(2,128)(2,1)S(1)} %all_to_all.15), kind=kLoop, calls=%fused_computation.2 | loop fusion | flops 1310720 | bytes 1966080 | tf_op jit(solution)/shard_map/convert_element_type | solution.py:248
  65.6 8.7 %all-to-all-start.1 = ((bf16[256,5,2,128]{3,2,1,0:T(2,128)(2,1)}), bf16[256,5,2,128]{3,2,1,0:T(2,128)(2,1)S(1)}, u32[]{:S(2)}, u32[]{:S(2)}) async-start(bf16[256,5,2,128]{3,2,1,0:T(2,128)(2,1)} %fusion), calls=%async_computation.1 | async-start | bytes 1310720 | tf_op jit(solution)/shard_map/all_to_all | solution.py:249
  74.4 9.2 %collective-permute-start.7 = (bf16[3,64,256]{2,1,0:T(8,128)(2,1)S(1)}, bf16[3,64,256]{2,1,0:T(8,128)(2,1)S(1)}, u32[]{:S(2)}, u32[]{:S(2)}) collective-permute-start(bf16[3,64,256]{2,1,0:T(8,128)(2,1)S(1)} %get-tuple-element.61), channel_id=1, source_target_pairs={{1,0},{2,1},{3,2},{4,3},{5,4},{6,5},{7,6},{8,7},{9,8},{10,9},{11,1... | collective-permute-start | bytes 294920 | tf_op jit(solution)/shard_map/ppermute | solution.py:194
  83.6 1.9 %collective-permute-start.6 = (bf16[3,64,256]{2,1,0:T(8,128)(2,1)S(1)}, bf16[3,64,256]{2,1,0:T(8,128)(2,1)S(1)}, u32[]{:S(2)}, u32[]{:S(2)}) collective-permute-start(bf16[3,64,256]{2,1,0:T(8,128)(2,1)S(1)} %get-tuple-element.62), channel_id=1, source_target_pairs={{0,1},{1,2},{2,3},{3,4},{4,5},{5,6},{6,7},{7,8},{8,9},{9,10},{10,1... | collective-permute-start | bytes 294920 | tf_op jit(solution)/shard_map/ppermute | solution.py:193
  85.6 3.1 %collective-permute-start.9 = (bf16[6,3,256]{2,1,0:T(4,128)(2,1)S(1)}, bf16[6,3,256]{2,1,0:T(4,128)(2,1)S(1)}, u32[]{:S(2)}, u32[]{:S(2)}) collective-permute-start(bf16[6,3,256]{2,1,0:T(4,128)(2,1)S(1)} %get-tuple-element.59), channel_id=1, source_target_pairs={{64,0},{128,64},{192,128},{256,192},{320,256},{384,320},{448,384},... | collective-permute-start | bytes 27656 | tf_op jit(solution)/shard_map/ppermute | solution.py:196
  88.7 2.8 %collective-permute-start.8 = (bf16[6,3,256]{2,1,0:T(4,128)(2,1)S(1)}, bf16[6,3,256]{2,1,0:T(4,128)(2,1)S(1)}, u32[]{:S(2)}, u32[]{:S(2)}) collective-permute-start(bf16[6,3,256]{2,1,0:T(4,128)(2,1)S(1)} %get-tuple-element.60), channel_id=1, source_target_pairs={{0,64},{64,128},{128,192},{192,256},{256,320},{320,384},{384,448},... | collective-permute-start | bytes 27656 | tf_op jit(solution)/shard_map/ppermute | solution.py:195
  91.5 2.7 %all-to-all-done.1 = bf16[256,5,2,128]{3,2,1,0:T(2,128)(2,1)S(1)} async-done(((bf16[256,5,2,128]{3,2,1,0:T(2,128)(2,1)}), bf16[256,5,2,128]{3,2,1,0:T(2,128)(2,1)S(1)}, u32[]{:S(2)}, u32[]{:S(2)}) %all-to-all-start.1) | async-done | bytes 655392 | tf_op jit(solution)/shard_map/all_to_all | solution.py:249
  94.8 2.1 %collective-permute-done.6.up_ref = bf16[3,64,256]{2,1,0:T(8,128)(2,1)S(1)} collective-permute-done((bf16[3,64,256]{2,1,0:T(8,128)(2,1)S(1)}, bf16[3,64,256]{2,1,0:T(8,128)(2,1)S(1)}, u32[]{:S(2)}, u32[]{:S(2)}) %collective-permute-start.6) | collective-permute-done | bytes 98336 | tf_op jit(solution)/shard_map/ppermute | solution.py:193
  96.9 1.2 broadcast_in_dim.45
  98.1 11.4 %all-to-all-start.2 = ((bf16[256,5,2,128]{3,2,1,0:T(2,128)(2,1)}), bf16[256,5,2,128]{3,2,1,0:T(2,128)(2,1)S(1)}, u32[]{:S(2)}, u32[]{:S(2)}) async-start(bf16[256,5,2,128]{3,2,1,0:T(2,128)(2,1)} %broadcast_in_dim.45), calls=%async_computation.2 | async-start | bytes 1310720 | tf_op jit(solution)/shard_map/all_to_all | solution.py:252
  109.5 9.2 %collective-permute-start.11 = (bf16[3,6,256]{2,1,0:T(8,128)(2,1)S(1)}, bf16[3,6,256]{2,1,0:T(8,128)(2,1)S(1)}, u32[]{:S(2)}, u32[]{:S(2)}) collective-permute-start(bf16[3,6,256]{2,1,0:T(8,128)(2,1)S(1)} %get-tuple-element.72), channel_id=1, source_target_pairs={{1,0},{2,1},{3,2},{4,3},{5,4},{6,5},{7,6},{8,7},{9,8},{10,9},{11,1... | collective-permute-start | bytes 27656 | tf_op jit(solution)/shard_map/ppermute | solution.py:205
  118.7 1.9 %collective-permute-start.10 = (bf16[3,6,256]{2,1,0:T(8,128)(2,1)S(1)}, bf16[3,6,256]{2,1,0:T(8,128)(2,1)S(1)}, u32[]{:S(2)}, u32[]{:S(2)}) collective-permute-start(bf16[3,6,256]{2,1,0:T(8,128)(2,1)S(1)} %get-tuple-element.73), channel_id=1, source_target_pairs={{0,1},{1,2},{2,3},{3,4},{4,5},{5,6},{6,7},{7,8},{8,9},{9,10},{10,1... | collective-permute-start | bytes 27656 | tf_op jit(solution)/shard_map/ppermute | solution.py:204
  120.7 10.0 %collective-permute-done.10.top_ref = bf16[3,6,256]{2,1,0:T(8,128)(2,1)S(1)} collective-permute-done((bf16[3,6,256]{2,1,0:T(8,128)(2,1)S(1)}, bf16[3,6,256]{2,1,0:T(8,128)(2,1)S(1)}, u32[]{:S(2)}, u32[]{:S(2)}) %collective-permute-start.10) | collective-permute-done | bytes 9248 | tf_op jit(solution)/shard_map/ppermute | solution.py:204
  130.6 2.7 %state.1 = bf16[6,64,256]{2,1,0:T(8,128)(2,1)} custom-call(bf16[6,64,256]{2,1,0:T(8,128)(2,1)S(1)} %get-tuple-element.27.own_ref, bf16[3,64,256]{2,1,0:T(8,128)(2,1)S(1)} %collective-permute-done.6.up_ref, bf16[3,64,256]{2,1,0:T(8,128)(2,1)S(1)} %collective-permute-done.7.down_ref, bf16[6,3,256]{2,1,0:T(4,128)(2,1)S(1)} %collective-permute-done.8.left_ref, ...), custom_call_target="tpu_custom_call" | custom-call | flops 10000000 | bytes 3000000 | tf_op jit(solution)/shard_map/state/pallas_call | solution.py:255
  133.3 7.1 %collective-permute-start.12 = (bf16[256,5,2,128]{3,2,1,0:T(2,128)(2,1)S(1)}, bf16[256,5,2,128]{3,2,1,0:T(2,128)(2,1)S(1)}, u32[]{:S(2)}, u32[]{:S(2)}) collective-permute-start(bf16[256,5,2,128]{3,2,1,0:T(2,128)(2,1)S(1)} %all-to-all-done.2), channel_id=1, source_target_pairs={{0,64},{64,0},{1,65},{65,1},{2,66},{66,2},{3,67},{67,3},{4,68},{68... | collective-permute-start | bytes 1966088 | tf_op jit(solution)/shard_map/ppermute | solution.py:264
  140.8 1.3 collective-permute-done.12
  144.4 1.5 %unpack.1 = (f32[256,1024]{1,0:T(8,128)}, f32[1024,256]{1,0:T(8,128)}) custom-call(s32[1]{0:T(128)} %bitcast.22.core_ref, bf16[2048,128]{1,0:T(8,128)(2,1)S(1)} %bitcast.40, bf16[2048,128]{1,0:T(8,128)(2,1)S(1)} %bitcast.41), custom_call_target="tpu_custom_call" | custom-call | tf_op jit(solution)/shard_map/unpack/pallas_call | solution.py:267
  (49 shorter events, 3.9 us)
Async XLA Ops:
  0.6 48.2 %copy-start.1 = (bf16[1,6,64,256]{3,2,1,0:T(8,128)(2,1)S(1)}, bf16[1,6,64,256]{3,2,1,0:T(8,128)(2,1)}, u32[]{:S(2)}) copy-start(bf16[1,6,64,256]{3,2,1,0:T(8,128)(2,1)} %param.12) | copy-start | bytes 589828
  0.7 48.2 %copy-start.9 = (f32[256]{0:T(256)S(1)}, f32[256]{0:T(256)}, u32[]{:S(2)}) copy-start(f32[256]{0:T(256)} %param.23) | copy-start | bytes 3076
  0.7 48.2 %copy-start.8 = (f32[256]{0:T(256)S(1)}, f32[256]{0:T(256)}, u32[]{:S(2)}) copy-start(f32[256]{0:T(256)} %param.22) | copy-start | bytes 3076
  0.7 48.2 %copy-start.3 = (bf16[1024,256]{1,0:T(8,128)(2,1)S(1)}, bf16[1024,256]{1,0:T(8,128)(2,1)}, u32[]{:S(2)}) copy-start(bf16[1024,256]{1,0:T(8,128)(2,1)} %w_out_ref.1) | copy-start | bytes 1572868
  0.7 48.2 %copy-start.4 = (f32[1024]{0:T(1024)S(1)}, f32[1024]{0:T(1024)}, u32[]{:S(2)}) copy-start(f32[1024]{0:T(1024)} %param.20) | copy-start | bytes 12292
  0.7 48.2 %copy-start.2 = (bf16[256,1024]{1,0:T(8,128)(2,1)S(1)}, bf16[256,1024]{1,0:T(8,128)(2,1)}, u32[]{:S(2)}) copy-start(bf16[256,1024]{1,0:T(8,128)(2,1)} %w_in_ref.1) | copy-start | bytes 1572868
  0.7 48.2 %copy-start.7 = (f32[256]{0:T(256)S(1)}, f32[256]{0:T(256)}, u32[]{:S(2)}) copy-start(f32[256]{0:T(256)} %param.18) | copy-start | bytes 3076
  0.7 48.2 %copy-start.6 = (f32[256]{0:T(256)S(1)}, f32[256]{0:T(256)}, u32[]{:S(2)}) copy-start(f32[256]{0:T(256)} %param.17) | copy-start | bytes 3076
  0.7 48.2 %copy-start.5 = (f32[256]{0:T(256)S(1)}, f32[256]{0:T(256)}, u32[]{:S(2)}) copy-start(f32[256]{0:T(256)} %param.16) | copy-start | bytes 3076
  1.6 25.5 %collective-permute-start.3 = (bf16[6,3,256]{2,1,0:T(4,128)(2,1)S(1)}, bf16[6,3,256]{2,1,0:T(4,128)(2,1)S(1)}, u32[]{:S(2)}, u32[]{:S(2)}) collective-permute-start(bf16[6,3,256]{2,1,0:T(4,128)(2,1)S(1)} %get-tuple-element.63), channel_id=1, source_target_pairs={{64,0},{128,64},{192,128},{256,192},{320,256},{384,320},{448,384},... | collective-permute-start | bytes 27656 | tf_op jit(solution)/shard_map/ppermute | solution.py:196
  4.2 22.9 %collective-permute-start.2 = (bf16[6,3,256]{2,1,0:T(4,128)(2,1)S(1)}, bf16[6,3,256]{2,1,0:T(4,128)(2,1)S(1)}, u32[]{:S(2)}, u32[]{:S(2)}) collective-permute-start(bf16[6,3,256]{2,1,0:T(4,128)(2,1)S(1)} %get-tuple-element.64), channel_id=1, source_target_pairs={{0,64},{64,128},{128,192},{192,256},{256,320},{320,384},{384,448},... | collective-permute-start | bytes 27656 | tf_op jit(solution)/shard_map/ppermute | solution.py:195
  8.3 40.5 %collective-permute-start.1 = (bf16[3,64,256]{2,1,0:T(8,128)(2,1)S(1)}, bf16[3,64,256]{2,1,0:T(8,128)(2,1)S(1)}, u32[]{:S(2)}, u32[]{:S(2)}) collective-permute-start(bf16[3,64,256]{2,1,0:T(8,128)(2,1)S(1)} %get-tuple-element.65), channel_id=1, source_target_pairs={{1,0},{2,1},{3,2},{4,3},{5,4},{6,5},{7,6},{8,7},{9,8},{10,9},{11,1... | collective-permute-start | bytes 294920 | tf_op jit(solution)/shard_map/ppermute | solution.py:194
  24.4 24.4 %collective-permute-start = (bf16[3,64,256]{2,1,0:T(8,128)(2,1)S(1)}, bf16[3,64,256]{2,1,0:T(8,128)(2,1)S(1)}, u32[]{:S(2)}, u32[]{:S(2)}) collective-permute-start(bf16[3,64,256]{2,1,0:T(8,128)(2,1)S(1)} %get-tuple-element.66), channel_id=1, source_target_pairs={{0,1},{1,2},{2,3},{3,4},{4,5},{5,6},{6,7},{7,8},{8,9},{9,10},{10,1... | collective-permute-start | bytes 294920 | tf_op jit(solution)/shard_map/ppermute | solution.py:193
  27.1 14.1 %collective-permute-start.5 = (bf16[3,6,256]{2,1,0:T(8,128)(2,1)S(1)}, bf16[3,6,256]{2,1,0:T(8,128)(2,1)S(1)}, u32[]{:S(2)}, u32[]{:S(2)}) collective-permute-start(bf16[3,6,256]{2,1,0:T(8,128)(2,1)S(1)} %get-tuple-element.74), channel_id=1, source_target_pairs={{1,0},{2,1},{3,2},{4,3},{5,4},{6,5},{7,6},{8,7},{9,8},{10,9},{11,1... | collective-permute-start | bytes 27656 | tf_op jit(solution)/shard_map/ppermute | solution.py:205
  37.4 11.4 %collective-permute-start.4 = (bf16[3,6,256]{2,1,0:T(8,128)(2,1)S(1)}, bf16[3,6,256]{2,1,0:T(8,128)(2,1)S(1)}, u32[]{:S(2)}, u32[]{:S(2)}) collective-permute-start(bf16[3,6,256]{2,1,0:T(8,128)(2,1)S(1)} %get-tuple-element.75), channel_id=1, source_target_pairs={{0,1},{1,2},{2,3},{3,4},{4,5},{5,6},{6,7},{7,8},{8,9},{9,10},{10,1... | collective-permute-start | bytes 27656 | tf_op jit(solution)/shard_map/ppermute | solution.py:204
  65.6 28.5 %all-to-all-start.1 = ((bf16[256,5,2,128]{3,2,1,0:T(2,128)(2,1)}), bf16[256,5,2,128]{3,2,1,0:T(2,128)(2,1)S(1)}, u32[]{:S(2)}, u32[]{:S(2)}) async-start(bf16[256,5,2,128]{3,2,1,0:T(2,128)(2,1)} %fusion), calls=%async_computation.1 | async-start | bytes 1310720 | tf_op jit(solution)/shard_map/all_to_all | solution.py:249
  74.4 20.4 %collective-permute-start.7 = (bf16[3,64,256]{2,1,0:T(8,128)(2,1)S(1)}, bf16[3,64,256]{2,1,0:T(8,128)(2,1)S(1)}, u32[]{:S(2)}, u32[]{:S(2)}) collective-permute-start(bf16[3,64,256]{2,1,0:T(8,128)(2,1)S(1)} %get-tuple-element.61), channel_id=1, source_target_pairs={{1,0},{2,1},{3,2},{4,3},{5,4},{6,5},{7,6},{8,7},{9,8},{10,9},{11,1... | collective-permute-start | bytes 294920 | tf_op jit(solution)/shard_map/ppermute | solution.py:194
  83.6 13.3 %collective-permute-start.6 = (bf16[3,64,256]{2,1,0:T(8,128)(2,1)S(1)}, bf16[3,64,256]{2,1,0:T(8,128)(2,1)S(1)}, u32[]{:S(2)}, u32[]{:S(2)}) collective-permute-start(bf16[3,64,256]{2,1,0:T(8,128)(2,1)S(1)} %get-tuple-element.62), channel_id=1, source_target_pairs={{0,1},{1,2},{2,3},{3,4},{4,5},{5,6},{6,7},{7,8},{8,9},{9,10},{10,1... | collective-permute-start | bytes 294920 | tf_op jit(solution)/shard_map/ppermute | solution.py:193
  85.6 9.2 %collective-permute-start.9 = (bf16[6,3,256]{2,1,0:T(4,128)(2,1)S(1)}, bf16[6,3,256]{2,1,0:T(4,128)(2,1)S(1)}, u32[]{:S(2)}, u32[]{:S(2)}) collective-permute-start(bf16[6,3,256]{2,1,0:T(4,128)(2,1)S(1)} %get-tuple-element.59), channel_id=1, source_target_pairs={{64,0},{128,64},{192,128},{256,192},{320,256},{384,320},{448,384},... | collective-permute-start | bytes 27656 | tf_op jit(solution)/shard_map/ppermute | solution.py:196
  88.7 41.9 %copy-start = (bf16[1,6,64,256]{3,2,1,0:T(8,128)(2,1)S(1)}, bf16[1,6,64,256]{3,2,1,0:T(8,128)(2,1)}, u32[]{:S(2)}) copy-start(bf16[1,6,64,256]{3,2,1,0:T(8,128)(2,1)} %param.14) | copy-start | bytes 589828
  88.7 6.1 %collective-permute-start.8 = (bf16[6,3,256]{2,1,0:T(4,128)(2,1)S(1)}, bf16[6,3,256]{2,1,0:T(4,128)(2,1)S(1)}, u32[]{:S(2)}, u32[]{:S(2)}) collective-permute-start(bf16[6,3,256]{2,1,0:T(4,128)(2,1)S(1)} %get-tuple-element.60), channel_id=1, source_target_pairs={{0,64},{64,128},{128,192},{192,256},{256,320},{320,384},{384,448},... | collective-permute-start | bytes 27656 | tf_op jit(solution)/shard_map/ppermute | solution.py:195
  98.1 35.3 %all-to-all-start.2 = ((bf16[256,5,2,128]{3,2,1,0:T(2,128)(2,1)}), bf16[256,5,2,128]{3,2,1,0:T(2,128)(2,1)S(1)}, u32[]{:S(2)}, u32[]{:S(2)}) async-start(bf16[256,5,2,128]{3,2,1,0:T(2,128)(2,1)} %broadcast_in_dim.45), calls=%async_computation.2 | async-start | bytes 1310720 | tf_op jit(solution)/shard_map/all_to_all | solution.py:252
  109.5 11.2 %collective-permute-start.11 = (bf16[3,6,256]{2,1,0:T(8,128)(2,1)S(1)}, bf16[3,6,256]{2,1,0:T(8,128)(2,1)S(1)}, u32[]{:S(2)}, u32[]{:S(2)}) collective-permute-start(bf16[3,6,256]{2,1,0:T(8,128)(2,1)S(1)} %get-tuple-element.72), channel_id=1, source_target_pairs={{1,0},{2,1},{3,2},{4,3},{5,4},{6,5},{7,6},{8,7},{9,8},{10,9},{11,1... | collective-permute-start | bytes 27656 | tf_op jit(solution)/shard_map/ppermute | solution.py:205
  118.7 11.9 %collective-permute-start.10 = (bf16[3,6,256]{2,1,0:T(8,128)(2,1)S(1)}, bf16[3,6,256]{2,1,0:T(8,128)(2,1)S(1)}, u32[]{:S(2)}, u32[]{:S(2)}) collective-permute-start(bf16[3,6,256]{2,1,0:T(8,128)(2,1)S(1)} %get-tuple-element.73), channel_id=1, source_target_pairs={{0,1},{1,2},{2,3},{3,4},{4,5},{5,6},{6,7},{7,8},{8,9},{9,10},{10,1... | collective-permute-start | bytes 27656 | tf_op jit(solution)/shard_map/ppermute | solution.py:204
  133.3 8.8 %collective-permute-start.12 = (bf16[256,5,2,128]{3,2,1,0:T(2,128)(2,1)S(1)}, bf16[256,5,2,128]{3,2,1,0:T(2,128)(2,1)S(1)}, u32[]{:S(2)}, u32[]{:S(2)}) collective-permute-start(bf16[256,5,2,128]{3,2,1,0:T(2,128)(2,1)S(1)} %all-to-all-done.2), channel_id=1, source_target_pairs={{0,64},{64,0},{1,65},{65,1},{2,66},{66,2},{3,67},{67,3},{4,68},{68... | collective-permute-start | bytes 1966088 | tf_op jit(solution)/shard_map/ppermute | solution.py:264

commit v3 on v2

--- a/solution.py
+++ b/solution.py
@@ -21,19 +21,30 @@
     return lax.dot_general(a, b, (((ca,), (cb,)), ((), ())), preferred_element_type=F32)
 
 
-def fill_padded(pad_ref, own_ref, up_ref, down_ref, left_ref, right_ref, top_ref, low_ref):
+def fill_padded(odd_ref, pad_ref, own_ref, near_rows_ref, far_rows_ref, near_cols_ref, far_cols_ref):
     rows, cols, _ = own_ref.shape
+    low = rows + 3
+    near_at = jnp.where(odd_ref[0] == 1, 0, low)
+    far_at = low - near_at
     for t in range(2):
         ln = slice(t * LANES, (t + 1) * LANES)
-        pad_ref[t, 0:3, 8 : 8 + cols] = up_ref[:, :, ln].astype(F32)
         pad_ref[t, 3 : 3 + rows, 8 : 8 + cols] = own_ref[:, :, ln].astype(F32)
-        pad_ref[t, 3 + rows : 6 + rows, 8 : 8 + cols] = down_ref[:, :, ln].astype(F32)
-        pad_ref[t, 3 : 3 + rows, 5:8] = left_ref[:, :, ln].astype(F32)
-        pad_ref[t, 3 : 3 + rows, 8 + cols : 11 + cols] = right_ref[:, :, ln].astype(F32)
-        pad_ref[t, 0:3, 5:8] = top_ref[:, 0:3, ln].astype(F32)
-        pad_ref[t, 0:3, 8 + cols : 11 + cols] = top_ref[:, 3:6, ln].astype(F32)
-        pad_ref[t, 3 + rows : 6 + rows, 5:8] = low_ref[:, 0:3, ln].astype(F32)
-        pad_ref[t, 3 + rows : 6 + rows, 8 + cols : 11 + cols] = low_ref[:, 3:6, ln].astype(F32)
+        pad_ref[t, pl.ds(near_at, 3), 8 : 8 + cols] = near_rows_ref[:, :, ln].astype(F32)
+        pad_ref[t, pl.ds(far_at, 3), 8 : 8 + cols] = far_rows_ref[:, :, ln].astype(F32)
+
+    def place(left_ref, right_ref):
+        for t in range(2):
+            ln = slice(t * LANES, (t + 1) * LANES)
+            pad_ref[t, :, 5:8] = left_ref[:, :, ln].astype(F32)
+            pad_ref[t, :, 8 + cols : 11 + cols] = right_ref[:, :, ln].astype(F32)
+
+    @pl.when(odd_ref[1] == 0)
+    def _():
+        place(far_cols_ref, near_cols_ref)
+
+    @pl.when(odd_ref[1] != 0)
+    def _():
+        place(near_cols_ref, far_cols_ref)
 
 
 def convolve(pad_ref, k_ref, out_ref, rows, cols, flip):
@@ -75,7 +86,7 @@
 
 
 def block_kernel(
-    own_ref, up_ref, down_ref, left_ref, right_ref, top_ref, low_ref, mask_ref, masked_ref, k_ref, dw_bias_ref,
+    odd_ref, own_ref, near_rows_ref, far_rows_ref, near_cols_ref, far_cols_ref, mask_ref, masked_ref, k_ref, dw_bias_ref,
     gain_ref, bias_ref, w_in_ref, b_in_ref, w_out_ref, b_out_ref, scale_ref,
     out_ref, grad_ref, big_ref, small_ref,
     pad_ref, depth_ref, terms_ref,
@@ -84,7 +95,7 @@
     cells = rows * cols
     hidden = w_in_ref.shape[1]
     halves = channels // LANES
-    fill_padded(pad_ref, own_ref, up_ref, down_ref, left_ref, right_ref, top_ref, low_ref)
+    fill_padded(odd_ref, pad_ref, own_ref, near_rows_ref, far_rows_ref, near_cols_ref, far_cols_ref)
     convolve(pad_ref, k_ref, depth_ref, rows, cols, False)
     depth = jnp.concatenate([depth_ref[t].reshape(cells, LANES) for t in range(2)], axis=1)
     depth = depth + dw_bias_ref[...]
@@ -150,10 +161,10 @@
 
 
 def state_kernel(
-    own_ref, up_ref, down_ref, left_ref, right_ref, top_ref, low_ref, cot_ref, k_ref, out_ref, pad_ref, sum_ref
+    odd_ref, own_ref, near_rows_ref, far_rows_ref, near_cols_ref, far_cols_ref, cot_ref, k_ref, out_ref, pad_ref, sum_ref
 ):
     rows, cols, _ = own_ref.shape
-    fill_padded(pad_ref, own_ref, up_ref, down_ref, left_ref, right_ref, top_ref, low_ref)
+    fill_padded(odd_ref, pad_ref, own_ref, near_rows_ref, far_rows_ref, near_cols_ref, far_cols_ref)
     convolve(pad_ref, k_ref, sum_ref, rows, cols, True)
     for t in range(2):
         ln = slice(t * LANES, (t + 1) * LANES)
@@ -180,30 +191,38 @@
         write(other_ref, mine_ref)
 
 
-def shifts(axis, wrap):
+def swaps(axis, wrap):
     size = lax.axis_size(axis)
-    up = [(i, (i + 1) % size) for i in range(size if wrap else size - 1)]
-    return up, [(j, i) for i, j in up]
-
-
-def halo_sides(field):
-    rows, cols, _ = field.shape
-    lat_up, lat_down = shifts(LAT, False)
-    lon_up, lon_down = shifts(LON, True)
-    up = lax.ppermute(field[rows - 3 :], LAT, lat_up)
-    down = lax.ppermute(field[:3], LAT, lat_down)
-    left = lax.ppermute(field[:, cols - 3 :], LON, lon_up)
-    right = lax.ppermute(field[:, :3], LON, lon_down)
-    return up, down, left, right
-
-
-def halo_corners(left, right):
-    rows = left.shape[0]
-    lat_up, lat_down = shifts(LAT, False)
-    sides = jnp.concatenate([left, right], axis=1)
-    top = lax.ppermute(sides[rows - 3 :], LAT, lat_up)
-    low = lax.ppermute(sides[:3], LAT, lat_down)
-    return top, low
+    near = [(i, i ^ 1) for i in range(size)]
+    far = []
+    for i in range(1, size if wrap else size - 1, 2):
+        far += [(i, (i + 1) % size), ((i + 1) % size, i)]
+    return near, far
+
+
+def swap_rows(field, odd):
+    rows = field.shape[0]
+    near, far = swaps(LAT, False)
+    first, last = field[:3], field[rows - 3 :]
+    far_rows = lax.ppermute(jnp.where(odd, last, first), LAT, far)
+    near_rows = lax.ppermute(jnp.where(odd, first, last), LAT, near)
+    return near_rows, far_rows
+
+
+def swap_cols(field, near_rows, far_rows, odd_lat, odd_lon):
+    cols = field.shape[1]
+    near, far = swaps(LON, True)
+
+    def strip(at):
+        part = slice(at, at + 3)
+        before = jnp.where(odd_lat, near_rows[:, part], far_rows[:, part])
+        after = jnp.where(odd_lat, far_rows[:, part], near_rows[:, part])
+        return jnp.concatenate([before, field[:, part], after], axis=0)
+
+    first, last = strip(0), strip(cols - 3)
+    far_cols = lax.ppermute(jnp.where(odd_lon, last, first), LON, far)
+    near_cols = lax.ppermute(jnp.where(odd_lon, first, last), LON, near)
+    return near_cols, far_cols
 
 
 def local(
@@ -216,13 +235,17 @@
     core = lax.axis_index("core")
     own = ocean_state[0]
     cot = cotangent[0]
-    up, down, left, right = halo_sides(own)
-    top, low = halo_corners(left, right)
+    odd_lat = lax.axis_index("z") & 1
+    odd = jnp.stack([odd_lat, core]).astype(jnp.int32)
+    odd_lat, odd_lon = odd_lat == 1, core == 1
+    near_rows, far_rows = swap_rows(own, odd_lat)
+    near_cols, far_cols = swap_cols(own, near_rows, far_rows, odd_lat, odd_lon)
     mask = jnp.broadcast_to(land_sea[0].astype(BF16)[..., None], cot.shape)
     masked = mask * cot
     taps = dw_kernel.reshape(49, 2, LANES).transpose(1, 0, 2)
     pad = pltpu.VMEM((2, rows + 6, cols + 16, LANES), F32)
     plane = pltpu.VMEM((2, rows, cols, LANES), F32)
+    smem, vmem = pl.BlockSpec(memory_space=pltpu.SMEM), pl.BlockSpec(memory_space=pltpu.VMEM)
     params = pltpu.CompilerParams(vmem_limit_bytes=VMEM_BYTES)
     output, grad_depth, big, small = pl.pallas_call(
         block_kernel,
@@ -232,34 +255,35 @@
             jax.ShapeDtypeStruct((4 * hidden, LANES), BF16),
             jax.ShapeDtypeStruct((2, 64, LANES), F32),
         ),
+        in_specs=[smem] + [vmem] * 16,
         scratch_shapes=[pad, plane, pltpu.VMEM((2, 7, 7, 8, LANES), F32)],
         compiler_params=params,
         cost_estimate=pl.CostEstimate(flops=1300000000, transcendentals=400000, bytes_accessed=6000000),
         name="block",
     )(
-        own, up, down, left, right, top, low, mask.reshape(cells, channels), masked.reshape(cells, channels), taps,
+        odd, own, near_rows, far_rows, near_cols, far_cols, mask.reshape(cells, channels), masked.reshape(cells, channels), taps,
         dw_bias[None], ln_gain[None], ln_bias[None], w_in, b_in[None], w_out, b_out[None], layer_scale[None],
     )
-    sides = halo_sides(grad_depth)
+    rows_sent = swap_rows(grad_depth, odd_lat)
     small_rows = small.transpose(1, 0, 2).astype(BF16)
     small_rows = jnp.pad(small_rows, ((0, 2 * far - 64), (0, 0), (0, 0)))[:, None]
     chunks = jnp.concatenate([big.reshape(2 * far, 4, 2, LANES), small_rows], axis=1)
-    pair = lax.all_to_all(chunks.reshape(2, far, 5, 2, LANES), "core", 0, 0)
+    pair = lax.all_to_all(chunks.reshape(2, far * 10, LANES), "core", 0, 0)
     value = (pair[0].astype(F32) + pair[1].astype(F32)).astype(BF16)
-    value = lax.all_to_all(value, FAR, 0, 0)
+    value = lax.all_to_all(value.reshape(far, 5, 2, LANES), FAR, 0, 0)
     value = jnp.sum(value.astype(F32), axis=0).astype(BF16)
-    value, sides = lax.optimization_barrier((value, sides))
+    value, rows_sent = lax.optimization_barrier((value, rows_sent))
     value = lax.all_to_all(jnp.broadcast_to(value[None], (far, 5, 2, LANES)), FAR, 0, 0)
-    g_up, g_down, g_left, g_right = sides
-    g_top, g_low = halo_corners(g_left, g_right)
+    cols_sent = swap_cols(grad_depth, *rows_sent, odd_lat, odd_lon)
     grad_state = pl.pallas_call(
         state_kernel,
         out_shape=jax.ShapeDtypeStruct((rows, cols, channels), BF16),
+        in_specs=[smem] + [vmem] * 7,
         scratch_shapes=[pad, plane],
         compiler_params=params,
         cost_estimate=pl.CostEstimate(flops=10000000, transcendentals=0, bytes_accessed=3000000),
         name="state",
-    )(grad_depth, g_up, g_down, g_left, g_right, g_top, g_low, cot, taps)
+    )(odd, grad_depth, *rows_sent, *cols_sent, cot, taps)
     value, grad_state = lax.optimization_barrier((value, grad_state))
     other = lax.ppermute(value, "core", [(0, 1), (1, 0)])
     total_cells = cells * lax.axis_size(LON) * lax.axis_size(LAT)
@@ -270,11 +294,7 @@
             jax.ShapeDtypeStruct((channels, hidden), F32),
             jax.ShapeDtypeStruct((hidden, channels), F32),
         ),
-        in_specs=[
-            pl.BlockSpec(memory_space=pltpu.SMEM),
-            pl.BlockSpec(memory_space=pltpu.VMEM),
-            pl.BlockSpec(memory_space=pltpu.VMEM),
-        ],
+        in_specs=[smem, vmem, vmem],
         compiler_params=params,
         name="unpack",
     )(

time: 147 us -> 131 us (0.89)
  the two profiles are of different devices: /device:TPU:7 before, /device:TPU:1 now
where the time goes in v3:
time: 131 us; the launch traced here: 130 us
  starting transfers between devices  71 us (54%)
  waiting for transfers between devices  27.1 us (21%)
  Pallas kernels  12.5 us (10%)
  other arithmetic  6.5 us (5%)
  blocking collectives  6.14 us (5%)
  local copies, waits for them, and re-layouts  5.94 us (5%)
    all_to_all x1, starting transfers between devices, local(): value = lax.all_to_all(value.reshape(far, 5, 2, LANES), FAR, 0, 0)  24.5 us
    all_to_all x1, waiting for transfers between devices, local(): value = lax.all_to_all(value.reshape(far, 5, 2, LANES), FAR, 0, 0)  16.2 us
    ppermute x2, starting transfers between devices, swap_rows(): near_rows = lax.ppermute(jnp.where(odd, first, last), LAT, near)  12.3 us
    all_to_all x1, starting transfers between devices, local(): lax.all_to_all(jnp.broadcast_to(value[None], (far, 5, 2, LANES)), FAR, 0, 0)  12.1 us
    ppermute x2, starting transfers between devices, swap_cols(): far_cols = lax.ppermute(jnp.where(odd_lon, last, first), LON, far)  8.56 us
    pallas_call x1, Pallas kernels, local(): pl.pallas_call(block_kernel, out_shape=(jax.ShapeDtypeStruct((rows, cols,...  7.65 us
    ppermute x2, waiting for transfers between devices, swap_cols(): far_cols = lax.ppermute(jnp.where(odd_lon, last, first), LON, far)  7.44 us
    ppermute x1, starting transfers between devices, local(): other = lax.ppermute(value, 'core', [(0, 1), (1, 0)])  6.88 us
  transfers between devices with their start and end apart: 11, of which 4 were waited for; matrix products, arithmetic and copies ran while one was open for 4% of the time, Pallas kernels for 3%

profile of v3, /device:TPU:1, one launch (start us, length us, event | category | flops | bytes accessed | tf_op | source)
XLA Modules:
  0.0 130.2 jit_solution(14022348650035998732)
XLA Ops:
  0.7 1.1 select_bitcast_fusion
  1.8 0.7 collective-permute-start.1
  2.5 8.2 %collective-permute-start = (bf16[3,64,256]{2,1,0:T(8,128)(2,1)S(1)}, bf16[3,64,256]{2,1,0:T(8,128)(2,1)S(1)}, u32[]{:S(2)}, u32[]{:S(2)}) collective-permute-start(bf16[3,64,256]{2,1,0:T(8,128)(2,1)S(1)} %get-tuple-element.70), channel_id=1, source_target_pairs={{0,1},{1,0},{2,3},{3,2},{4,5},{5,4},{6,7},{7,6},{8,9},{9,8},{10,11... | collective-permute-start | bytes 294920 | tf_op jit(solution)/shard_map/ppermute | solution.py:208
  10.7 0.7 convert_reduce_fusion
  11.5 1.0 bitcast_multiply_fusion.masked_ref
  12.5 0.8 fusion.1
  13.4 4.3 %collective-permute-start.3 = (bf16[12,3,256]{2,1,0:T(4,128)(2,1)S(1)}, bf16[12,3,256]{2,1,0:T(4,128)(2,1)S(1)}, u32[]{:S(2)}, u32[]{:S(2)}) collective-permute-start(bf16[12,3,256]{2,1,0:T(4,128)(2,1)S(1)} %get-tuple-element.78), channel_id=1, source_target_pairs={{64,128},{128,64},{192,256},{256,192},{320,384},{384,320},{448,0},... | collective-permute-start | bytes 55304 | tf_op jit(solution)/shard_map/ppermute | solution.py:223
  17.7 3.2 %collective-permute-start.2 = (bf16[12,3,256]{2,1,0:T(4,128)(2,1)S(1)}, bf16[12,3,256]{2,1,0:T(4,128)(2,1)S(1)}, u32[]{:S(2)}, u32[]{:S(2)}) collective-permute-start(bf16[12,3,256]{2,1,0:T(4,128)(2,1)S(1)} %get-tuple-element.79), channel_id=1, source_target_pairs={{0,64},{64,0},{128,192},{192,128},{256,320},{320,256},{384,448},{4... | collective-permute-start | bytes 55304 | tf_op jit(solution)/shard_map/ppermute | solution.py:224
  21.0 0.8 reshape.105
  22.1 7.7 %block.1 = (bf16[6,64,256]{2,1,0:T(8,128)(2,1)}, bf16[6,64,256]{2,1,0:T(8,128)(2,1)S(1)}, bf16[4096,128]{1,0:T(8,128)(2,1)S(1)}, f32[2,64,128]{2,1,0:T(8,128)S(1)}) custom-call(s32[2]{0:T(128)S(1)} %pad_add_fusion.odd_ref, bf16[6,64,256]{2,1,0:T(8,128)(2,1)S(1)} %bitcast.47, bf16[3,64,256]{2,1,0:T(8,128)(2,1)S(1)} %collective-permute-done.near_rows_ref, ...), custom_call_target="tpu_custom_call" | custom-call | flops 1300000000 | bytes 6000000 | tf_op jit(solution)/shard_map/block/pallas_call | solution.py:250
  30.1 1.8 %pad_maximum_fusion = bf16[512,5,2,128]{3,2,1,0:T(2,128)(2,1)S(1)} fusion(bf16[512,1,2,128]{3,2,1,0:T(2,128)(2,1)S(1)} %copy.30, bf16[512,4,2,128]{3,2,1,0:T(2,128)(2,1)S(1)} %bitcast.44), kind=kLoop, calls=%fused_computation | loop fusion | flops 655360 | bytes 2621440 | tf_op jit(solution)/shard_map/concatenate | solution.py:270
  31.8 6.1 %all_to_all.15 = bf16[2,2560,128]{2,1,0:T(8,128)(2,1)S(1)} all-to-all(bf16[2,2560,128]{2,1,0:T(8,128)(2,1)S(1)} %bitcast.56), channel_id=1, replica_groups=mesh['y_lo'=4,'core'=2,'x'=4,'y_hi'=2,'z'=8] {'core'}, dimensions={0} | all-to-all | bytes 2621440 | tf_op jit(solution)/shard_map/all_to_all | solution.py:271
  38.0 1.0 add_convert_fusion
  39.0 24.5 %all-to-all-start.1 = ((bf16[256,5,2,128]{3,2,1,0:T(2,128)(2,1)}), bf16[256,5,2,128]{3,2,1,0:T(2,128)(2,1)S(1)}, u32[]{:S(2)}, u32[]{:S(2)}) async-start(bf16[256,5,2,128]{3,2,1,0:T(2,128)(2,1)} %bitcast.18), calls=%async_computation.1 | async-start | bytes 1310720 | tf_op jit(solution)/shard_map/all_to_all | solution.py:273
  63.6 0.7 collective-permute-start.5
  64.2 4.2 %collective-permute-start.4 = (bf16[3,64,256]{2,1,0:T(8,128)(2,1)S(1)}, bf16[3,64,256]{2,1,0:T(8,128)(2,1)S(1)}, u32[]{:S(2)}, u32[]{:S(2)}) collective-permute-start(bf16[3,64,256]{2,1,0:T(8,128)(2,1)S(1)} %get-tuple-element.62), channel_id=1, source_target_pairs={{0,1},{1,0},{2,3},{3,2},{4,5},{5,4},{6,7},{7,6},{8,9},{9,8},{10,11... | collective-permute-start | bytes 294920 | tf_op jit(solution)/shard_map/ppermute | solution.py:208
  68.4 16.2 %all-to-all-done.1 = bf16[256,5,2,128]{3,2,1,0:T(2,128)(2,1)S(1)} async-done(((bf16[256,5,2,128]{3,2,1,0:T(2,128)(2,1)}), bf16[256,5,2,128]{3,2,1,0:T(2,128)(2,1)S(1)}, u32[]{:S(2)}, u32[]{:S(2)}) %all-to-all-start.1) | async-done | bytes 655392 | tf_op jit(solution)/shard_map/all_to_all | solution.py:273
  84.6 0.6 reduce_sum.12
  85.3 1.2 broadcast_in_dim.48
  86.4 12.1 %all-to-all-start.2 = ((bf16[256,5,2,128]{3,2,1,0:T(2,128)(2,1)}), bf16[256,5,2,128]{3,2,1,0:T(2,128)(2,1)S(1)}, u32[]{:S(2)}, u32[]{:S(2)}) async-start(bf16[256,5,2,128]{3,2,1,0:T(2,128)(2,1)} %broadcast_in_dim.48), calls=%async_computation.2 | async-start | bytes 1310720 | tf_op jit(solution)/shard_map/all_to_all | solution.py:276
  98.6 4.2 %collective-permute-start.7 = (bf16[12,3,256]{2,1,0:T(4,128)(2,1)S(1)}, bf16[12,3,256]{2,1,0:T(4,128)(2,1)S(1)}, u32[]{:S(2)}, u32[]{:S(2)}) collective-permute-start(bf16[12,3,256]{2,1,0:T(4,128)(2,1)S(1)} %get-tuple-element.76), channel_id=1, source_target_pairs={{64,128},{128,64},{192,256},{256,192},{320,384},{384,320},{448,0},... | collective-permute-start | bytes 55304 | tf_op jit(solution)/shard_map/ppermute | solution.py:223
  102.9 2.1 %collective-permute-start.6 = (bf16[12,3,256]{2,1,0:T(4,128)(2,1)S(1)}, bf16[12,3,256]{2,1,0:T(4,128)(2,1)S(1)}, u32[]{:S(2)}, u32[]{:S(2)}) collective-permute-start(bf16[12,3,256]{2,1,0:T(4,128)(2,1)S(1)} %get-tuple-element.77), channel_id=1, source_target_pairs={{0,64},{64,0},{128,192},{192,128},{256,320},{320,256},{384,448},{4... | collective-permute-start | bytes 55304 | tf_op jit(solution)/shard_map/ppermute | solution.py:224
  104.9 7.4 %collective-permute-done.7.far_cols_ref = bf16[12,3,256]{2,1,0:T(4,128)(2,1)S(1)} collective-permute-done((bf16[12,3,256]{2,1,0:T(4,128)(2,1)S(1)}, bf16[12,3,256]{2,1,0:T(4,128)(2,1)S(1)}, u32[]{:S(2)}, u32[]{:S(2)}) %collective-permute-start.7) | collective-permute-done | bytes 18464 | tf_op jit(solution)/shard_map/ppermute | solution.py:223
  112.4 3.3 %state.1 = bf16[6,64,256]{2,1,0:T(8,128)(2,1)} custom-call(s32[2]{0:T(128)S(1)} %pad_add_fusion.odd_ref, bf16[6,64,256]{2,1,0:T(8,128)(2,1)S(1)} %get-tuple-element.25.own_ref, bf16[3,64,256]{2,1,0:T(8,128)(2,1)S(1)} %collective-permute-done.4.near_rows_ref, bf16[3,64,256]{2,1,0:T(8,128)(2,1)S(1)} %collective-permute-done.5.far_rows_ref, ...), custom_call_target="tpu_custom_call" | custom-call | flops 10000000 | bytes 3000000 | tf_op jit(solution)/shard_map/state/pallas_call | solution.py:278
  115.7 2.1 %all-to-all-done.2 = bf16[256,5,2,128]{3,2,1,0:T(2,128)(2,1)S(1)} async-done(((bf16[256,5,2,128]{3,2,1,0:T(2,128)(2,1)}), bf16[256,5,2,128]{3,2,1,0:T(2,128)(2,1)S(1)}, u32[]{:S(2)}, u32[]{:S(2)}) %all-to-all-start.2) | async-done | bytes 655392 | tf_op jit(solution)/shard_map/all_to_all | solution.py:276
  117.8 6.9 %collective-permute-start.8 = (bf16[256,5,2,128]{3,2,1,0:T(2,128)(2,1)S(1)}, bf16[256,5,2,128]{3,2,1,0:T(2,128)(2,1)S(1)}, u32[]{:S(2)}, u32[]{:S(2)}) collective-permute-start(bf16[256,5,2,128]{3,2,1,0:T(2,128)(2,1)S(1)} %all-to-all-done.2), channel_id=1, source_target_pairs={{0,64},{64,0},{1,65},{65,1},{2,66},{66,2},{3,67},{67,3},{4,68},{68... | collective-permute-start | bytes 1966088 | tf_op jit(solution)/shard_map/ppermute | solution.py:288
  124.7 0.4 slice.135
  125.1 1.3 %collective-permute-done.8 = bf16[256,5,2,128]{3,2,1,0:T(2,128)(2,1)S(1)} collective-permute-done((bf16[256,5,2,128]{3,2,1,0:T(2,128)(2,1)S(1)}, bf16[256,5,2,128]{3,2,1,0:T(2,128)(2,1)S(1)}, u32[]{:S(2)}, u32[]{:S(2)}) %collective-permute-start.8) | collective-permute-done | bytes 655392 | tf_op jit(solution)/shard_map/ppermute | solution.py:288
  126.5 0.6 slice.154
  127.1 0.6 slice_bitcast_fusion
  127.7 0.6 copy.31
  128.7 1.5 %unpack.1 = (f32[256,1024]{1,0:T(8,128)}, f32[1024,256]{1,0:T(8,128)}) custom-call(s32[1]{0:T(128)} %bitcast.1.core_ref, bf16[2048,128]{1,0:T(8,128)(2,1)S(1)} %bitcast.42, bf16[2048,128]{1,0:T(8,128)(2,1)S(1)} %bitcast.43), custom_call_target="tpu_custom_call" | custom-call | tf_op jit(solution)/shard_map/unpack/pallas_call | solution.py:291
  (44 shorter events, 1.3 us)
Async XLA Ops:
  0.6 21.4 %copy-start.1 = (bf16[1,6,64,256]{3,2,1,0:T(8,128)(2,1)S(1)}, bf16[1,6,64,256]{3,2,1,0:T(8,128)(2,1)}, u32[]{:S(2)}) copy-start(bf16[1,6,64,256]{3,2,1,0:T(8,128)(2,1)} %param.12) | copy-start | bytes 589828
  0.7 21.4 %copy-start.9 = (f32[256]{0:T(256)S(1)}, f32[256]{0:T(256)}, u32[]{:S(2)}) copy-start(f32[256]{0:T(256)} %param.23) | copy-start | bytes 3076
  0.7 21.4 %copy-start.8 = (f32[256]{0:T(256)S(1)}, f32[256]{0:T(256)}, u32[]{:S(2)}) copy-start(f32[256]{0:T(256)} %param.22) | copy-start | bytes 3076
  0.7 21.4 %copy-start.3 = (bf16[1024,256]{1,0:T(8,128)(2,1)S(1)}, bf16[1024,256]{1,0:T(8,128)(2,1)}, u32[]{:S(2)}) copy-start(bf16[1024,256]{1,0:T(8,128)(2,1)} %w_out_ref.1) | copy-start | bytes 1572868
  0.7 21.4 %copy-start.4 = (f32[1024]{0:T(1024)S(1)}, f32[1024]{0:T(1024)}, u32[]{:S(2)}) copy-start(f32[1024]{0:T(1024)} %param.20) | copy-start | bytes 12292
  0.7 21.4 %copy-start.2 = (bf16[256,1024]{1,0:T(8,128)(2,1)S(1)}, bf16[256,1024]{1,0:T(8,128)(2,1)}, u32[]{:S(2)}) copy-start(bf16[256,1024]{1,0:T(8,128)(2,1)} %w_in_ref.1) | copy-start | bytes 1572868
  0.7 21.4 %copy-start.7 = (f32[256]{0:T(256)S(1)}, f32[256]{0:T(256)}, u32[]{:S(2)}) copy-start(f32[256]{0:T(256)} %param.18) | copy-start | bytes 3076
  0.7 21.4 %copy-start.6 = (f32[256]{0:T(256)S(1)}, f32[256]{0:T(256)}, u32[]{:S(2)}) copy-start(f32[256]{0:T(256)} %param.17) | copy-start | bytes 3076
  0.7 21.4 %copy-start.5 = (f32[256]{0:T(256)S(1)}, f32[256]{0:T(256)}, u32[]{:S(2)}) copy-start(f32[256]{0:T(256)} %param.16) | copy-start | bytes 3076
  1.8 11.5 %collective-permute-start.1 = (bf16[3,64,256]{2,1,0:T(8,128)(2,1)S(1)}, bf16[3,64,256]{2,1,0:T(8,128)(2,1)S(1)}, u32[]{:S(2)}, u32[]{:S(2)}) collective-permute-start(bf16[3,64,256]{2,1,0:T(8,128)(2,1)S(1)} %get-tuple-element.69), channel_id=1, source_target_pairs={{1,2},{2,1},{3,4},{4,3},{5,6},{6,5},{7,8},{8,7},{9,10},{10,9},{11,... | collective-permute-start | bytes 294920 | tf_op jit(solution)/shard_map/ppermute | solution.py:207
  2.5 10.8 %collective-permute-start = (bf16[3,64,256]{2,1,0:T(8,128)(2,1)S(1)}, bf16[3,64,256]{2,1,0:T(8,128)(2,1)S(1)}, u32[]{:S(2)}, u32[]{:S(2)}) collective-permute-start(bf16[3,64,256]{2,1,0:T(8,128)(2,1)S(1)} %get-tuple-element.70), channel_id=1, source_target_pairs={{0,1},{1,0},{2,3},{3,2},{4,5},{5,4},{6,7},{7,6},{8,9},{9,8},{10,11... | collective-permute-start | bytes 294920 | tf_op jit(solution)/shard_map/ppermute | solution.py:208
  13.4 8.5 %collective-permute-start.3 = (bf16[12,3,256]{2,1,0:T(4,128)(2,1)S(1)}, bf16[12,3,256]{2,1,0:T(4,128)(2,1)S(1)}, u32[]{:S(2)}, u32[]{:S(2)}) collective-permute-start(bf16[12,3,256]{2,1,0:T(4,128)(2,1)S(1)} %get-tuple-element.78), channel_id=1, source_target_pairs={{64,128},{128,64},{192,256},{256,192},{320,384},{384,320},{448,0},... | collective-permute-start | bytes 55304 | tf_op jit(solution)/shard_map/ppermute | solution.py:223
  17.7 4.2 %collective-permute-start.2 = (bf16[12,3,256]{2,1,0:T(4,128)(2,1)S(1)}, bf16[12,3,256]{2,1,0:T(4,128)(2,1)S(1)}, u32[]{:S(2)}, u32[]{:S(2)}) collective-permute-start(bf16[12,3,256]{2,1,0:T(4,128)(2,1)S(1)} %get-tuple-element.79), channel_id=1, source_target_pairs={{0,64},{64,0},{128,192},{192,128},{256,320},{320,256},{384,448},{4... | collective-permute-start | bytes 55304 | tf_op jit(solution)/shard_map/ppermute | solution.py:224
  39.0 45.6 %all-to-all-start.1 = ((bf16[256,5,2,128]{3,2,1,0:T(2,128)(2,1)}), bf16[256,5,2,128]{3,2,1,0:T(2,128)(2,1)S(1)}, u32[]{:S(2)}, u32[]{:S(2)}) async-start(bf16[256,5,2,128]{3,2,1,0:T(2,128)(2,1)} %bitcast.18), calls=%async_computation.1 | async-start | bytes 1310720 | tf_op jit(solution)/shard_map/all_to_all | solution.py:273
  63.6 21.7 %collective-permute-start.5 = (bf16[3,64,256]{2,1,0:T(8,128)(2,1)S(1)}, bf16[3,64,256]{2,1,0:T(8,128)(2,1)S(1)}, u32[]{:S(2)}, u32[]{:S(2)}) collective-permute-start(bf16[3,64,256]{2,1,0:T(8,128)(2,1)S(1)} %get-tuple-element.61), channel_id=1, source_target_pairs={{1,2},{2,1},{3,4},{4,3},{5,6},{6,5},{7,8},{8,7},{9,10},{10,9},{11,... | collective-permute-start | bytes 294920 | tf_op jit(solution)/shard_map/ppermute | solution.py:207
  64.2 48.1 %copy-start = (bf16[1,6,64,256]{3,2,1,0:T(8,128)(2,1)S(1)}, bf16[1,6,64,256]{3,2,1,0:T(8,128)(2,1)}, u32[]{:S(2)}) copy-start(bf16[1,6,64,256]{3,2,1,0:T(8,128)(2,1)} %param.14) | copy-start | bytes 589828
  64.2 21.0 %collective-permute-start.4 = (bf16[3,64,256]{2,1,0:T(8,128)(2,1)S(1)}, bf16[3,64,256]{2,1,0:T(8,128)(2,1)S(1)}, u32[]{:S(2)}, u32[]{:S(2)}) collective-permute-start(bf16[3,64,256]{2,1,0:T(8,128)(2,1)S(1)} %get-tuple-element.62), channel_id=1, source_target_pairs={{0,1},{1,0},{2,3},{3,2},{4,5},{5,4},{6,7},{7,6},{8,9},{9,8},{10,11... | collective-permute-start | bytes 294920 | tf_op jit(solution)/shard_map/ppermute | solution.py:208
  86.4 31.4 %all-to-all-start.2 = ((bf16[256,5,2,128]{3,2,1,0:T(2,128)(2,1)}), bf16[256,5,2,128]{3,2,1,0:T(2,128)(2,1)S(1)}, u32[]{:S(2)}, u32[]{:S(2)}) async-start(bf16[256,5,2,128]{3,2,1,0:T(2,128)(2,1)} %broadcast_in_dim.48), calls=%async_computation.2 | async-start | bytes 1310720 | tf_op jit(solution)/shard_map/all_to_all | solution.py:276
  98.6 13.7 %collective-permute-start.7 = (bf16[12,3,256]{2,1,0:T(4,128)(2,1)S(1)}, bf16[12,3,256]{2,1,0:T(4,128)(2,1)S(1)}, u32[]{:S(2)}, u32[]{:S(2)}) collective-permute-start(bf16[12,3,256]{2,1,0:T(4,128)(2,1)S(1)} %get-tuple-element.76), channel_id=1, source_target_pairs={{64,128},{128,64},{192,256},{256,192},{320,384},{384,320},{448,0},... | collective-permute-start | bytes 55304 | tf_op jit(solution)/shard_map/ppermute | solution.py:223
  102.9 9.5 %collective-permute-start.6 = (bf16[12,3,256]{2,1,0:T(4,128)(2,1)S(1)}, bf16[12,3,256]{2,1,0:T(4,128)(2,1)S(1)}, u32[]{:S(2)}, u32[]{:S(2)}) collective-permute-start(bf16[12,3,256]{2,1,0:T(4,128)(2,1)S(1)} %get-tuple-element.77), channel_id=1, source_target_pairs={{0,64},{64,0},{128,192},{192,128},{256,320},{320,256},{384,448},{4... | collective-permute-start | bytes 55304 | tf_op jit(solution)/shard_map/ppermute | solution.py:224
  117.8 8.6 %collective-permute-start.8 = (bf16[256,5,2,128]{3,2,1,0:T(2,128)(2,1)S(1)}, bf16[256,5,2,128]{3,2,1,0:T(2,128)(2,1)S(1)}, u32[]{:S(2)}, u32[]{:S(2)}) collective-permute-start(bf16[256,5,2,128]{3,2,1,0:T(2,128)(2,1)S(1)} %all-to-all-done.2), channel_id=1, source_target_pairs={{0,64},{64,0},{1,65},{65,1},{2,66},{66,2},{3,67},{67,3},{4,68},{68... | collective-permute-start | bytes 1966088 | tf_op jit(solution)/shard_map/ppermute | solution.py:288

commit v4 on v3

--- a/solution.py
+++ b/solution.py
@@ -10,7 +10,10 @@
 
 LON = ("y_lo", "core")
 LAT = ("x", "y_hi", "z")
-FAR = ("x", "y_hi", "y_lo", "z")
+PLANE = ("x", "z")
+COLUMN = ("y_hi", "y_lo")
+BIG_ROWS = 64
+CHUNK_ROWS = 72
 LANES = 128
 VMEM_BYTES = 44 << 20
 F32 = jnp.float32
@@ -48,24 +51,24 @@
 
 
 def convolve(pad_ref, k_ref, out_ref, rows, cols, flip):
-    blocks = cols // 8
-
-    def step(n, carry):
-        t = n // blocks
-        at = pl.multiple_of((n % blocks) * 8, 8)
-        acc = [jnp.zeros((8, LANES), F32) for _ in range(rows)]
-        for j in range(7):
-            window = [pad_ref[t, r, pl.ds(at + 5 + j, 8), :] for r in range(rows + 6)]
-            for i in range(7):
-                tap = (6 - i) * 7 + 6 - j if flip else i * 7 + j
-                weight = k_ref[t, tap : tap + 1, :]
-                for p in range(rows):
-                    acc[p] = acc[p] + window[p + i] * weight
-        for p in range(rows):
-            out_ref[t, p, pl.ds(at, 8), :] = acc[p]
-        return carry
-
-    lax.fori_loop(0, 2 * blocks, step, 0)
+    for t in range(2):
+        ln = slice(t * LANES, (t + 1) * LANES)
+
+        def step(n, carry, t=t, ln=ln):
+            at = pl.multiple_of(n * 8, 8)
+            acc = [jnp.zeros((8, LANES), F32) for _ in range(rows)]
+            for j in range(7):
+                window = [pad_ref[t, r, pl.ds(at + 5 + j, 8), :] for r in range(rows + 6)]
+                for i in range(7):
+                    row, col = (6 - i, 6 - j) if flip else (i, j)
+                    weight = k_ref[row, col : col + 1, ln]
+                    for p in range(rows):
+                        acc[p] = acc[p] + window[p + i] * weight
+            for p in range(rows):
+                out_ref[t, p, pl.ds(at, 8), :] = acc[p]
+            return carry
+
+        lax.fori_loop(0, cols // 8, step, 0)
 
 
 def kernel_sums(pad_ref, grad_ref, out_ref, rows, cols):
@@ -85,11 +88,16 @@
     lax.fori_loop(0, 14, step, 0)
 
 
+def write_chunks(chunk_ref, base, part):
+    for n in range(part.shape[0] // BIG_ROWS):
+        chunk_ref[base + n, 0:BIG_ROWS, :] = part[n * BIG_ROWS : (n + 1) * BIG_ROWS]
+
+
 def block_kernel(
     odd_ref, own_ref, near_rows_ref, far_rows_ref, near_cols_ref, far_cols_ref, mask_ref, masked_ref, k_ref, dw_bias_ref,
     gain_ref, bias_ref, w_in_ref, b_in_ref, w_out_ref, b_out_ref, scale_ref,
-    out_ref, grad_ref, big_ref, small_ref,
-    pad_ref, depth_ref, terms_ref,
+    out_ref, grad_ref, chunk_ref,
+    pad_ref, depth_ref, terms_ref, small_ref,
 ):
     rows, cols, channels = own_ref.shape
     cells = rows * cols
@@ -126,11 +134,11 @@
         g_in = dot(normed, grad_pre, 0, 0).astype(BF16)
         g_out = dot(act, grad_branch, 0, 0).astype(BF16)
         for t in range(width // LANES):
-            base = (h * (width // LANES) + t) * channels
-            big_ref[base : base + channels, :] = g_in[:, t * LANES : (t + 1) * LANES]
+            base = (h * (width // LANES) + t) * (channels // BIG_ROWS)
+            write_chunks(chunk_ref, base, g_in[:, t * LANES : (t + 1) * LANES])
         for t in range(halves):
-            base = hidden * halves + t * hidden + h * width
-            big_ref[base : base + width, :] = g_out[:, t * LANES : (t + 1) * LANES]
+            base = (hidden * halves + t * hidden + h * width) // BIG_ROWS
+            write_chunks(chunk_ref, base, g_out[:, t * LANES : (t + 1) * LANES])
         b_in_sums.append(jnp.sum(grad_pre.astype(F32), axis=0, keepdims=True))
     branch = branch + b_out_ref[...]
     mask = mask_ref[...].astype(F32)
@@ -158,6 +166,14 @@
         for n, single in enumerate(singles):
             small_ref[t, 49 + n : 50 + n, :] = single[:, ln]
         small_ref[t, 49 + len(singles) :, :] = jnp.zeros((64 - 49 - len(singles), LANES), F32)
+    chunks = chunk_ref.shape[0]
+    for c in range(chunks):
+        n = c % (chunks // 2)
+        if n < 16:
+            piece = small_ref[n // 8, (n % 8) * 8 : (n % 8) * 8 + 8, :].astype(BF16)
+        else:
+            piece = jnp.zeros((8, LANES), BF16)
+        chunk_ref[c, BIG_ROWS:, :] = piece
 
 
 def state_kernel(
@@ -171,16 +187,20 @@
         out_ref[:, :, ln] = (cot_ref[:, :, ln].astype(F32) + sum_ref[t]).astype(BF16)
 
 
-def unpack_kernel(factor, core_ref, mine_ref, other_ref, w_in_ref, w_out_ref):
+def unpack_kernel(
+    factor, core_ref, mine_ref, other_ref, k_ref, singles_ref, w_in_ref, b_in_ref, w_out_ref, small_ref
+):
     channels, hidden = w_in_ref.shape
+
+    def rows_of(ref, at, size):
+        part = ref[at // BIG_ROWS : (at + size) // BIG_ROWS, 0:BIG_ROWS, :]
+        return part.astype(F32).reshape(size, LANES) * factor
 
     def write(first_ref, second_ref):
         for t in range(hidden // LANES):
-            part = first_ref[t * channels : (t + 1) * channels, :]
-            w_in_ref[:, t * LANES : (t + 1) * LANES] = part.astype(F32) * factor
+            w_in_ref[:, t * LANES : (t + 1) * LANES] = rows_of(first_ref, t * channels, channels)
         for t in range(channels // LANES):
-            part = second_ref[t * hidden : (t + 1) * hidden, :]
-            w_out_ref[:, t * LANES : (t + 1) * LANES] = part.astype(F32) * factor
+            w_out_ref[:, t * LANES : (t + 1) * LANES] = rows_of(second_ref, t * hidden, hidden)
 
     @pl.when(core_ref[0] == 0)
     def _():
@@ -189,6 +209,21 @@
     @pl.when(core_ref[0] != 0)
     def _():
         write(other_ref, mine_ref)
+
+    small_ref[...] = mine_ref[0:16, BIG_ROWS:, :].astype(F32).reshape(128, LANES) * factor
+    blocks = hidden // channels
+    for t in range(2):
+        ln = slice(t * LANES, (t + 1) * LANES)
+        for j in range(7):
+            for i in range(7):
+                at = t * 64 + j * 7 + i
+                k_ref[i, j : j + 1, ln] = small_ref[at : at + 1, :]
+        at = t * 64 + 49
+        for n in range(blocks):
+            part = slice(n * channels + t * LANES, n * channels + (t + 1) * LANES)
+            b_in_ref[:, part] = small_ref[at + n : at + n + 1, :]
+        for n in range(5):
+            singles_ref[n, :, ln] = small_ref[at + blocks + n : at + blocks + n + 1, :]
 
 
 def swaps(axis, wrap):
@@ -231,7 +266,7 @@
     _, rows, cols, channels = ocean_state.shape
     cells = rows * cols
     hidden = w_in.shape[1]
-    far = lax.axis_size(FAR)
+    plane, column = lax.axis_size(PLANE), lax.axis_size(COLUMN)
     core = lax.axis_index("core")
     own = ocean_state[0]
     cot = cotangent[0]
@@ -242,83 +277,80 @@
     near_cols, far_cols = swap_cols(own, near_rows, far_rows, odd_lat, odd_lon)
     mask = jnp.broadcast_to(land_sea[0].astype(BF16)[..., None], cot.shape)
     masked = mask * cot
-    taps = dw_kernel.reshape(49, 2, LANES).transpose(1, 0, 2)
     pad = pltpu.VMEM((2, rows + 6, cols + 16, LANES), F32)
-    plane = pltpu.VMEM((2, rows, cols, LANES), F32)
+    cells_scratch = pltpu.VMEM((2, rows, cols, LANES), F32)
     smem, vmem = pl.BlockSpec(memory_space=pltpu.SMEM), pl.BlockSpec(memory_space=pltpu.VMEM)
     params = pltpu.CompilerParams(vmem_limit_bytes=VMEM_BYTES)
-    output, grad_depth, big, small = pl.pallas_call(
+    output, grad_depth, chunks = pl.pallas_call(
         block_kernel,
         out_shape=(
             jax.ShapeDtypeStruct((rows, cols, channels), BF16),
             jax.ShapeDtypeStruct((rows, cols, channels), BF16),
-            jax.ShapeDtypeStruct((4 * hidden, LANES), BF16),
-            jax.ShapeDtypeStruct((2, 64, LANES), F32),
+            jax.ShapeDtypeStruct((2 * plane, CHUNK_ROWS, LANES), BF16),
         ),
         in_specs=[smem] + [vmem] * 16,
-        scratch_shapes=[pad, plane, pltpu.VMEM((2, 7, 7, 8, LANES), F32)],
+        scratch_shapes=[
+            pad,
+            cells_scratch,
+            pltpu.VMEM((2, 7, 7, 8, LANES), F32),
+            pltpu.VMEM((2, 64, LANES), F32),
+        ],
         compiler_params=params,
         cost_estimate=pl.CostEstimate(flops=1300000000, transcendentals=400000, bytes_accessed=6000000),
         name="block",
     )(
-        odd, own, near_rows, far_rows, near_cols, far_cols, mask.reshape(cells, channels), masked.reshape(cells, channels), taps,
+        odd, own, near_rows, far_rows, near_cols, far_cols, mask.reshape(cells, channels), masked.reshape(cells, channels), dw_kernel,
         dw_bias[None], ln_gain[None], ln_bias[None], w_in, b_in[None], w_out, b_out[None], layer_scale[None],
     )
     rows_sent = swap_rows(grad_depth, odd_lat)
-    small_rows = small.transpose(1, 0, 2).astype(BF16)
-    small_rows = jnp.pad(small_rows, ((0, 2 * far - 64), (0, 0), (0, 0)))[:, None]
-    chunks = jnp.concatenate([big.reshape(2 * far, 4, 2, LANES), small_rows], axis=1)
-    pair = lax.all_to_all(chunks.reshape(2, far * 10, LANES), "core", 0, 0)
+    pair = lax.all_to_all(chunks.reshape(2, plane, CHUNK_ROWS, LANES), "core", 0, 0)
     value = (pair[0].astype(F32) + pair[1].astype(F32)).astype(BF16)
-    value = lax.all_to_all(value.reshape(far, 5, 2, LANES), FAR, 0, 0)
+    value = lax.all_to_all(value, PLANE, 0, 0)
     value = jnp.sum(value.astype(F32), axis=0).astype(BF16)
     value, rows_sent = lax.optimization_barrier((value, rows_sent))
-    value = lax.all_to_all(jnp.broadcast_to(value[None], (far, 5, 2, LANES)), FAR, 0, 0)
+    value = lax.all_to_all(jnp.broadcast_to(value[None], (column,) + value.shape), COLUMN, 0, 0)
+    value = jnp.sum(value.astype(F32), axis=0).astype(BF16)
+    value = lax.all_to_all(jnp.broadcast_to(value[None], (plane,) + value.shape), PLANE, 0, 0)
     cols_sent = swap_cols(grad_depth, *rows_sent, odd_lat, odd_lon)
     grad_state = pl.pallas_call(
         state_kernel,
         out_shape=jax.ShapeDtypeStruct((rows, cols, channels), BF16),
         in_specs=[smem] + [vmem] * 7,
-        scratch_shapes=[pad, plane],
+        scratch_shapes=[pad, cells_scratch],
         compiler_params=params,
         cost_estimate=pl.CostEstimate(flops=10000000, transcendentals=0, bytes_accessed=3000000),
         name="state",
-    )(odd, grad_depth, *rows_sent, *cols_sent, cot, taps)
+    )(odd, grad_depth, *rows_sent, *cols_sent, cot, dw_kernel)
     value, grad_state = lax.optimization_barrier((value, grad_state))
     other = lax.ppermute(value, "core", [(0, 1), (1, 0)])
     total_cells = cells * lax.axis_size(LON) * lax.axis_size(LAT)
     factor = 1.0 / math.sqrt(total_cells)
-    grad_w_in, grad_w_out = pl.pallas_call(
+    grad_kernel, singles, grad_w_in, grad_b_in, grad_w_out = pl.pallas_call(
         functools.partial(unpack_kernel, factor),
         out_shape=(
+            jax.ShapeDtypeStruct(dw_kernel.shape, F32),
+            jax.ShapeDtypeStruct((5, 1, channels), F32),
             jax.ShapeDtypeStruct((channels, hidden), F32),
+            jax.ShapeDtypeStruct((1, hidden), F32),
             jax.ShapeDtypeStruct((hidden, channels), F32),
         ),
         in_specs=[smem, vmem, vmem],
+        scratch_shapes=[pltpu.VMEM((128, LANES), F32)],
         compiler_params=params,
         name="unpack",
-    )(
-        core.astype(jnp.int32).reshape(1),
-        value[:, :4].reshape(2 * hidden, LANES),
-        other[:, :4].reshape(2 * hidden, LANES),
-    )
-    small_sum = jnp.where(core == 0, value[:64, 4], other[:64, 4]).astype(F32) * factor
-    small_sum = small_sum.reshape(64, channels)
-    blocks = hidden // channels
-    singles = 49 + blocks
-    grad_kernel = small_sum[:49].reshape(7, 7, channels).transpose(1, 0, 2)
+    )(core.astype(jnp.int32).reshape(1), value, other)
     return (
         output[None],
         grad_state[None],
         grad_kernel,
-        small_sum[singles],
-        small_sum[singles + 1],
-        small_sum[singles + 2],
+        singles[0, 0],
+        singles[1, 0],
+        singles[2, 0],
         grad_w_in,
-        small_sum[49:singles].reshape(hidden),
+        grad_b_in[0],
         grad_w_out,
-        small_sum[singles + 3],
-        small_sum[singles + 4],
+        singles[3, 0],
+        singles[4, 0],
     )
 
 

time: 131 us -> 120 us (0.916)
  blocking collectives: 6.14 us -> 22.9 us
  starting transfers between devices: 71 us -> 59.3 us
  waiting for transfers between devices: 27.1 us -> 15.5 us
  local copies, waits for them, and re-layouts: 5.94 us -> 3.56 us
  other arithmetic: 6.5 us -> 4.16 us
    all_to_all x1 -> x2, blocking collectives: 6.14 us -> 22.9 us  [the longest x1 16.7 us: local(): lax.all_to_all(jnp.broadcast_to(value[None], (column,) + value.shape), CO...]
    all_to_all x2, starting transfers between devices: 36.6 us -> 22 us  [the longest x1 13.9 us: local(): value = lax.all_to_all(value, PLANE, 0, 0)]
    ppermute x2, waiting for transfers between devices: 7.44 us -> 0.01 us  [swap_cols(): far_cols = lax.ppermute(jnp.where(odd_lon, last, first), LON, far)]
    all_to_all x2, waiting for transfers between devices: 18.3 us -> 11.5 us  [the longest x1 9.41 us: local(): value = lax.all_to_all(value, PLANE, 0, 0)]
    ppermute x2, waiting for transfers between devices: 0.01 us -> 1.9 us  [swap_cols(): near_cols = lax.ppermute(jnp.where(odd_lon, first, last), LON, near)]
    concatenate x1 -> x0, other arithmetic: 1.76 us -> none  [local(): jnp.concatenate([big.reshape(2 * far, 4, 2, LANES), small_rows], axis=1)]
    ppermute x2, starting transfers between devices: 12.3 us -> 13.7 us  [swap_rows(): near_rows = lax.ppermute(jnp.where(odd, first, last), LAT, near)]
  transfers between devices with their start and end apart: 11 -> 11, of which waited for: 4 -> 6; matrix products, arithmetic and copies ran while one was open for 4% -> 2% of each run, Pallas kernels for 3% -> 3%
where the time goes in v4:
time: 120 us; the launch traced here: 119 us
  starting transfers between devices  59.3 us (49%)
  blocking collectives  22.9 us (19%)
  waiting for transfers between devices  15.5 us (13%)
  Pallas kernels  12.7 us (11%)
  other arithmetic  4.16 us (3%)
  local copies, waits for them, and re-layouts  3.56 us (3%)
    all_to_all x1, blocking collectives, local(): lax.all_to_all(jnp.broadcast_to(value[None], (column,) + value.shape), CO...  16.7 us
    all_to_all x1, starting transfers between devices, local(): value = lax.all_to_all(value, PLANE, 0, 0)  13.9 us
    ppermute x2, starting transfers between devices, swap_rows(): near_rows = lax.ppermute(jnp.where(odd, first, last), LAT, near)  13.7 us
    all_to_all x1, waiting for transfers between devices, local(): value = lax.all_to_all(value, PLANE, 0, 0)  9.41 us
    ppermute x2, starting transfers between devices, swap_cols(): far_cols = lax.ppermute(jnp.where(odd_lon, last, first), LON, far)  9.13 us
    all_to_all x1, starting transfers between devices, local(): lax.all_to_all(jnp.broadcast_to(value[None], (plane,) + value.shape), PLA...  8.18 us
    ppermute x1, starting transfers between devices, local(): other = lax.ppermute(value, 'core', [(0, 1), (1, 0)])  7.91 us
    pallas_call x1, Pallas kernels, local(): pl.pallas_call(block_kernel, out_shape=(jax.ShapeDtypeStruct((rows, cols,...  7.76 us
  transfers between devices with their start and end apart: 11, of which 6 were waited for; matrix products, arithmetic and copies ran while one was open for 2% of the time, Pallas kernels for 3%

profile of v4, /device:TPU:1, one launch (start us, length us, event | category | flops | bytes accessed | tf_op | source)
XLA Modules:
  0.0 119.0 jit_solution(18353288399094886746)
XLA Ops:
  0.7 1.1 select_bitcast_fusion
  1.8 0.7 collective-permute-start.1
  2.5 8.2 %collective-permute-start = (bf16[3,64,256]{2,1,0:T(8,128)(2,1)S(1)}, bf16[3,64,256]{2,1,0:T(8,128)(2,1)S(1)}, u32[]{:S(2)}, u32[]{:S(2)}) collective-permute-start(bf16[3,64,256]{2,1,0:T(8,128)(2,1)S(1)} %get-tuple-element.52), channel_id=1, source_target_pairs={{0,1},{1,0},{2,3},{3,2},{4,5},{5,4},{6,7},{7,6},{8,9},{9,8},{10,11... | collective-permute-start | bytes 294920 | tf_op jit(solution)/shard_map/ppermute | solution.py:243
  10.7 0.7 convert_reduce_fusion
  11.5 1.0 bitcast_multiply_fusion.masked_ref
  12.5 0.8 fusion.2
  13.4 4.3 %collective-permute-start.3 = (bf16[12,3,256]{2,1,0:T(4,128)(2,1)S(1)}, bf16[12,3,256]{2,1,0:T(4,128)(2,1)S(1)}, u32[]{:S(2)}, u32[]{:S(2)}) collective-permute-start(bf16[12,3,256]{2,1,0:T(4,128)(2,1)S(1)} %get-tuple-element.55), channel_id=1, source_target_pairs={{64,128},{128,64},{192,256},{256,192},{320,384},{384,320},{448,0},... | collective-permute-start | bytes 55304 | tf_op jit(solution)/shard_map/ppermute | solution.py:258
  17.7 3.2 %collective-permute-start.2 = (bf16[12,3,256]{2,1,0:T(4,128)(2,1)S(1)}, bf16[12,3,256]{2,1,0:T(4,128)(2,1)S(1)}, u32[]{:S(2)}, u32[]{:S(2)}) collective-permute-start(bf16[12,3,256]{2,1,0:T(4,128)(2,1)S(1)} %get-tuple-element.56), channel_id=1, source_target_pairs={{0,64},{64,0},{128,192},{192,128},{256,320},{320,256},{384,448},{4... | collective-permute-start | bytes 55304 | tf_op jit(solution)/shard_map/ppermute | solution.py:259
  21.0 0.7 collective-permute-done.2.near_cols_ref
  21.8 0.1 broadcast_in_dim.42.mask_ref
  22.0 1.0 copy-done.4
  23.0 7.8 %block.1 = (bf16[6,64,256]{2,1,0:T(8,128)(2,1)}, bf16[6,64,256]{2,1,0:T(8,128)(2,1)S(1)}, bf16[64,72,128]{2,1,0:T(8,128)(2,1)S(1)}) custom-call(s32[2]{0:T(128)S(1)} %pad_add_fusion.odd_ref, bf16[6,64,256]{2,1,0:T(8,128)(2,1)S(1)} %bitcast.30, bf16[3,64,256]{2,1,0:T(8,128)(2,1)S(1)} %collective-permute-done.near_rows_ref, ...), custom_call_target="tpu_custom_call" | custom-call | flops 1300000000 | bytes 6000000 | tf_op jit(solution)/shard_map/block/pallas_call | solution.py:284
  30.8 6.2 %all_to_all.20 = bf16[2,32,72,128]{3,2,1,0:T(8,128)(2,1)S(1)} all-to-all(bf16[2,32,72,128]{3,2,1,0:T(8,128)(2,1)S(1)} %bitcast.27), channel_id=1, replica_groups=mesh['y_lo'=4,'core'=2,'x'=4,'y_hi'=2,'z'=8] {'core'}, dimensions={0} | all-to-all | bytes 2359296 | tf_op jit(solution)/shard_map/all_to_all | solution.py:306
  37.0 1.0 fusion
  37.9 13.9 %all-to-all-start.1 = ((bf16[32,72,128]{2,1,0:T(8,128)(2,1)}), bf16[32,72,128]{2,1,0:T(8,128)(2,1)S(1)}, u32[]{:S(2)}, u32[]{:S(2)}) async-start(bf16[32,72,128]{2,1,0:T(8,128)(2,1)} %fusion), calls=%async_computation.1 | async-start | bytes 1179648 | tf_op jit(solution)/shard_map/all_to_all | solution.py:308
  51.8 0.7 collective-permute-start.5
  52.5 5.6 %collective-permute-start.4 = (bf16[3,64,256]{2,1,0:T(8,128)(2,1)S(1)}, bf16[3,64,256]{2,1,0:T(8,128)(2,1)S(1)}, u32[]{:S(2)}, u32[]{:S(2)}) collective-permute-start(bf16[3,64,256]{2,1,0:T(8,128)(2,1)S(1)} %get-tuple-element.44), channel_id=1, source_target_pairs={{0,1},{1,0},{2,3},{3,2},{4,5},{5,4},{6,7},{7,6},{8,9},{9,8},{10,11... | collective-permute-start | bytes 294920 | tf_op jit(solution)/shard_map/ppermute | solution.py:243
  58.1 9.4 %all-to-all-done.1 = bf16[32,72,128]{2,1,0:T(8,128)(2,1)S(1)} async-done(((bf16[32,72,128]{2,1,0:T(8,128)(2,1)}), bf16[32,72,128]{2,1,0:T(8,128)(2,1)S(1)}, u32[]{:S(2)}, u32[]{:S(2)}) %all-to-all-start.1) | async-done | bytes 589856 | tf_op jit(solution)/shard_map/all_to_all | solution.py:308
  67.5 0.1 reduce_sum.24
  67.6 0.5 collective-permute-done.4.near_rows_ref
  68.1 16.7 %all_to_all.21 = bf16[8,72,128]{2,1,0:T(8,128)(2,1)S(1)} all-to-all(bf16[8,72,128]{2,1,0:T(8,128)(2,1)S(1)} %broadcast_in_dim.50), channel_id=1, replica_groups=mesh['y_lo'=4,'core'=2,'x'=4,'y_hi'=2,'z'=8] {'y_hi','y_lo'}, dimensions={0} | all-to-all | bytes 294912 | tf_op jit(solution)/shard_map/all_to_all | solution.py:311
  84.9 0.9 broadcast_in_dim.51
  85.8 8.2 %all-to-all-start.3 = ((bf16[32,72,128]{2,1,0:T(8,128)(2,1)}), bf16[32,72,128]{2,1,0:T(8,128)(2,1)S(1)}, u32[]{:S(2)}, u32[]{:S(2)}) async-start(bf16[32,72,128]{2,1,0:T(8,128)(2,1)} %broadcast_in_dim.51), calls=%async_computation.3 | async-start | bytes 1179648 | tf_op jit(solution)/shard_map/all_to_all | solution.py:313
  94.1 4.8 %collective-permute-start.7 = (bf16[12,3,256]{2,1,0:T(4,128)(2,1)S(1)}, bf16[12,3,256]{2,1,0:T(4,128)(2,1)S(1)}, u32[]{:S(2)}, u32[]{:S(2)}) collective-permute-start(bf16[12,3,256]{2,1,0:T(4,128)(2,1)S(1)} %get-tuple-element.53), channel_id=1, source_target_pairs={{64,128},{128,64},{192,256},{256,192},{320,384},{384,320},{448,0},... | collective-permute-start | bytes 55304 | tf_op jit(solution)/shard_map/ppermute | solution.py:258
  98.9 1.9 %collective-permute-start.6 = (bf16[12,3,256]{2,1,0:T(4,128)(2,1)S(1)}, bf16[12,3,256]{2,1,0:T(4,128)(2,1)S(1)}, u32[]{:S(2)}, u32[]{:S(2)}) collective-permute-start(bf16[12,3,256]{2,1,0:T(4,128)(2,1)S(1)} %get-tuple-element.54), channel_id=1, source_target_pairs={{0,64},{64,0},{128,192},{192,128},{256,320},{320,256},{384,448},{4... | collective-permute-start | bytes 55304 | tf_op jit(solution)/shard_map/ppermute | solution.py:259
  100.8 1.2 collective-permute-done.6.near_cols_ref
  102.0 3.3 %state.1 = bf16[6,64,256]{2,1,0:T(8,128)(2,1)} custom-call(s32[2]{0:T(128)S(1)} %pad_add_fusion.odd_ref, bf16[6,64,256]{2,1,0:T(8,128)(2,1)S(1)} %get-tuple-element.26.own_ref, bf16[3,64,256]{2,1,0:T(8,128)(2,1)S(1)} %collective-permute-done.4.near_rows_ref, bf16[3,64,256]{2,1,0:T(8,128)(2,1)S(1)} %collective-permute-done.5.far_rows_ref, ...), custom_call_target="tpu_custom_call" | custom-call | flops 10000000 | bytes 3000000 | tf_op jit(solution)/shard_map/state/pallas_call | solution.py:315
  105.3 2.0 %all-to-all-done.3.mine_ref = bf16[32,72,128]{2,1,0:T(8,128)(2,1)S(1)} async-done(((bf16[32,72,128]{2,1,0:T(8,128)(2,1)}), bf16[32,72,128]{2,1,0:T(8,128)(2,1)S(1)}, u32[]{:S(2)}, u32[]{:S(2)}) %all-to-all-start.3) | async-done | bytes 589856 | tf_op jit(solution)/shard_map/all_to_all | solution.py:313
  107.4 7.9 %collective-permute-start.8 = (bf16[32,72,128]{2,1,0:T(8,128)(2,1)S(1)}, bf16[32,72,128]{2,1,0:T(8,128)(2,1)S(1)}, u32[]{:S(2)}, u32[]{:S(2)}) collective-permute-start(bf16[32,72,128]{2,1,0:T(8,128)(2,1)S(1)} %all-to-all-done.3.mine_ref), channel_id=1, source_target_pairs={{0,64},{64,0},{1,65},{65,1},{2,66},{66,2},{3,67},{67,3},{4,68},{68... | collective-permute-start | bytes 1769480 | tf_op jit(solution)/shard_map/ppermute | solution.py:325
  115.3 1.6 %collective-permute-done.8.other_ref = bf16[32,72,128]{2,1,0:T(8,128)(2,1)S(1)} collective-permute-done((bf16[32,72,128]{2,1,0:T(8,128)(2,1)S(1)}, bf16[32,72,128]{2,1,0:T(8,128)(2,1)S(1)}, u32[]{:S(2)}, u32[]{:S(2)}) %collective-permute-start.8) | collective-permute-done | bytes 589856 | tf_op jit(solution)/shard_map/ppermute | solution.py:325
  116.9 1.6 %unpack.1 = (f32[7,7,256]{2,1,0:T(8,128)}, f32[5,1,256]{2,1,0:T(1,128)S(1)}, f32[256,1024]{1,0:T(8,128)}, f32[1,1024]{1,0:T(1,128)}, f32[1024,256]{1,0:T(8,128)}) custom-call(s32[1]{0:T(128)} %bitcast.1.core_ref, bf16[32,72,128]{2,1,0:T(8,128)(2,1)S(1)} %all-to-all-done.3.mine_ref, bf16[32,72,128]{2,1,0:T(8,128)(2,1)S(1)} %collective-permute-done.8.other_ref), custom_call_target="tpu_custom_call" | custom-call | tf_op jit(solution)/shard_map/unpack/pallas_call | solution.py:328
  118.4 0.6 fusion.3
  (36 shorter events, 0.4 us)
Async XLA Ops:
  0.6 21.3 %copy-start.1 = (bf16[1,6,64,256]{3,2,1,0:T(8,128)(2,1)S(1)}, bf16[1,6,64,256]{3,2,1,0:T(8,128)(2,1)}, u32[]{:S(2)}) copy-start(bf16[1,6,64,256]{3,2,1,0:T(8,128)(2,1)} %param.12) | copy-start | bytes 589828
  0.7 21.3 %copy-start.2 = (f32[7,7,256]{2,1,0:T(8,128)S(1)}, f32[7,7,256]{2,1,0:T(8,128)}, u32[]{:S(2)}) copy-start(f32[7,7,256]{2,1,0:T(8,128)} %k_ref.3) | copy-start | bytes 150532
  0.7 21.3 %copy-start.10 = (f32[256]{0:T(256)S(1)}, f32[256]{0:T(256)}, u32[]{:S(2)}) copy-start(f32[256]{0:T(256)} %param.23) | copy-start | bytes 3076
  0.7 21.3 %copy-start.9 = (f32[256]{0:T(256)S(1)}, f32[256]{0:T(256)}, u32[]{:S(2)}) copy-start(f32[256]{0:T(256)} %param.22) | copy-start | bytes 3076
  0.7 21.3 %copy-start.5 = (f32[1024]{0:T(1024)S(1)}, f32[1024]{0:T(1024)}, u32[]{:S(2)}) copy-start(f32[1024]{0:T(1024)} %param.20) | copy-start | bytes 12292
  0.7 21.3 %copy-start.3 = (bf16[256,1024]{1,0:T(8,128)(2,1)S(1)}, bf16[256,1024]{1,0:T(8,128)(2,1)}, u32[]{:S(2)}) copy-start(bf16[256,1024]{1,0:T(8,128)(2,1)} %w_in_ref.1) | copy-start | bytes 1572868
  0.7 21.3 %copy-start.8 = (f32[256]{0:T(256)S(1)}, f32[256]{0:T(256)}, u32[]{:S(2)}) copy-start(f32[256]{0:T(256)} %param.18) | copy-start | bytes 3076
  0.7 21.3 %copy-start.7 = (f32[256]{0:T(256)S(1)}, f32[256]{0:T(256)}, u32[]{:S(2)}) copy-start(f32[256]{0:T(256)} %param.17) | copy-start | bytes 3076
  0.7 21.3 %copy-start.6 = (f32[256]{0:T(256)S(1)}, f32[256]{0:T(256)}, u32[]{:S(2)}) copy-start(f32[256]{0:T(256)} %param.16) | copy-start | bytes 3076
  1.8 11.5 %collective-permute-start.1 = (bf16[3,64,256]{2,1,0:T(8,128)(2,1)S(1)}, bf16[3,64,256]{2,1,0:T(8,128)(2,1)S(1)}, u32[]{:S(2)}, u32[]{:S(2)}) collective-permute-start(bf16[3,64,256]{2,1,0:T(8,128)(2,1)S(1)} %get-tuple-element.51), channel_id=1, source_target_pairs={{1,2},{2,1},{3,4},{4,3},{5,6},{6,5},{7,8},{8,7},{9,10},{10,9},{11,... | collective-permute-start | bytes 294920 | tf_op jit(solution)/shard_map/ppermute | solution.py:242
  2.5 10.8 %collective-permute-start = (bf16[3,64,256]{2,1,0:T(8,128)(2,1)S(1)}, bf16[3,64,256]{2,1,0:T(8,128)(2,1)S(1)}, u32[]{:S(2)}, u32[]{:S(2)}) collective-permute-start(bf16[3,64,256]{2,1,0:T(8,128)(2,1)S(1)} %get-tuple-element.52), channel_id=1, source_target_pairs={{0,1},{1,0},{2,3},{3,2},{4,5},{5,4},{6,7},{7,6},{8,9},{9,8},{10,11... | collective-permute-start | bytes 294920 | tf_op jit(solution)/shard_map/ppermute | solution.py:243
  13.4 7.6 %collective-permute-start.3 = (bf16[12,3,256]{2,1,0:T(4,128)(2,1)S(1)}, bf16[12,3,256]{2,1,0:T(4,128)(2,1)S(1)}, u32[]{:S(2)}, u32[]{:S(2)}) collective-permute-start(bf16[12,3,256]{2,1,0:T(4,128)(2,1)S(1)} %get-tuple-element.55), channel_id=1, source_target_pairs={{64,128},{128,64},{192,256},{256,192},{320,384},{384,320},{448,0},... | collective-permute-start | bytes 55304 | tf_op jit(solution)/shard_map/ppermute | solution.py:258
  17.7 4.0 %collective-permute-start.2 = (bf16[12,3,256]{2,1,0:T(4,128)(2,1)S(1)}, bf16[12,3,256]{2,1,0:T(4,128)(2,1)S(1)}, u32[]{:S(2)}, u32[]{:S(2)}) collective-permute-start(bf16[12,3,256]{2,1,0:T(4,128)(2,1)S(1)} %get-tuple-element.56), channel_id=1, source_target_pairs={{0,64},{64,0},{128,192},{192,128},{256,320},{320,256},{384,448},{4... | collective-permute-start | bytes 55304 | tf_op jit(solution)/shard_map/ppermute | solution.py:259
  22.0 1.0 copy-start.4
  37.9 29.6 %all-to-all-start.1 = ((bf16[32,72,128]{2,1,0:T(8,128)(2,1)}), bf16[32,72,128]{2,1,0:T(8,128)(2,1)S(1)}, u32[]{:S(2)}, u32[]{:S(2)}) async-start(bf16[32,72,128]{2,1,0:T(8,128)(2,1)} %fusion), calls=%async_computation.1 | async-start | bytes 1179648 | tf_op jit(solution)/shard_map/all_to_all | solution.py:308
  51.8 15.8 %collective-permute-start.5 = (bf16[3,64,256]{2,1,0:T(8,128)(2,1)S(1)}, bf16[3,64,256]{2,1,0:T(8,128)(2,1)S(1)}, u32[]{:S(2)}, u32[]{:S(2)}) collective-permute-start(bf16[3,64,256]{2,1,0:T(8,128)(2,1)S(1)} %get-tuple-element.43), channel_id=1, source_target_pairs={{1,2},{2,1},{3,4},{4,3},{5,6},{6,5},{7,8},{8,7},{9,10},{10,9},{11,... | collective-permute-start | bytes 294920 | tf_op jit(solution)/shard_map/ppermute | solution.py:242
  52.5 15.6 %collective-permute-start.4 = (bf16[3,64,256]{2,1,0:T(8,128)(2,1)S(1)}, bf16[3,64,256]{2,1,0:T(8,128)(2,1)S(1)}, u32[]{:S(2)}, u32[]{:S(2)}) collective-permute-start(bf16[3,64,256]{2,1,0:T(8,128)(2,1)S(1)} %get-tuple-element.44), channel_id=1, source_target_pairs={{0,1},{1,0},{2,3},{3,2},{4,5},{5,4},{6,7},{7,6},{8,9},{9,8},{10,11... | collective-permute-start | bytes 294920 | tf_op jit(solution)/shard_map/ppermute | solution.py:243
  68.1 33.9 %copy-start = (bf16[1,6,64,256]{3,2,1,0:T(8,128)(2,1)S(1)}, bf16[1,6,64,256]{3,2,1,0:T(8,128)(2,1)}, u32[]{:S(2)}) copy-start(bf16[1,6,64,256]{3,2,1,0:T(8,128)(2,1)} %param.14) | copy-start | bytes 589828
  85.8 21.6 %all-to-all-start.3 = ((bf16[32,72,128]{2,1,0:T(8,128)(2,1)}), bf16[32,72,128]{2,1,0:T(8,128)(2,1)S(1)}, u32[]{:S(2)}, u32[]{:S(2)}) async-start(bf16[32,72,128]{2,1,0:T(8,128)(2,1)} %broadcast_in_dim.51), calls=%async_computation.3 | async-start | bytes 1179648 | tf_op jit(solution)/shard_map/all_to_all | solution.py:313
  94.1 6.7 %collective-permute-start.7 = (bf16[12,3,256]{2,1,0:T(4,128)(2,1)S(1)}, bf16[12,3,256]{2,1,0:T(4,128)(2,1)S(1)}, u32[]{:S(2)}, u32[]{:S(2)}) collective-permute-start(bf16[12,3,256]{2,1,0:T(4,128)(2,1)S(1)} %get-tuple-element.53), channel_id=1, source_target_pairs={{64,128},{128,64},{192,256},{256,192},{320,384},{384,320},{448,0},... | collective-permute-start | bytes 55304 | tf_op jit(solution)/shard_map/ppermute | solution.py:258
  98.9 3.1 %collective-permute-start.6 = (bf16[12,3,256]{2,1,0:T(4,128)(2,1)S(1)}, bf16[12,3,256]{2,1,0:T(4,128)(2,1)S(1)}, u32[]{:S(2)}, u32[]{:S(2)}) collective-permute-start(bf16[12,3,256]{2,1,0:T(4,128)(2,1)S(1)} %get-tuple-element.54), channel_id=1, source_target_pairs={{0,64},{64,0},{128,192},{192,128},{256,320},{320,256},{384,448},{4... | collective-permute-start | bytes 55304 | tf_op jit(solution)/shard_map/ppermute | solution.py:259
  107.4 9.5 %collective-permute-start.8 = (bf16[32,72,128]{2,1,0:T(8,128)(2,1)S(1)}, bf16[32,72,128]{2,1,0:T(8,128)(2,1)S(1)}, u32[]{:S(2)}, u32[]{:S(2)}) collective-permute-start(bf16[32,72,128]{2,1,0:T(8,128)(2,1)S(1)} %all-to-all-done.3.mine_ref), channel_id=1, source_target_pairs={{0,64},{64,0},{1,65},{65,1},{2,66},{66,2},{3,67},{67,3},{4,68},{68... | collective-permute-start | bytes 1769480 | tf_op jit(solution)/shard_map/ppermute | solution.py:325

commit v5 on v4

--- a/solution.py
+++ b/solution.py
@@ -3,6 +3,7 @@
 
 import jax
 import jax.numpy as jnp
+import numpy as np
 from jax import lax
 from jax.experimental import pallas as pl
 from jax.experimental.pallas import tpu as pltpu
@@ -10,12 +11,12 @@
 
 LON = ("y_lo", "core")
 LAT = ("x", "y_hi", "z")
-PLANE = ("x", "z")
-COLUMN = ("y_hi", "y_lo")
+SIZES = {"y_lo": 4, "core": 2, "x": 4, "y_hi": 2, "z": 8}
+EVERY = tuple(SIZES)
 BIG_ROWS = 64
 CHUNK_ROWS = 72
 LANES = 128
-VMEM_BYTES = 44 << 20
+VMEM_BYTES = 32 << 20
 F32 = jnp.float32
 BF16 = jnp.bfloat16
 
@@ -188,7 +189,8 @@
 
 
 def unpack_kernel(
-    factor, core_ref, mine_ref, other_ref, k_ref, singles_ref, w_in_ref, b_in_ref, w_out_ref, small_ref
+    factor, core_ref, mine_ref, other_ref, k_ref, one_ref, two_ref, three_ref, w_in_ref, b_in_ref, w_out_ref, four_ref,
+    five_ref, small_ref,
 ):
     channels, hidden = w_in_ref.shape
 
@@ -222,8 +224,28 @@
         for n in range(blocks):
             part = slice(n * channels + t * LANES, n * channels + (t + 1) * LANES)
             b_in_ref[:, part] = small_ref[at + n : at + n + 1, :]
-        for n in range(5):
-            singles_ref[n, :, ln] = small_ref[at + blocks + n : at + blocks + n + 1, :]
+        for n, ref in enumerate((one_ref, two_ref, three_ref, four_ref, five_ref)):
+            ref[:, ln] = small_ref[at + blocks + n : at + blocks + n + 1, :]
+
+
+def groups_along(first_core, second_core):
+    index = np.arange(math.prod(SIZES.values())).reshape(tuple(SIZES.values()))
+    groups = []
+    for core, axes in enumerate((first_core, second_core)):
+        mine = index.take(core, axis=EVERY.index("core"))
+        names = [name for name in EVERY if name != "core"]
+        order = [name for name in names if name not in axes] + list(axes)
+        size = math.prod(SIZES[name] for name in axes)
+        groups += mine.transpose([names.index(name) for name in order]).reshape(-1, size).tolist()
+    return groups
+
+
+PLANE = groups_along(("x", "z"), ("x", "y_hi", "y_lo"))
+COLUMN = groups_along(("y_hi", "y_lo"), ("z",))
+
+
+def exchange(value, groups):
+    return lax.all_to_all(value, EVERY, 0, 0, axis_index_groups=groups)
 
 
 def swaps(axis, wrap):
@@ -266,7 +288,7 @@
     _, rows, cols, channels = ocean_state.shape
     cells = rows * cols
     hidden = w_in.shape[1]
-    plane, column = lax.axis_size(PLANE), lax.axis_size(COLUMN)
+    plane, column = len(PLANE[0]), len(COLUMN[0])
     core = lax.axis_index("core")
     own = ocean_state[0]
     cot = cotangent[0]
@@ -305,12 +327,12 @@
     rows_sent = swap_rows(grad_depth, odd_lat)
     pair = lax.all_to_all(chunks.reshape(2, plane, CHUNK_ROWS, LANES), "core", 0, 0)
     value = (pair[0].astype(F32) + pair[1].astype(F32)).astype(BF16)
-    value = lax.all_to_all(value, PLANE, 0, 0)
+    value = exchange(value, PLANE)
     value = jnp.sum(value.astype(F32), axis=0).astype(BF16)
     value, rows_sent = lax.optimization_barrier((value, rows_sent))
-    value = lax.all_to_all(jnp.broadcast_to(value[None], (column,) + value.shape), COLUMN, 0, 0)
+    value = exchange(jnp.broadcast_to(value[None], (column,) + value.shape), COLUMN)
     value = jnp.sum(value.astype(F32), axis=0).astype(BF16)
-    value = lax.all_to_all(jnp.broadcast_to(value[None], (plane,) + value.shape), PLANE, 0, 0)
+    value = exchange(jnp.broadcast_to(value[None], (plane,) + value.shape), PLANE)
     cols_sent = swap_cols(grad_depth, *rows_sent, odd_lat, odd_lon)
     grad_state = pl.pallas_call(
         state_kernel,
@@ -325,37 +347,31 @@
     other = lax.ppermute(value, "core", [(0, 1), (1, 0)])
     total_cells = cells * lax.axis_size(LON) * lax.axis_size(LAT)
     factor = 1.0 / math.sqrt(total_cells)
-    grad_kernel, singles, grad_w_in, grad_b_in, grad_w_out = pl.pallas_call(
+    single = jax.ShapeDtypeStruct((1, channels), F32)
+    sums = pl.pallas_call(
         functools.partial(unpack_kernel, factor),
         out_shape=(
             jax.ShapeDtypeStruct(dw_kernel.shape, F32),
-            jax.ShapeDtypeStruct((5, 1, channels), F32),
+            single,
+            single,
+            single,
             jax.ShapeDtypeStruct((channels, hidden), F32),
             jax.ShapeDtypeStruct((1, hidden), F32),
             jax.ShapeDtypeStruct((hidden, channels), F32),
+            single,
+            single,
         ),
         in_specs=[smem, vmem, vmem],
         scratch_shapes=[pltpu.VMEM((128, LANES), F32)],
         compiler_params=params,
         name="unpack",
     )(core.astype(jnp.int32).reshape(1), value, other)
-    return (
-        output[None],
-        grad_state[None],
-        grad_kernel,
-        singles[0, 0],
-        singles[1, 0],
-        singles[2, 0],
-        grad_w_in,
-        grad_b_in[0],
-        grad_w_out,
-        singles[3, 0],
-        singles[4, 0],
-    )
+    sums = [part[0] if part.shape[0] == 1 else part for part in sums]
+    return (output[None], grad_state[None], *sums)
 
 
 def solution(mesh):
-    mesh = Mesh(mesh.devices.reshape(4, 2, 4, 2, 8), ("y_lo", "core", "x", "y_hi", "z"))
+    mesh = Mesh(mesh.devices.reshape(tuple(SIZES.values())), EVERY)
     field = P(None, LAT, LON, None)
     in_specs = (field, P(None, LAT, LON), field) + (P(),) * 9
     out_specs = (field, field) + (P(),) * 9

time: 120 us -> 113 us (0.942)
  starting transfers between devices: 59.3 us -> 54.7 us
  waiting for transfers between devices: 15.5 us -> 14 us
    ppermute x1, starting transfers between devices: 7.91 us -> 4.24 us  [local(): other = lax.ppermute(value, 'core', [(0, 1), (1, 0)])]
    ppermute x2, starting transfers between devices: 13.7 us -> 11.1 us  [swap_rows(): near_rows = lax.ppermute(jnp.where(odd, first, last), LAT, near)]
    ppermute x2, starting transfers between devices: 5.13 us -> 6.89 us  [swap_cols(): near_cols = lax.ppermute(jnp.where(odd_lon, first, last), LON, near)]
    ppermute x2, starting transfers between devices: 9.13 us -> 7.89 us  [swap_cols(): far_cols = lax.ppermute(jnp.where(odd_lon, last, first), LON, far)]
  transfers between devices with their start and end apart: 11 -> 11, of which waited for: 6 -> 5; matrix products, arithmetic and copies ran while one was open for 2% -> 3% of each run, Pallas kernels for 3% -> 3%
where the time goes in v5:
time: 113 us; the launch traced here: 112 us
  starting transfers between devices  54.7 us (48%)
  blocking collectives  22.3 us (20%)
  waiting for transfers between devices  14 us (12%)
  Pallas kernels  12.7 us (11%)
  other arithmetic  4.16 us (4%)
  local copies, waits for them, and re-layouts  2.98 us (3%)
    all_to_all x2, starting transfers between devices, exchange(): return lax.all_to_all(value, EVERY, 0, 0, axis_index_groups=groups)  23.2 us
    all_to_all x1, blocking collectives, exchange(): return lax.all_to_all(value, EVERY, 0, 0, axis_index_groups=groups)  16.1 us
    ppermute x2, starting transfers between devices, swap_rows(): near_rows = lax.ppermute(jnp.where(odd, first, last), LAT, near)  11.1 us
    all_to_all x2, waiting for transfers between devices, exchange(): return lax.all_to_all(value, EVERY, 0, 0, axis_index_groups=groups)  10.8 us
    ppermute x2, starting transfers between devices, swap_cols(): far_cols = lax.ppermute(jnp.where(odd_lon, last, first), LON, far)  7.89 us
    pallas_call x1, Pallas kernels, local(): pl.pallas_call(block_kernel, out_shape=(jax.ShapeDtypeStruct((rows, cols,...  7.76 us
    ppermute x2, starting transfers between devices, swap_cols(): near_cols = lax.ppermute(jnp.where(odd_lon, first, last), LON, near)  6.89 us
    all_to_all x1, blocking collectives, local(): lax.all_to_all(chunks.reshape(2, plane, CHUNK_ROWS, LANES), 'core', 0, 0)  6.16 us
  transfers between devices with their start and end apart: 11, of which 5 were waited for; matrix products, arithmetic and copies ran while one was open for 3% of the time, Pallas kernels for 3%

profile of v5, /device:TPU:1, one launch (start us, length us, event | category | flops | bytes accessed | tf_op | source)
XLA Modules:
  0.0 111.8 jit_solution(2466521535014846850)
XLA Ops:
  0.7 1.1 select_bitcast_fusion
  1.8 0.7 collective-permute-start.1
  2.5 8.2 %collective-permute-start = (bf16[3,64,256]{2,1,0:T(8,128)(2,1)S(1)}, bf16[3,64,256]{2,1,0:T(8,128)(2,1)S(1)}, u32[]{:S(2)}, u32[]{:S(2)}) collective-permute-start(bf16[3,64,256]{2,1,0:T(8,128)(2,1)S(1)} %get-tuple-element.60), channel_id=1, source_target_pairs={{0,1},{1,0},{2,3},{3,2},{4,5},{5,4},{6,7},{7,6},{8,9},{9,8},{10,11... | collective-permute-start | bytes 294920 | tf_op jit(solution)/shard_map/ppermute | solution.py:265
  10.7 0.7 convert_reduce_fusion
  11.4 0.1 convert_element_type.29
  11.5 1.0 bitcast_multiply_fusion.masked_ref
  12.5 0.8 fusion.2
  13.4 4.3 %collective-permute-start.3 = (bf16[12,3,256]{2,1,0:T(4,128)(2,1)S(1)}, bf16[12,3,256]{2,1,0:T(4,128)(2,1)S(1)}, u32[]{:S(2)}, u32[]{:S(2)}) collective-permute-start(bf16[12,3,256]{2,1,0:T(4,128)(2,1)S(1)} %get-tuple-element.63), channel_id=1, source_target_pairs={{64,128},{128,64},{192,256},{256,192},{320,384},{384,320},{448,0},... | collective-permute-start | bytes 55304 | tf_op jit(solution)/shard_map/ppermute | solution.py:280
  17.7 3.2 %collective-permute-start.2 = (bf16[12,3,256]{2,1,0:T(4,128)(2,1)S(1)}, bf16[12,3,256]{2,1,0:T(4,128)(2,1)S(1)}, u32[]{:S(2)}, u32[]{:S(2)}) collective-permute-start(bf16[12,3,256]{2,1,0:T(4,128)(2,1)S(1)} %get-tuple-element.64), channel_id=1, source_target_pairs={{0,64},{64,0},{128,192},{192,128},{256,320},{320,256},{384,448},{4... | collective-permute-start | bytes 55304 | tf_op jit(solution)/shard_map/ppermute | solution.py:281
  21.0 0.1 pad_add_fusion.odd_ref
  21.0 0.7 collective-permute-done.2.near_cols_ref
  21.8 0.1 broadcast_in_dim.42.mask_ref
  22.0 1.0 copy-done.4
  23.0 7.8 %block.1 = (bf16[6,64,256]{2,1,0:T(8,128)(2,1)}, bf16[6,64,256]{2,1,0:T(8,128)(2,1)S(1)}, bf16[64,72,128]{2,1,0:T(8,128)(2,1)S(1)}) custom-call(s32[2]{0:T(128)S(1)} %pad_add_fusion.odd_ref, bf16[6,64,256]{2,1,0:T(8,128)(2,1)S(1)} %bitcast.30, bf16[3,64,256]{2,1,0:T(8,128)(2,1)S(1)} %collective-permute-done.near_rows_ref, ...), custom_call_target="tpu_custom_call" | custom-call | flops 1300000000 | bytes 6000000 | tf_op jit(solution)/shard_map/block/pallas_call | solution.py:306
  30.8 6.2 %all_to_all.20 = bf16[2,32,72,128]{3,2,1,0:T(8,128)(2,1)S(1)} all-to-all(bf16[2,32,72,128]{3,2,1,0:T(8,128)(2,1)S(1)} %bitcast.27), channel_id=1, replica_groups=mesh['y_lo'=4,'core'=2,'x'=4,'y_hi'=2,'z'=8] {'core'}, dimensions={0} | all-to-all | bytes 2359296 | tf_op jit(solution)/shard_map/all_to_all | solution.py:328
  37.0 1.0 fusion
  37.9 14.9 %all-to-all-start.1 = ((bf16[32,72,128]{2,1,0:T(8,128)(2,1)}), bf16[32,72,128]{2,1,0:T(8,128)(2,1)S(1)}, u32[]{:S(2)}, u32[]{:S(2)}) async-start(bf16[32,72,128]{2,1,0:T(8,128)(2,1)} %fusion), calls=%async_computation.1 | async-start | bytes 1179648 | tf_op jit(solution)/shard_map/all_to_all | solution.py:248
  52.9 0.7 collective-permute-start.5
  53.6 3.0 %collective-permute-start.4 = (bf16[3,64,256]{2,1,0:T(8,128)(2,1)S(1)}, bf16[3,64,256]{2,1,0:T(8,128)(2,1)S(1)}, u32[]{:S(2)}, u32[]{:S(2)}) collective-permute-start(bf16[3,64,256]{2,1,0:T(8,128)(2,1)S(1)} %get-tuple-element.52), channel_id=1, source_target_pairs={{0,1},{1,0},{2,3},{3,2},{4,5},{5,4},{6,7},{7,6},{8,9},{9,8},{10,11... | collective-permute-start | bytes 294920 | tf_op jit(solution)/shard_map/ppermute | solution.py:265
  56.6 9.3 %all-to-all-done.1 = bf16[32,72,128]{2,1,0:T(8,128)(2,1)S(1)} async-done(((bf16[32,72,128]{2,1,0:T(8,128)(2,1)}), bf16[32,72,128]{2,1,0:T(8,128)(2,1)S(1)}, u32[]{:S(2)}, u32[]{:S(2)}) %all-to-all-start.1) | async-done | bytes 589856 | tf_op jit(solution)/shard_map/all_to_all | solution.py:248
  65.9 0.1 reduce_sum.24
  66.1 16.1 %all_to_all.21 = bf16[8,72,128]{2,1,0:T(8,128)(2,1)S(1)} all-to-all(bf16[8,72,128]{2,1,0:T(8,128)(2,1)S(1)} %broadcast_in_dim.50), channel_id=1, replica_groups={{0,128,256,384,8,136,264,392},{1,129,257,385,9,137,265,393},{2,130,258,..., dimensions={0} | all-to-all | bytes 294912 | tf_op jit(solution)/shard_map/all_to_all | solution.py:248
  82.2 0.9 broadcast_in_dim.51
  83.1 8.3 %all-to-all-start.3 = ((bf16[32,72,128]{2,1,0:T(8,128)(2,1)}), bf16[32,72,128]{2,1,0:T(8,128)(2,1)S(1)}, u32[]{:S(2)}, u32[]{:S(2)}) async-start(bf16[32,72,128]{2,1,0:T(8,128)(2,1)} %broadcast_in_dim.51), calls=%async_computation.3 | async-start | bytes 1179648 | tf_op jit(solution)/shard_map/all_to_all | solution.py:248
  91.5 3.6 %collective-permute-start.7 = (bf16[12,3,256]{2,1,0:T(4,128)(2,1)S(1)}, bf16[12,3,256]{2,1,0:T(4,128)(2,1)S(1)}, u32[]{:S(2)}, u32[]{:S(2)}) collective-permute-start(bf16[12,3,256]{2,1,0:T(4,128)(2,1)S(1)} %get-tuple-element.61), channel_id=1, source_target_pairs={{64,128},{128,64},{192,256},{256,192},{320,384},{384,320},{448,0},... | collective-permute-start | bytes 55304 | tf_op jit(solution)/shard_map/ppermute | solution.py:280
  95.0 3.7 %collective-permute-start.6 = (bf16[12,3,256]{2,1,0:T(4,128)(2,1)S(1)}, bf16[12,3,256]{2,1,0:T(4,128)(2,1)S(1)}, u32[]{:S(2)}, u32[]{:S(2)}) collective-permute-start(bf16[12,3,256]{2,1,0:T(4,128)(2,1)S(1)} %get-tuple-element.62), channel_id=1, source_target_pairs={{0,64},{64,0},{128,192},{192,128},{256,320},{320,256},{384,448},{4... | collective-permute-start | bytes 55304 | tf_op jit(solution)/shard_map/ppermute | solution.py:281
  98.7 0.8 collective-permute-done.6.near_cols_ref
  99.6 3.3 %state.1 = bf16[6,64,256]{2,1,0:T(8,128)(2,1)} custom-call(s32[2]{0:T(128)S(1)} %pad_add_fusion.odd_ref, bf16[6,64,256]{2,1,0:T(8,128)(2,1)S(1)} %get-tuple-element.30.own_ref, bf16[3,64,256]{2,1,0:T(8,128)(2,1)S(1)} %collective-permute-done.4.near_rows_ref, bf16[3,64,256]{2,1,0:T(8,128)(2,1)S(1)} %collective-permute-done.5.far_rows_ref, ...), custom_call_target="tpu_custom_call" | custom-call | flops 10000000 | bytes 3000000 | tf_op jit(solution)/shard_map/state/pallas_call | solution.py:337
  102.9 1.5 %all-to-all-done.3.mine_ref = bf16[32,72,128]{2,1,0:T(8,128)(2,1)S(1)} async-done(((bf16[32,72,128]{2,1,0:T(8,128)(2,1)}), bf16[32,72,128]{2,1,0:T(8,128)(2,1)S(1)}, u32[]{:S(2)}, u32[]{:S(2)}) %all-to-all-start.3) | async-done | bytes 589856 | tf_op jit(solution)/shard_map/all_to_all | solution.py:248
  104.4 4.2 %collective-permute-start.8 = (bf16[32,72,128]{2,1,0:T(8,128)(2,1)S(1)}, bf16[32,72,128]{2,1,0:T(8,128)(2,1)S(1)}, u32[]{:S(2)}, u32[]{:S(2)}) collective-permute-start(bf16[32,72,128]{2,1,0:T(8,128)(2,1)S(1)} %all-to-all-done.3.mine_ref), channel_id=1, source_target_pairs={{0,64},{64,0},{1,65},{65,1},{2,66},{66,2},{3,67},{67,3},{4,68},{68... | collective-permute-start | bytes 1769480 | tf_op jit(solution)/shard_map/ppermute | solution.py:347
  108.6 1.6 %collective-permute-done.8.other_ref = bf16[32,72,128]{2,1,0:T(8,128)(2,1)S(1)} collective-permute-done((bf16[32,72,128]{2,1,0:T(8,128)(2,1)S(1)}, bf16[32,72,128]{2,1,0:T(8,128)(2,1)S(1)}, u32[]{:S(2)}, u32[]{:S(2)}) %collective-permute-start.8) | collective-permute-done | bytes 589856 | tf_op jit(solution)/shard_map/ppermute | solution.py:347
  110.2 1.6 %unpack.1 = (f32[7,7,256]{2,1,0:T(8,128)}, f32[1,256]{1,0:T(1,128)}, f32[1,256]{1,0:T(1,128)}, f32[1,256]{1,0:T(1,128)}, f32[256,1024]{1,0:T(8,128)}, /*index=5*...) custom-call(s32[1]{0:T(128)} %bitcast.1.core_ref, ...), custom_call_target="tpu_custom_call" | custom-call | tf_op jit(solution)/shard_map/unpack/pallas_call | solution.py:351
  (35 shorter events, 0.3 us)
Async XLA Ops:
  0.6 21.3 %copy-start.1 = (bf16[1,6,64,256]{3,2,1,0:T(8,128)(2,1)S(1)}, bf16[1,6,64,256]{3,2,1,0:T(8,128)(2,1)}, u32[]{:S(2)}) copy-start(bf16[1,6,64,256]{3,2,1,0:T(8,128)(2,1)} %param.12) | copy-start | bytes 589828
  0.7 21.3 %copy-start.2 = (f32[7,7,256]{2,1,0:T(8,128)S(1)}, f32[7,7,256]{2,1,0:T(8,128)}, u32[]{:S(2)}) copy-start(f32[7,7,256]{2,1,0:T(8,128)} %k_ref.3) | copy-start | bytes 150532
  0.7 21.3 %copy-start.10 = (f32[256]{0:T(256)S(1)}, f32[256]{0:T(256)}, u32[]{:S(2)}) copy-start(f32[256]{0:T(256)} %param.23) | copy-start | bytes 3076
  0.7 21.3 %copy-start.9 = (f32[256]{0:T(256)S(1)}, f32[256]{0:T(256)}, u32[]{:S(2)}) copy-start(f32[256]{0:T(256)} %param.22) | copy-start | bytes 3076
  0.7 21.3 %copy-start.5 = (f32[1024]{0:T(1024)S(1)}, f32[1024]{0:T(1024)}, u32[]{:S(2)}) copy-start(f32[1024]{0:T(1024)} %param.20) | copy-start | bytes 12292
  0.7 21.3 %copy-start.3 = (bf16[256,1024]{1,0:T(8,128)(2,1)S(1)}, bf16[256,1024]{1,0:T(8,128)(2,1)}, u32[]{:S(2)}) copy-start(bf16[256,1024]{1,0:T(8,128)(2,1)} %w_in_ref.1) | copy-start | bytes 1572868
  0.7 21.3 %copy-start.8 = (f32[256]{0:T(256)S(1)}, f32[256]{0:T(256)}, u32[]{:S(2)}) copy-start(f32[256]{0:T(256)} %param.18) | copy-start | bytes 3076
  0.7 21.3 %copy-start.7 = (f32[256]{0:T(256)S(1)}, f32[256]{0:T(256)}, u32[]{:S(2)}) copy-start(f32[256]{0:T(256)} %param.17) | copy-start | bytes 3076
  0.7 21.3 %copy-start.6 = (f32[256]{0:T(256)S(1)}, f32[256]{0:T(256)}, u32[]{:S(2)}) copy-start(f32[256]{0:T(256)} %param.16) | copy-start | bytes 3076
  1.8 11.5 %collective-permute-start.1 = (bf16[3,64,256]{2,1,0:T(8,128)(2,1)S(1)}, bf16[3,64,256]{2,1,0:T(8,128)(2,1)S(1)}, u32[]{:S(2)}, u32[]{:S(2)}) collective-permute-start(bf16[3,64,256]{2,1,0:T(8,128)(2,1)S(1)} %get-tuple-element.59), channel_id=1, source_target_pairs={{1,2},{2,1},{3,4},{4,3},{5,6},{6,5},{7,8},{8,7},{9,10},{10,9},{11,... | collective-permute-start | bytes 294920 | tf_op jit(solution)/shard_map/ppermute | solution.py:264
  2.5 10.8 %collective-permute-start = (bf16[3,64,256]{2,1,0:T(8,128)(2,1)S(1)}, bf16[3,64,256]{2,1,0:T(8,128)(2,1)S(1)}, u32[]{:S(2)}, u32[]{:S(2)}) collective-permute-start(bf16[3,64,256]{2,1,0:T(8,128)(2,1)S(1)} %get-tuple-element.60), channel_id=1, source_target_pairs={{0,1},{1,0},{2,3},{3,2},{4,5},{5,4},{6,7},{7,6},{8,9},{9,8},{10,11... | collective-permute-start | bytes 294920 | tf_op jit(solution)/shard_map/ppermute | solution.py:265
  13.4 7.6 %collective-permute-start.3 = (bf16[12,3,256]{2,1,0:T(4,128)(2,1)S(1)}, bf16[12,3,256]{2,1,0:T(4,128)(2,1)S(1)}, u32[]{:S(2)}, u32[]{:S(2)}) collective-permute-start(bf16[12,3,256]{2,1,0:T(4,128)(2,1)S(1)} %get-tuple-element.63), channel_id=1, source_target_pairs={{64,128},{128,64},{192,256},{256,192},{320,384},{384,320},{448,0},... | collective-permute-start | bytes 55304 | tf_op jit(solution)/shard_map/ppermute | solution.py:280
  17.7 4.0 %collective-permute-start.2 = (bf16[12,3,256]{2,1,0:T(4,128)(2,1)S(1)}, bf16[12,3,256]{2,1,0:T(4,128)(2,1)S(1)}, u32[]{:S(2)}, u32[]{:S(2)}) collective-permute-start(bf16[12,3,256]{2,1,0:T(4,128)(2,1)S(1)} %get-tuple-element.64), channel_id=1, source_target_pairs={{0,64},{64,0},{128,192},{192,128},{256,320},{320,256},{384,448},{4... | collective-permute-start | bytes 55304 | tf_op jit(solution)/shard_map/ppermute | solution.py:281
  22.0 1.0 copy-start.4
  37.9 28.0 %all-to-all-start.1 = ((bf16[32,72,128]{2,1,0:T(8,128)(2,1)}), bf16[32,72,128]{2,1,0:T(8,128)(2,1)S(1)}, u32[]{:S(2)}, u32[]{:S(2)}) async-start(bf16[32,72,128]{2,1,0:T(8,128)(2,1)} %fusion), calls=%async_computation.1 | async-start | bytes 1179648 | tf_op jit(solution)/shard_map/all_to_all | solution.py:248
  52.9 13.1 %collective-permute-start.5 = (bf16[3,64,256]{2,1,0:T(8,128)(2,1)S(1)}, bf16[3,64,256]{2,1,0:T(8,128)(2,1)S(1)}, u32[]{:S(2)}, u32[]{:S(2)}) collective-permute-start(bf16[3,64,256]{2,1,0:T(8,128)(2,1)S(1)} %get-tuple-element.51), channel_id=1, source_target_pairs={{1,2},{2,1},{3,4},{4,3},{5,6},{6,5},{7,8},{8,7},{9,10},{10,9},{11,... | collective-permute-start | bytes 294920 | tf_op jit(solution)/shard_map/ppermute | solution.py:264
  53.6 12.4 %collective-permute-start.4 = (bf16[3,64,256]{2,1,0:T(8,128)(2,1)S(1)}, bf16[3,64,256]{2,1,0:T(8,128)(2,1)S(1)}, u32[]{:S(2)}, u32[]{:S(2)}) collective-permute-start(bf16[3,64,256]{2,1,0:T(8,128)(2,1)S(1)} %get-tuple-element.52), channel_id=1, source_target_pairs={{0,1},{1,0},{2,3},{3,2},{4,5},{5,4},{6,7},{7,6},{8,9},{9,8},{10,11... | collective-permute-start | bytes 294920 | tf_op jit(solution)/shard_map/ppermute | solution.py:265
  66.0 33.5 %copy-start = (bf16[1,6,64,256]{3,2,1,0:T(8,128)(2,1)S(1)}, bf16[1,6,64,256]{3,2,1,0:T(8,128)(2,1)}, u32[]{:S(2)}) copy-start(bf16[1,6,64,256]{3,2,1,0:T(8,128)(2,1)} %param.14) | copy-start | bytes 589828
  83.1 21.3 %all-to-all-start.3 = ((bf16[32,72,128]{2,1,0:T(8,128)(2,1)}), bf16[32,72,128]{2,1,0:T(8,128)(2,1)S(1)}, u32[]{:S(2)}, u32[]{:S(2)}) async-start(bf16[32,72,128]{2,1,0:T(8,128)(2,1)} %broadcast_in_dim.51), calls=%async_computation.3 | async-start | bytes 1179648 | tf_op jit(solution)/shard_map/all_to_all | solution.py:248
  91.5 7.3 %collective-permute-start.7 = (bf16[12,3,256]{2,1,0:T(4,128)(2,1)S(1)}, bf16[12,3,256]{2,1,0:T(4,128)(2,1)S(1)}, u32[]{:S(2)}, u32[]{:S(2)}) collective-permute-start(bf16[12,3,256]{2,1,0:T(4,128)(2,1)S(1)} %get-tuple-element.61), channel_id=1, source_target_pairs={{64,128},{128,64},{192,256},{256,192},{320,384},{384,320},{448,0},... | collective-permute-start | bytes 55304 | tf_op jit(solution)/shard_map/ppermute | solution.py:280
  95.0 4.5 %collective-permute-start.6 = (bf16[12,3,256]{2,1,0:T(4,128)(2,1)S(1)}, bf16[12,3,256]{2,1,0:T(4,128)(2,1)S(1)}, u32[]{:S(2)}, u32[]{:S(2)}) collective-permute-start(bf16[12,3,256]{2,1,0:T(4,128)(2,1)S(1)} %get-tuple-element.62), channel_id=1, source_target_pairs={{0,64},{64,0},{128,192},{192,128},{256,320},{320,256},{384,448},{4... | collective-permute-start | bytes 55304 | tf_op jit(solution)/shard_map/ppermute | solution.py:281
  104.4 5.9 %collective-permute-start.8 = (bf16[32,72,128]{2,1,0:T(8,128)(2,1)S(1)}, bf16[32,72,128]{2,1,0:T(8,128)(2,1)S(1)}, u32[]{:S(2)}, u32[]{:S(2)}) collective-permute-start(bf16[32,72,128]{2,1,0:T(8,128)(2,1)S(1)} %all-to-all-done.3.mine_ref), channel_id=1, source_target_pairs={{0,64},{64,0},{1,65},{65,1},{2,66},{66,2},{3,67},{67,3},{4,68},{68... | collective-permute-start | bytes 1769480 | tf_op jit(solution)/shard_map/ppermute | solution.py:347

commit v6 on v5

--- a/solution.py
+++ b/solution.py
@@ -329,11 +329,12 @@
     value = (pair[0].astype(F32) + pair[1].astype(F32)).astype(BF16)
     value = exchange(value, PLANE)
     value = jnp.sum(value.astype(F32), axis=0).astype(BF16)
-    value, rows_sent = lax.optimization_barrier((value, rows_sent))
     value = exchange(jnp.broadcast_to(value[None], (column,) + value.shape), COLUMN)
     value = jnp.sum(value.astype(F32), axis=0).astype(BF16)
+    value, rows_sent = lax.optimization_barrier((value, rows_sent))
     value = exchange(jnp.broadcast_to(value[None], (plane,) + value.shape), PLANE)
     cols_sent = swap_cols(grad_depth, *rows_sent, odd_lat, odd_lon)
+    value, cols_sent = lax.optimization_barrier((value, cols_sent))
     grad_state = pl.pallas_call(
         state_kernel,
         out_shape=jax.ShapeDtypeStruct((rows, cols, channels), BF16),
@@ -343,7 +344,6 @@
         cost_estimate=pl.CostEstimate(flops=10000000, transcendentals=0, bytes_accessed=3000000),
         name="state",
     )(odd, grad_depth, *rows_sent, *cols_sent, cot, dw_kernel)
-    value, grad_state = lax.optimization_barrier((value, grad_state))
     other = lax.ppermute(value, "core", [(0, 1), (1, 0)])
     total_cells = cells * lax.axis_size(LON) * lax.axis_size(LAT)
     factor = 1.0 / math.sqrt(total_cells)

time: 113 us -> 116 us (1.027)
  blocking collectives: 22.3 us -> 33.9 us
  waiting for transfers between devices: 14 us -> 7.82 us
  starting transfers between devices: 54.7 us -> 52.7 us
    all_to_all x1, blocking collectives: 16.1 us -> 27.8 us  [exchange(): return lax.all_to_all(value, EVERY, 0, 0, axis_index_groups=groups)]
    all_to_all x2, starting transfers between devices: 23.2 us -> 16.6 us  [exchange(): return lax.all_to_all(value, EVERY, 0, 0, axis_index_groups=groups)]
    all_to_all x2, waiting for transfers between devices: 10.8 us -> 5.42 us  [exchange(): return lax.all_to_all(value, EVERY, 0, 0, axis_index_groups=groups)]
    ppermute x2, starting transfers between devices: 11.1 us -> 14 us  [swap_rows(): near_rows = lax.ppermute(jnp.where(odd, first, last), LAT, near)]
    ppermute x2, starting transfers between devices: 7.89 us -> 10.2 us  [swap_cols(): far_cols = lax.ppermute(jnp.where(odd_lon, last, first), LON, far)]
    ppermute x2, starting transfers between devices: 6.89 us -> 5.13 us  [swap_cols(): near_cols = lax.ppermute(jnp.where(odd_lon, first, last), LON, near)]
    ppermute x1, waiting for transfers between devices: 1.61 us -> 0.01 us  [local(): other = lax.ppermute(value, 'core', [(0, 1), (1, 0)])]
  transfers between devices with their start and end apart: 11 -> 11, of which waited for: 5 -> 6; matrix products, arithmetic and copies ran while one was open for 3% -> 2% of each run, Pallas kernels for 3% -> 3%
where the time goes in v6:
time: 116 us; the launch traced here: 115 us
  starting transfers between devices  52.7 us (45%)
  blocking collectives  33.9 us (29%)
  Pallas kernels  12.7 us (11%)
  waiting for transfers between devices  7.82 us (7%)
  local copies, waits for them, and re-layouts  3.64 us (3%)
  other arithmetic  3.35 us (3%)
    all_to_all x1, blocking collectives, exchange(): return lax.all_to_all(value, EVERY, 0, 0, axis_index_groups=groups)  27.8 us
    all_to_all x2, starting transfers between devices, exchange(): return lax.all_to_all(value, EVERY, 0, 0, axis_index_groups=groups)  16.6 us
    ppermute x2, starting transfers between devices, swap_rows(): near_rows = lax.ppermute(jnp.where(odd, first, last), LAT, near)  14 us
    ppermute x2, starting transfers between devices, swap_cols(): far_cols = lax.ppermute(jnp.where(odd_lon, last, first), LON, far)  10.2 us
    pallas_call x1, Pallas kernels, local(): pl.pallas_call(block_kernel, out_shape=(jax.ShapeDtypeStruct((rows, cols,...  7.76 us
    all_to_all x1, blocking collectives, local(): lax.all_to_all(chunks.reshape(2, plane, CHUNK_ROWS, LANES), 'core', 0, 0)  6.16 us
    all_to_all x2, waiting for transfers between devices, exchange(): return lax.all_to_all(value, EVERY, 0, 0, axis_index_groups=groups)  5.42 us
    ppermute x1, starting transfers between devices, local(): other = lax.ppermute(value, 'core', [(0, 1), (1, 0)])  5.26 us
  transfers between devices with their start and end apart: 11, of which 6 were waited for; matrix products, arithmetic and copies ran while one was open for 2% of the time, Pallas kernels for 3%

profile of v6, /device:TPU:1, one launch (start us, length us, event | category | flops | bytes accessed | tf_op | source)
XLA Modules:
  0.0 115.1 jit_solution(957214176380979499)
XLA Ops:
  0.7 1.1 select_bitcast_fusion
  1.8 0.7 collective-permute-start.1
  2.5 8.2 %collective-permute-start = (bf16[3,64,256]{2,1,0:T(8,128)(2,1)S(1)}, bf16[3,64,256]{2,1,0:T(8,128)(2,1)S(1)}, u32[]{:S(2)}, u32[]{:S(2)}) collective-permute-start(bf16[3,64,256]{2,1,0:T(8,128)(2,1)S(1)} %get-tuple-element.62), channel_id=1, source_target_pairs={{0,1},{1,0},{2,3},{3,2},{4,5},{5,4},{6,7},{7,6},{8,9},{9,8},{10,11... | collective-permute-start | bytes 294920 | tf_op jit(solution)/shard_map/ppermute | solution.py:265
  10.7 0.7 convert_reduce_fusion
  11.5 1.0 bitcast_multiply_fusion.masked_ref
  12.5 0.8 fusion.2
  13.4 4.3 %collective-permute-start.3 = (bf16[12,3,256]{2,1,0:T(4,128)(2,1)S(1)}, bf16[12,3,256]{2,1,0:T(4,128)(2,1)S(1)}, u32[]{:S(2)}, u32[]{:S(2)}) collective-permute-start(bf16[12,3,256]{2,1,0:T(4,128)(2,1)S(1)} %get-tuple-element.65), channel_id=1, source_target_pairs={{64,128},{128,64},{192,256},{256,192},{320,384},{384,320},{448,0},... | collective-permute-start | bytes 55304 | tf_op jit(solution)/shard_map/ppermute | solution.py:280
  17.7 3.2 %collective-permute-start.2 = (bf16[12,3,256]{2,1,0:T(4,128)(2,1)S(1)}, bf16[12,3,256]{2,1,0:T(4,128)(2,1)S(1)}, u32[]{:S(2)}, u32[]{:S(2)}) collective-permute-start(bf16[12,3,256]{2,1,0:T(4,128)(2,1)S(1)} %get-tuple-element.66), channel_id=1, source_target_pairs={{0,64},{64,0},{128,192},{192,128},{256,320},{320,256},{384,448},{4... | collective-permute-start | bytes 55304 | tf_op jit(solution)/shard_map/ppermute | solution.py:281
  21.0 0.7 collective-permute-done.2.near_cols_ref
  21.8 0.1 broadcast_in_dim.42.mask_ref
  22.0 1.0 copy-done.4
  23.0 7.8 %block.1 = (bf16[6,64,256]{2,1,0:T(8,128)(2,1)}, bf16[6,64,256]{2,1,0:T(8,128)(2,1)S(1)}, bf16[64,72,128]{2,1,0:T(8,128)(2,1)S(1)}) custom-call(s32[2]{0:T(128)S(1)} %pad_add_fusion.odd_ref, bf16[6,64,256]{2,1,0:T(8,128)(2,1)S(1)} %bitcast.30, bf16[3,64,256]{2,1,0:T(8,128)(2,1)S(1)} %collective-permute-done.near_rows_ref, ...), custom_call_target="tpu_custom_call" | custom-call | flops 1300000000 | bytes 6000000 | tf_op jit(solution)/shard_map/block/pallas_call | solution.py:306
  30.8 6.2 %all_to_all.20 = bf16[2,32,72,128]{3,2,1,0:T(8,128)(2,1)S(1)} all-to-all(bf16[2,32,72,128]{3,2,1,0:T(8,128)(2,1)S(1)} %bitcast.27), channel_id=1, replica_groups=mesh['y_lo'=4,'core'=2,'x'=4,'y_hi'=2,'z'=8] {'core'}, dimensions={0} | all-to-all | bytes 2359296 | tf_op jit(solution)/shard_map/all_to_all | solution.py:328
  37.0 0.2 fusion
  37.1 27.8 %all_to_all.21 = bf16[32,72,128]{2,1,0:T(8,128)(2,1)S(1)} all-to-all(bf16[32,72,128]{2,1,0:T(8,128)(2,1)S(1)} %fusion), channel_id=1, replica_groups={{0,1,2,3,4,5,6,7,16,17,18,19,20,21,22,23,32,33,34,35,36,37,38,39,48,49,..., dimensions={0} | all-to-all | bytes 1179648 | tf_op jit(solution)/shard_map/all_to_all | solution.py:248
  64.9 0.1 reduce_sum.24
  65.0 0.7 broadcast_in_dim.50
  65.7 6.6 %all-to-all-start.2 = ((bf16[8,72,128]{2,1,0:T(8,128)(2,1)}), bf16[8,72,128]{2,1,0:T(8,128)(2,1)S(1)}, u32[]{:S(2)}, u32[]{:S(2)}) async-start(bf16[8,72,128]{2,1,0:T(8,128)(2,1)} %broadcast_in_dim.50), calls=%async_computation.2 | async-start | bytes 294912 | tf_op jit(solution)/shard_map/all_to_all | solution.py:248
  72.3 0.8 collective-permute-start.5
  73.1 5.8 %collective-permute-start.4 = (bf16[3,64,256]{2,1,0:T(8,128)(2,1)S(1)}, bf16[3,64,256]{2,1,0:T(8,128)(2,1)S(1)}, u32[]{:S(2)}, u32[]{:S(2)}) collective-permute-start(bf16[3,64,256]{2,1,0:T(8,128)(2,1)S(1)} %get-tuple-element.54), channel_id=1, source_target_pairs={{0,1},{1,0},{2,3},{3,2},{4,5},{5,4},{6,7},{7,6},{8,9},{9,8},{10,11... | collective-permute-start | bytes 294920 | tf_op jit(solution)/shard_map/ppermute | solution.py:265
  78.9 1.5 %all-to-all-done.2 = bf16[8,72,128]{2,1,0:T(8,128)(2,1)S(1)} async-done(((bf16[8,72,128]{2,1,0:T(8,128)(2,1)}), bf16[8,72,128]{2,1,0:T(8,128)(2,1)S(1)}, u32[]{:S(2)}, u32[]{:S(2)}) %all-to-all-start.2) | async-done | bytes 147488 | tf_op jit(solution)/shard_map/all_to_all | solution.py:248
  80.5 0.5 collective-permute-done.4.near_rows_ref
  80.9 0.9 broadcast_in_dim.51
  81.8 10.0 %all-to-all-start.3 = ((bf16[32,72,128]{2,1,0:T(8,128)(2,1)}), bf16[32,72,128]{2,1,0:T(8,128)(2,1)S(1)}, u32[]{:S(2)}, u32[]{:S(2)}) async-start(bf16[32,72,128]{2,1,0:T(8,128)(2,1)} %broadcast_in_dim.51), calls=%async_computation.3 | async-start | bytes 1179648 | tf_op jit(solution)/shard_map/all_to_all | solution.py:248
  92.0 5.9 %collective-permute-start.7 = (bf16[12,3,256]{2,1,0:T(4,128)(2,1)S(1)}, bf16[12,3,256]{2,1,0:T(4,128)(2,1)S(1)}, u32[]{:S(2)}, u32[]{:S(2)}) collective-permute-start(bf16[12,3,256]{2,1,0:T(4,128)(2,1)S(1)} %get-tuple-element.63), channel_id=1, source_target_pairs={{64,128},{128,64},{192,256},{256,192},{320,384},{384,320},{448,0},... | collective-permute-start | bytes 55304 | tf_op jit(solution)/shard_map/ppermute | solution.py:280
  97.9 1.9 %collective-permute-start.6 = (bf16[12,3,256]{2,1,0:T(4,128)(2,1)S(1)}, bf16[12,3,256]{2,1,0:T(4,128)(2,1)S(1)}, u32[]{:S(2)}, u32[]{:S(2)}) collective-permute-start(bf16[12,3,256]{2,1,0:T(4,128)(2,1)S(1)} %get-tuple-element.64), channel_id=1, source_target_pairs={{0,64},{64,0},{128,192},{192,128},{256,320},{320,256},{384,448},{4... | collective-permute-start | bytes 55304 | tf_op jit(solution)/shard_map/ppermute | solution.py:281
  99.8 0.8 collective-permute-done.7.far_cols_ref
  100.6 0.4 collective-permute-done.6.near_cols_ref
  100.9 3.9 %all-to-all-done.3.mine_ref = bf16[32,72,128]{2,1,0:T(8,128)(2,1)S(1)} async-done(((bf16[32,72,128]{2,1,0:T(8,128)(2,1)}), bf16[32,72,128]{2,1,0:T(8,128)(2,1)S(1)}, u32[]{:S(2)}, u32[]{:S(2)}) %all-to-all-start.3) | async-done | bytes 589856 | tf_op jit(solution)/shard_map/all_to_all | solution.py:248
  104.9 5.3 %collective-permute-start.8 = (bf16[32,72,128]{2,1,0:T(8,128)(2,1)S(1)}, bf16[32,72,128]{2,1,0:T(8,128)(2,1)S(1)}, u32[]{:S(2)}, u32[]{:S(2)}) collective-permute-start(bf16[32,72,128]{2,1,0:T(8,128)(2,1)S(1)} %all-to-all-done.3.mine_ref), channel_id=1, source_target_pairs={{0,64},{64,0},{1,65},{65,1},{2,66},{66,2},{3,67},{67,3},{4,68},{68... | collective-permute-start | bytes 1769480 | tf_op jit(solution)/shard_map/ppermute | solution.py:347
  110.1 3.4 %state.1 = bf16[6,64,256]{2,1,0:T(8,128)(2,1)} custom-call(s32[2]{0:T(128)S(1)} %pad_add_fusion.odd_ref, bf16[6,64,256]{2,1,0:T(8,128)(2,1)S(1)} %get-tuple-element.30.own_ref, bf16[3,64,256]{2,1,0:T(8,128)(2,1)S(1)} %collective-permute-done.4.near_rows_ref, bf16[3,64,256]{2,1,0:T(8,128)(2,1)S(1)} %collective-permute-done.5.far_rows_ref, ...), custom_call_target="tpu_custom_call" | custom-call | flops 10000000 | bytes 3000000 | tf_op jit(solution)/shard_map/state/pallas_call | solution.py:338
  113.5 1.6 %unpack.1 = (f32[7,7,256]{2,1,0:T(8,128)}, f32[1,256]{1,0:T(1,128)}, f32[1,256]{1,0:T(1,128)}, f32[1,256]{1,0:T(1,128)}, f32[256,1024]{1,0:T(8,128)}, /*index=5*...) custom-call(s32[1]{0:T(128)} %bitcast.1.core_ref, ...), custom_call_target="tpu_custom_call" | custom-call | tf_op jit(solution)/shard_map/unpack/pallas_call | solution.py:351
  (35 shorter events, 0.4 us)
Async XLA Ops:
  0.6 21.3 %copy-start.1 = (bf16[1,6,64,256]{3,2,1,0:T(8,128)(2,1)S(1)}, bf16[1,6,64,256]{3,2,1,0:T(8,128)(2,1)}, u32[]{:S(2)}) copy-start(bf16[1,6,64,256]{3,2,1,0:T(8,128)(2,1)} %param.12) | copy-start | bytes 589828
  0.7 21.3 %copy-start.2 = (f32[7,7,256]{2,1,0:T(8,128)S(1)}, f32[7,7,256]{2,1,0:T(8,128)}, u32[]{:S(2)}) copy-start(f32[7,7,256]{2,1,0:T(8,128)} %k_ref.3) | copy-start | bytes 150532
  0.7 21.3 %copy-start.10 = (f32[256]{0:T(256)S(1)}, f32[256]{0:T(256)}, u32[]{:S(2)}) copy-start(f32[256]{0:T(256)} %param.23) | copy-start | bytes 3076
  0.7 21.3 %copy-start.9 = (f32[256]{0:T(256)S(1)}, f32[256]{0:T(256)}, u32[]{:S(2)}) copy-start(f32[256]{0:T(256)} %param.22) | copy-start | bytes 3076
  0.7 21.3 %copy-start.5 = (f32[1024]{0:T(1024)S(1)}, f32[1024]{0:T(1024)}, u32[]{:S(2)}) copy-start(f32[1024]{0:T(1024)} %param.20) | copy-start | bytes 12292
  0.7 21.3 %copy-start.3 = (bf16[256,1024]{1,0:T(8,128)(2,1)S(1)}, bf16[256,1024]{1,0:T(8,128)(2,1)}, u32[]{:S(2)}) copy-start(bf16[256,1024]{1,0:T(8,128)(2,1)} %w_in_ref.1) | copy-start | bytes 1572868
  0.7 21.3 %copy-start.8 = (f32[256]{0:T(256)S(1)}, f32[256]{0:T(256)}, u32[]{:S(2)}) copy-start(f32[256]{0:T(256)} %param.18) | copy-start | bytes 3076
  0.7 21.3 %copy-start.7 = (f32[256]{0:T(256)S(1)}, f32[256]{0:T(256)}, u32[]{:S(2)}) copy-start(f32[256]{0:T(256)} %param.17) | copy-start | bytes 3076
  0.7 21.3 %copy-start.6 = (f32[256]{0:T(256)S(1)}, f32[256]{0:T(256)}, u32[]{:S(2)}) copy-start(f32[256]{0:T(256)} %param.16) | copy-start | bytes 3076
  1.8 11.5 %collective-permute-start.1 = (bf16[3,64,256]{2,1,0:T(8,128)(2,1)S(1)}, bf16[3,64,256]{2,1,0:T(8,128)(2,1)S(1)}, u32[]{:S(2)}, u32[]{:S(2)}) collective-permute-start(bf16[3,64,256]{2,1,0:T(8,128)(2,1)S(1)} %get-tuple-element.61), channel_id=1, source_target_pairs={{1,2},{2,1},{3,4},{4,3},{5,6},{6,5},{7,8},{8,7},{9,10},{10,9},{11,... | collective-permute-start | bytes 294920 | tf_op jit(solution)/shard_map/ppermute | solution.py:264
  2.5 10.8 %collective-permute-start = (bf16[3,64,256]{2,1,0:T(8,128)(2,1)S(1)}, bf16[3,64,256]{2,1,0:T(8,128)(2,1)S(1)}, u32[]{:S(2)}, u32[]{:S(2)}) collective-permute-start(bf16[3,64,256]{2,1,0:T(8,128)(2,1)S(1)} %get-tuple-element.62), channel_id=1, source_target_pairs={{0,1},{1,0},{2,3},{3,2},{4,5},{5,4},{6,7},{7,6},{8,9},{9,8},{10,11... | collective-permute-start | bytes 294920 | tf_op jit(solution)/shard_map/ppermute | solution.py:265
  13.4 7.6 %collective-permute-start.3 = (bf16[12,3,256]{2,1,0:T(4,128)(2,1)S(1)}, bf16[12,3,256]{2,1,0:T(4,128)(2,1)S(1)}, u32[]{:S(2)}, u32[]{:S(2)}) collective-permute-start(bf16[12,3,256]{2,1,0:T(4,128)(2,1)S(1)} %get-tuple-element.65), channel_id=1, source_target_pairs={{64,128},{128,64},{192,256},{256,192},{320,384},{384,320},{448,0},... | collective-permute-start | bytes 55304 | tf_op jit(solution)/shard_map/ppermute | solution.py:280
  17.7 4.0 %collective-permute-start.2 = (bf16[12,3,256]{2,1,0:T(4,128)(2,1)S(1)}, bf16[12,3,256]{2,1,0:T(4,128)(2,1)S(1)}, u32[]{:S(2)}, u32[]{:S(2)}) collective-permute-start(bf16[12,3,256]{2,1,0:T(4,128)(2,1)S(1)} %get-tuple-element.66), channel_id=1, source_target_pairs={{0,64},{64,0},{128,192},{192,128},{256,320},{320,256},{384,448},{4... | collective-permute-start | bytes 55304 | tf_op jit(solution)/shard_map/ppermute | solution.py:281
  22.0 1.0 copy-start.4
  65.7 14.8 %all-to-all-start.2 = ((bf16[8,72,128]{2,1,0:T(8,128)(2,1)}), bf16[8,72,128]{2,1,0:T(8,128)(2,1)S(1)}, u32[]{:S(2)}, u32[]{:S(2)}) async-start(bf16[8,72,128]{2,1,0:T(8,128)(2,1)} %broadcast_in_dim.50), calls=%async_computation.2 | async-start | bytes 294912 | tf_op jit(solution)/shard_map/all_to_all | solution.py:248
  72.3 37.8 %copy-start = (bf16[1,6,64,256]{3,2,1,0:T(8,128)(2,1)S(1)}, bf16[1,6,64,256]{3,2,1,0:T(8,128)(2,1)}, u32[]{:S(2)}) copy-start(bf16[1,6,64,256]{3,2,1,0:T(8,128)(2,1)} %param.14) | copy-start | bytes 589828
  72.3 8.1 %collective-permute-start.5 = (bf16[3,64,256]{2,1,0:T(8,128)(2,1)S(1)}, bf16[3,64,256]{2,1,0:T(8,128)(2,1)S(1)}, u32[]{:S(2)}, u32[]{:S(2)}) collective-permute-start(bf16[3,64,256]{2,1,0:T(8,128)(2,1)S(1)} %get-tuple-element.53), channel_id=1, source_target_pairs={{1,2},{2,1},{3,4},{4,3},{5,6},{6,5},{7,8},{8,7},{9,10},{10,9},{11,... | collective-permute-start | bytes 294920 | tf_op jit(solution)/shard_map/ppermute | solution.py:264
  73.1 7.8 %collective-permute-start.4 = (bf16[3,64,256]{2,1,0:T(8,128)(2,1)S(1)}, bf16[3,64,256]{2,1,0:T(8,128)(2,1)S(1)}, u32[]{:S(2)}, u32[]{:S(2)}) collective-permute-start(bf16[3,64,256]{2,1,0:T(8,128)(2,1)S(1)} %get-tuple-element.54), channel_id=1, source_target_pairs={{0,1},{1,0},{2,3},{3,2},{4,5},{5,4},{6,7},{7,6},{8,9},{9,8},{10,11... | collective-permute-start | bytes 294920 | tf_op jit(solution)/shard_map/ppermute | solution.py:265
  81.8 23.0 %all-to-all-start.3 = ((bf16[32,72,128]{2,1,0:T(8,128)(2,1)}), bf16[32,72,128]{2,1,0:T(8,128)(2,1)S(1)}, u32[]{:S(2)}, u32[]{:S(2)}) async-start(bf16[32,72,128]{2,1,0:T(8,128)(2,1)} %broadcast_in_dim.51), calls=%async_computation.3 | async-start | bytes 1179648 | tf_op jit(solution)/shard_map/all_to_all | solution.py:248
  92.0 8.6 %collective-permute-start.7 = (bf16[12,3,256]{2,1,0:T(4,128)(2,1)S(1)}, bf16[12,3,256]{2,1,0:T(4,128)(2,1)S(1)}, u32[]{:S(2)}, u32[]{:S(2)}) collective-permute-start(bf16[12,3,256]{2,1,0:T(4,128)(2,1)S(1)} %get-tuple-element.63), channel_id=1, source_target_pairs={{64,128},{128,64},{192,256},{256,192},{320,384},{384,320},{448,0},... | collective-permute-start | bytes 55304 | tf_op jit(solution)/shard_map/ppermute | solution.py:280
  97.9 3.1 %collective-permute-start.6 = (bf16[12,3,256]{2,1,0:T(4,128)(2,1)S(1)}, bf16[12,3,256]{2,1,0:T(4,128)(2,1)S(1)}, u32[]{:S(2)}, u32[]{:S(2)}) collective-permute-start(bf16[12,3,256]{2,1,0:T(4,128)(2,1)S(1)} %get-tuple-element.64), channel_id=1, source_target_pairs={{0,64},{64,0},{128,192},{192,128},{256,320},{320,256},{384,448},{4... | collective-permute-start | bytes 55304 | tf_op jit(solution)/shard_map/ppermute | solution.py:281
  104.9 8.6 %collective-permute-start.8 = (bf16[32,72,128]{2,1,0:T(8,128)(2,1)S(1)}, bf16[32,72,128]{2,1,0:T(8,128)(2,1)S(1)}, u32[]{:S(2)}, u32[]{:S(2)}) collective-permute-start(bf16[32,72,128]{2,1,0:T(8,128)(2,1)S(1)} %all-to-all-done.3.mine_ref), channel_id=1, source_target_pairs={{0,64},{64,0},{1,65},{65,1},{2,66},{66,2},{3,67},{67,3},{4,68},{68... | collective-permute-start | bytes 1769480 | tf_op jit(solution)/shard_map/ppermute | solution.py:347

commit v7 on v6

--- a/solution.py
+++ b/solution.py
@@ -329,9 +329,9 @@
     value = (pair[0].astype(F32) + pair[1].astype(F32)).astype(BF16)
     value = exchange(value, PLANE)
     value = jnp.sum(value.astype(F32), axis=0).astype(BF16)
+    value, rows_sent = lax.optimization_barrier((value, rows_sent))
     value = exchange(jnp.broadcast_to(value[None], (column,) + value.shape), COLUMN)
     value = jnp.sum(value.astype(F32), axis=0).astype(BF16)
-    value, rows_sent = lax.optimization_barrier((value, rows_sent))
     value = exchange(jnp.broadcast_to(value[None], (plane,) + value.shape), PLANE)
     cols_sent = swap_cols(grad_depth, *rows_sent, odd_lat, odd_lon)
     value, cols_sent = lax.optimization_barrier((value, cols_sent))

time: 116 us -> 114 us (0.983)
  blocking collectives: 33.9 us -> 22.3 us
  waiting for transfers between devices: 7.82 us -> 15.7 us
  starting transfers between devices: 52.7 us -> 54.7 us
    all_to_all x1, blocking collectives: 27.8 us -> 16.1 us  [exchange(): return lax.all_to_all(value, EVERY, 0, 0, axis_index_groups=groups)]
    all_to_all x2, waiting for transfers between devices: 5.42 us -> 14.2 us  [exchange(): return lax.all_to_all(value, EVERY, 0, 0, axis_index_groups=groups)]
    all_to_all x2, starting transfers between devices: 16.6 us -> 23.2 us  [exchange(): return lax.all_to_all(value, EVERY, 0, 0, axis_index_groups=groups)]
    ppermute x2, starting transfers between devices: 14 us -> 11.1 us  [swap_rows(): near_rows = lax.ppermute(jnp.where(odd, first, last), LAT, near)]
    ppermute x2, starting transfers between devices: 10.2 us -> 7.89 us  [swap_cols(): far_cols = lax.ppermute(jnp.where(odd_lon, last, first), LON, far)]
    ppermute x2, starting transfers between devices: 5.13 us -> 6.89 us  [swap_cols(): near_cols = lax.ppermute(jnp.where(odd_lon, first, last), LON, near)]
  transfers between devices with their start and end apart: 11 -> 11, of which waited for: 6 -> 4; matrix products, arithmetic and copies ran while one was open for 2% -> 3% of each run, Pallas kernels for 3% -> 3%
where the time goes in v7:
time: 114 us
  starting transfers between devices  54.7 us (48%)
  blocking collectives  22.3 us (20%)
  waiting for transfers between devices  15.7 us (14%)
  Pallas kernels  12.7 us (11%)
  other arithmetic  4.16 us (4%)
  local copies, waits for them, and re-layouts  2.98 us (3%)
    all_to_all x2, starting transfers between devices, exchange(): return lax.all_to_all(value, EVERY, 0, 0, axis_index_groups=groups)  23.2 us
    all_to_all x1, blocking collectives, exchange(): return lax.all_to_all(value, EVERY, 0, 0, axis_index_groups=groups)  16.1 us
    all_to_all x2, waiting for transfers between devices, exchange(): return lax.all_to_all(value, EVERY, 0, 0, axis_index_groups=groups)  14.2 us
    ppermute x2, starting transfers between devices, swap_rows(): near_rows = lax.ppermute(jnp.where(odd, first, last), LAT, near)  11.1 us
    ppermute x2, starting transfers between devices, swap_cols(): far_cols = lax.ppermute(jnp.where(odd_lon, last, first), LON, far)  7.89 us
    pallas_call x1, Pallas kernels, local(): pl.pallas_call(block_kernel, out_shape=(jax.ShapeDtypeStruct((rows, cols,...  7.76 us
    ppermute x2, starting transfers between devices, swap_cols(): near_cols = lax.ppermute(jnp.where(odd_lon, first, last), LON, near)  6.89 us
    all_to_all x1, blocking collectives, local(): lax.all_to_all(chunks.reshape(2, plane, CHUNK_ROWS, LANES), 'core', 0, 0)  6.16 us
  transfers between devices with their start and end apart: 11, of which 4 were waited for; matrix products, arithmetic and copies ran while one was open for 3% of the time, Pallas kernels for 3%

profile of v7, /device:TPU:1, one launch (start us, length us, event | category | flops | bytes accessed | tf_op | source)
XLA Modules:
  0.0 113.6 jit_solution(6805430170958141945)
XLA Ops:
  0.7 1.1 select_bitcast_fusion
  1.8 0.7 collective-permute-start.1
  2.5 8.2 %collective-permute-start = (bf16[3,64,256]{2,1,0:T(8,128)(2,1)S(1)}, bf16[3,64,256]{2,1,0:T(8,128)(2,1)S(1)}, u32[]{:S(2)}, u32[]{:S(2)}) collective-permute-start(bf16[3,64,256]{2,1,0:T(8,128)(2,1)S(1)} %get-tuple-element.62), channel_id=1, source_target_pairs={{0,1},{1,0},{2,3},{3,2},{4,5},{5,4},{6,7},{7,6},{8,9},{9,8},{10,11... | collective-permute-start | bytes 294920 | tf_op jit(solution)/shard_map/ppermute | solution.py:265
  10.7 0.7 convert_reduce_fusion
  11.4 0.1 convert_element_type.29
  11.5 1.0 bitcast_multiply_fusion.masked_ref
  12.5 0.8 fusion.2
  13.4 4.3 %collective-permute-start.3 = (bf16[12,3,256]{2,1,0:T(4,128)(2,1)S(1)}, bf16[12,3,256]{2,1,0:T(4,128)(2,1)S(1)}, u32[]{:S(2)}, u32[]{:S(2)}) collective-permute-start(bf16[12,3,256]{2,1,0:T(4,128)(2,1)S(1)} %get-tuple-element.65), channel_id=1, source_target_pairs={{64,128},{128,64},{192,256},{256,192},{320,384},{384,320},{448,0},... | collective-permute-start | bytes 55304 | tf_op jit(solution)/shard_map/ppermute | solution.py:280
  17.7 3.2 %collective-permute-start.2 = (bf16[12,3,256]{2,1,0:T(4,128)(2,1)S(1)}, bf16[12,3,256]{2,1,0:T(4,128)(2,1)S(1)}, u32[]{:S(2)}, u32[]{:S(2)}) collective-permute-start(bf16[12,3,256]{2,1,0:T(4,128)(2,1)S(1)} %get-tuple-element.66), channel_id=1, source_target_pairs={{0,64},{64,0},{128,192},{192,128},{256,320},{320,256},{384,448},{4... | collective-permute-start | bytes 55304 | tf_op jit(solution)/shard_map/ppermute | solution.py:281
  21.0 0.1 pad_add_fusion.odd_ref
  21.0 0.7 collective-permute-done.2.near_cols_ref
  21.8 0.1 broadcast_in_dim.42.mask_ref
  22.0 0.0 copy-start.4
  22.0 1.0 copy-done.4
  23.0 7.8 %block.1 = (bf16[6,64,256]{2,1,0:T(8,128)(2,1)}, bf16[6,64,256]{2,1,0:T(8,128)(2,1)S(1)}, bf16[64,72,128]{2,1,0:T(8,128)(2,1)S(1)}) custom-call(s32[2]{0:T(128)S(1)} %pad_add_fusion.odd_ref, bf16[6,64,256]{2,1,0:T(8,128)(2,1)S(1)} %bitcast.30, bf16[3,64,256]{2,1,0:T(8,128)(2,1)S(1)} %collective-permute-done.near_rows_ref, ...), custom_call_target="tpu_custom_call" | custom-call | flops 1300000000 | bytes 6000000 | tf_op jit(solution)/shard_map/block/pallas_call | solution.py:306
  30.8 6.2 %all_to_all.20 = bf16[2,32,72,128]{3,2,1,0:T(8,128)(2,1)S(1)} all-to-all(bf16[2,32,72,128]{3,2,1,0:T(8,128)(2,1)S(1)} %bitcast.27), channel_id=1, replica_groups=mesh['y_lo'=4,'core'=2,'x'=4,'y_hi'=2,'z'=8] {'core'}, dimensions={0} | all-to-all | bytes 2359296 | tf_op jit(solution)/shard_map/all_to_all | solution.py:328
  37.0 1.0 fusion
  37.9 14.9 %all-to-all-start.1 = ((bf16[32,72,128]{2,1,0:T(8,128)(2,1)}), bf16[32,72,128]{2,1,0:T(8,128)(2,1)S(1)}, u32[]{:S(2)}, u32[]{:S(2)}) async-start(bf16[32,72,128]{2,1,0:T(8,128)(2,1)} %fusion), calls=%async_computation.1 | async-start | bytes 1179648 | tf_op jit(solution)/shard_map/all_to_all | solution.py:248
  52.9 0.7 collective-permute-start.5
  53.6 3.0 %collective-permute-start.4 = (bf16[3,64,256]{2,1,0:T(8,128)(2,1)S(1)}, bf16[3,64,256]{2,1,0:T(8,128)(2,1)S(1)}, u32[]{:S(2)}, u32[]{:S(2)}) collective-permute-start(bf16[3,64,256]{2,1,0:T(8,128)(2,1)S(1)} %get-tuple-element.54), channel_id=1, source_target_pairs={{0,1},{1,0},{2,3},{3,2},{4,5},{5,4},{6,7},{7,6},{8,9},{9,8},{10,11... | collective-permute-start | bytes 294920 | tf_op jit(solution)/shard_map/ppermute | solution.py:265
  56.6 9.3 %all-to-all-done.1 = bf16[32,72,128]{2,1,0:T(8,128)(2,1)S(1)} async-done(((bf16[32,72,128]{2,1,0:T(8,128)(2,1)}), bf16[32,72,128]{2,1,0:T(8,128)(2,1)S(1)}, u32[]{:S(2)}, u32[]{:S(2)}) %all-to-all-start.1) | async-done | bytes 589856 | tf_op jit(solution)/shard_map/all_to_all | solution.py:248
  65.9 0.1 reduce_sum.24
  66.1 16.1 %all_to_all.21 = bf16[8,72,128]{2,1,0:T(8,128)(2,1)S(1)} all-to-all(bf16[8,72,128]{2,1,0:T(8,128)(2,1)S(1)} %broadcast_in_dim.50), channel_id=1, replica_groups={{0,128,256,384,8,136,264,392},{1,129,257,385,9,137,265,393},{2,130,258,..., dimensions={0} | all-to-all | bytes 294912 | tf_op jit(solution)/shard_map/all_to_all | solution.py:248
  82.2 0.9 broadcast_in_dim.51
  83.1 8.3 %all-to-all-start.3 = ((bf16[32,72,128]{2,1,0:T(8,128)(2,1)}), bf16[32,72,128]{2,1,0:T(8,128)(2,1)S(1)}, u32[]{:S(2)}, u32[]{:S(2)}) async-start(bf16[32,72,128]{2,1,0:T(8,128)(2,1)} %broadcast_in_dim.51), calls=%async_computation.3 | async-start | bytes 1179648 | tf_op jit(solution)/shard_map/all_to_all | solution.py:248
  91.5 3.6 %collective-permute-start.7 = (bf16[12,3,256]{2,1,0:T(4,128)(2,1)S(1)}, bf16[12,3,256]{2,1,0:T(4,128)(2,1)S(1)}, u32[]{:S(2)}, u32[]{:S(2)}) collective-permute-start(bf16[12,3,256]{2,1,0:T(4,128)(2,1)S(1)} %get-tuple-element.63), channel_id=1, source_target_pairs={{64,128},{128,64},{192,256},{256,192},{320,384},{384,320},{448,0},... | collective-permute-start | bytes 55304 | tf_op jit(solution)/shard_map/ppermute | solution.py:280
  95.0 3.7 %collective-permute-start.6 = (bf16[12,3,256]{2,1,0:T(4,128)(2,1)S(1)}, bf16[12,3,256]{2,1,0:T(4,128)(2,1)S(1)}, u32[]{:S(2)}, u32[]{:S(2)}) collective-permute-start(bf16[12,3,256]{2,1,0:T(4,128)(2,1)S(1)} %get-tuple-element.64), channel_id=1, source_target_pairs={{0,64},{64,0},{128,192},{192,128},{256,320},{320,256},{384,448},{4... | collective-permute-start | bytes 55304 | tf_op jit(solution)/shard_map/ppermute | solution.py:281
  98.7 0.8 collective-permute-done.6.near_cols_ref
  99.6 4.8 %all-to-all-done.3.mine_ref = bf16[32,72,128]{2,1,0:T(8,128)(2,1)S(1)} async-done(((bf16[32,72,128]{2,1,0:T(8,128)(2,1)}), bf16[32,72,128]{2,1,0:T(8,128)(2,1)S(1)}, u32[]{:S(2)}, u32[]{:S(2)}) %all-to-all-start.3) | async-done | bytes 589856 | tf_op jit(solution)/shard_map/all_to_all | solution.py:248
  104.4 4.2 %collective-permute-start.8 = (bf16[32,72,128]{2,1,0:T(8,128)(2,1)S(1)}, bf16[32,72,128]{2,1,0:T(8,128)(2,1)S(1)}, u32[]{:S(2)}, u32[]{:S(2)}) collective-permute-start(bf16[32,72,128]{2,1,0:T(8,128)(2,1)S(1)} %all-to-all-done.3.mine_ref), channel_id=1, source_target_pairs={{0,64},{64,0},{1,65},{65,1},{2,66},{66,2},{3,67},{67,3},{4,68},{68... | collective-permute-start | bytes 1769480 | tf_op jit(solution)/shard_map/ppermute | solution.py:347
  108.6 3.4 %state.1 = bf16[6,64,256]{2,1,0:T(8,128)(2,1)} custom-call(s32[2]{0:T(128)S(1)} %pad_add_fusion.odd_ref, bf16[6,64,256]{2,1,0:T(8,128)(2,1)S(1)} %get-tuple-element.30.own_ref, bf16[3,64,256]{2,1,0:T(8,128)(2,1)S(1)} %collective-permute-done.4.near_rows_ref, bf16[3,64,256]{2,1,0:T(8,128)(2,1)S(1)} %collective-permute-done.5.far_rows_ref, ...), custom_call_target="tpu_custom_call" | custom-call | flops 10000000 | bytes 3000000 | tf_op jit(solution)/shard_map/state/pallas_call | solution.py:338
  112.0 1.6 %unpack.1 = (f32[7,7,256]{2,1,0:T(8,128)}, f32[1,256]{1,0:T(1,128)}, f32[1,256]{1,0:T(1,128)}, f32[1,256]{1,0:T(1,128)}, f32[256,1024]{1,0:T(8,128)}, /*index=5*...) custom-call(s32[1]{0:T(128)} %bitcast.1.core_ref, ...), custom_call_target="tpu_custom_call" | custom-call | tf_op jit(solution)/shard_map/unpack/pallas_call | solution.py:351
  (35 shorter events, 0.3 us)
Async XLA Ops:
  0.6 21.3 %copy-start.1 = (bf16[1,6,64,256]{3,2,1,0:T(8,128)(2,1)S(1)}, bf16[1,6,64,256]{3,2,1,0:T(8,128)(2,1)}, u32[]{:S(2)}) copy-start(bf16[1,6,64,256]{3,2,1,0:T(8,128)(2,1)} %param.12) | copy-start | bytes 589828
  0.7 21.3 %copy-start.2 = (f32[7,7,256]{2,1,0:T(8,128)S(1)}, f32[7,7,256]{2,1,0:T(8,128)}, u32[]{:S(2)}) copy-start(f32[7,7,256]{2,1,0:T(8,128)} %k_ref.3) | copy-start | bytes 150532
  0.7 21.3 %copy-start.10 = (f32[256]{0:T(256)S(1)}, f32[256]{0:T(256)}, u32[]{:S(2)}) copy-start(f32[256]{0:T(256)} %param.23) | copy-start | bytes 3076
  0.7 21.3 %copy-start.9 = (f32[256]{0:T(256)S(1)}, f32[256]{0:T(256)}, u32[]{:S(2)}) copy-start(f32[256]{0:T(256)} %param.22) | copy-start | bytes 3076
  0.7 21.3 %copy-start.5 = (f32[1024]{0:T(1024)S(1)}, f32[1024]{0:T(1024)}, u32[]{:S(2)}) copy-start(f32[1024]{0:T(1024)} %param.20) | copy-start | bytes 12292
  0.7 21.3 %copy-start.3 = (bf16[256,1024]{1,0:T(8,128)(2,1)S(1)}, bf16[256,1024]{1,0:T(8,128)(2,1)}, u32[]{:S(2)}) copy-start(bf16[256,1024]{1,0:T(8,128)(2,1)} %w_in_ref.1) | copy-start | bytes 1572868
  0.7 21.3 %copy-start.8 = (f32[256]{0:T(256)S(1)}, f32[256]{0:T(256)}, u32[]{:S(2)}) copy-start(f32[256]{0:T(256)} %param.18) | copy-start | bytes 3076
  0.7 21.3 %copy-start.7 = (f32[256]{0:T(256)S(1)}, f32[256]{0:T(256)}, u32[]{:S(2)}) copy-start(f32[256]{0:T(256)} %param.17) | copy-start | bytes 3076
  0.7 21.3 %copy-start.6 = (f32[256]{0:T(256)S(1)}, f32[256]{0:T(256)}, u32[]{:S(2)}) copy-start(f32[256]{0:T(256)} %param.16) | copy-start | bytes 3076
  1.8 11.5 %collective-permute-start.1 = (bf16[3,64,256]{2,1,0:T(8,128)(2,1)S(1)}, bf16[3,64,256]{2,1,0:T(8,128)(2,1)S(1)}, u32[]{:S(2)}, u32[]{:S(2)}) collective-permute-start(bf16[3,64,256]{2,1,0:T(8,128)(2,1)S(1)} %get-tuple-element.61), channel_id=1, source_target_pairs={{1,2},{2,1},{3,4},{4,3},{5,6},{6,5},{7,8},{8,7},{9,10},{10,9},{11,... | collective-permute-start | bytes 294920 | tf_op jit(solution)/shard_map/ppermute | solution.py:264
  2.5 10.8 %collective-permute-start = (bf16[3,64,256]{2,1,0:T(8,128)(2,1)S(1)}, bf16[3,64,256]{2,1,0:T(8,128)(2,1)S(1)}, u32[]{:S(2)}, u32[]{:S(2)}) collective-permute-start(bf16[3,64,256]{2,1,0:T(8,128)(2,1)S(1)} %get-tuple-element.62), channel_id=1, source_target_pairs={{0,1},{1,0},{2,3},{3,2},{4,5},{5,4},{6,7},{7,6},{8,9},{9,8},{10,11... | collective-permute-start | bytes 294920 | tf_op jit(solution)/shard_map/ppermute | solution.py:265
  13.4 7.6 %collective-permute-start.3 = (bf16[12,3,256]{2,1,0:T(4,128)(2,1)S(1)}, bf16[12,3,256]{2,1,0:T(4,128)(2,1)S(1)}, u32[]{:S(2)}, u32[]{:S(2)}) collective-permute-start(bf16[12,3,256]{2,1,0:T(4,128)(2,1)S(1)} %get-tuple-element.65), channel_id=1, source_target_pairs={{64,128},{128,64},{192,256},{256,192},{320,384},{384,320},{448,0},... | collective-permute-start | bytes 55304 | tf_op jit(solution)/shard_map/ppermute | solution.py:280
  17.7 4.0 %collective-permute-start.2 = (bf16[12,3,256]{2,1,0:T(4,128)(2,1)S(1)}, bf16[12,3,256]{2,1,0:T(4,128)(2,1)S(1)}, u32[]{:S(2)}, u32[]{:S(2)}) collective-permute-start(bf16[12,3,256]{2,1,0:T(4,128)(2,1)S(1)} %get-tuple-element.66), channel_id=1, source_target_pairs={{0,64},{64,0},{128,192},{192,128},{256,320},{320,256},{384,448},{4... | collective-permute-start | bytes 55304 | tf_op jit(solution)/shard_map/ppermute | solution.py:281
  22.0 1.0 copy-start.4
  37.9 28.0 %all-to-all-start.1 = ((bf16[32,72,128]{2,1,0:T(8,128)(2,1)}), bf16[32,72,128]{2,1,0:T(8,128)(2,1)S(1)}, u32[]{:S(2)}, u32[]{:S(2)}) async-start(bf16[32,72,128]{2,1,0:T(8,128)(2,1)} %fusion), calls=%async_computation.1 | async-start | bytes 1179648 | tf_op jit(solution)/shard_map/all_to_all | solution.py:248
  52.9 13.1 %collective-permute-start.5 = (bf16[3,64,256]{2,1,0:T(8,128)(2,1)S(1)}, bf16[3,64,256]{2,1,0:T(8,128)(2,1)S(1)}, u32[]{:S(2)}, u32[]{:S(2)}) collective-permute-start(bf16[3,64,256]{2,1,0:T(8,128)(2,1)S(1)} %get-tuple-element.53), channel_id=1, source_target_pairs={{1,2},{2,1},{3,4},{4,3},{5,6},{6,5},{7,8},{8,7},{9,10},{10,9},{11,... | collective-permute-start | bytes 294920 | tf_op jit(solution)/shard_map/ppermute | solution.py:264
  53.6 12.4 %collective-permute-start.4 = (bf16[3,64,256]{2,1,0:T(8,128)(2,1)S(1)}, bf16[3,64,256]{2,1,0:T(8,128)(2,1)S(1)}, u32[]{:S(2)}, u32[]{:S(2)}) collective-permute-start(bf16[3,64,256]{2,1,0:T(8,128)(2,1)S(1)} %get-tuple-element.54), channel_id=1, source_target_pairs={{0,1},{1,0},{2,3},{3,2},{4,5},{5,4},{6,7},{7,6},{8,9},{9,8},{10,11... | collective-permute-start | bytes 294920 | tf_op jit(solution)/shard_map/ppermute | solution.py:265
  66.0 42.6 %copy-start = (bf16[1,6,64,256]{3,2,1,0:T(8,128)(2,1)S(1)}, bf16[1,6,64,256]{3,2,1,0:T(8,128)(2,1)}, u32[]{:S(2)}) copy-start(bf16[1,6,64,256]{3,2,1,0:T(8,128)(2,1)} %param.14) | copy-start | bytes 589828
  83.1 21.3 %all-to-all-start.3 = ((bf16[32,72,128]{2,1,0:T(8,128)(2,1)}), bf16[32,72,128]{2,1,0:T(8,128)(2,1)S(1)}, u32[]{:S(2)}, u32[]{:S(2)}) async-start(bf16[32,72,128]{2,1,0:T(8,128)(2,1)} %broadcast_in_dim.51), calls=%async_computation.3 | async-start | bytes 1179648 | tf_op jit(solution)/shard_map/all_to_all | solution.py:248
  91.5 7.3 %collective-permute-start.7 = (bf16[12,3,256]{2,1,0:T(4,128)(2,1)S(1)}, bf16[12,3,256]{2,1,0:T(4,128)(2,1)S(1)}, u32[]{:S(2)}, u32[]{:S(2)}) collective-permute-start(bf16[12,3,256]{2,1,0:T(4,128)(2,1)S(1)} %get-tuple-element.63), channel_id=1, source_target_pairs={{64,128},{128,64},{192,256},{256,192},{320,384},{384,320},{448,0},... | collective-permute-start | bytes 55304 | tf_op jit(solution)/shard_map/ppermute | solution.py:280
  95.0 4.5 %collective-permute-start.6 = (bf16[12,3,256]{2,1,0:T(4,128)(2,1)S(1)}, bf16[12,3,256]{2,1,0:T(4,128)(2,1)S(1)}, u32[]{:S(2)}, u32[]{:S(2)}) collective-permute-start(bf16[12,3,256]{2,1,0:T(4,128)(2,1)S(1)} %get-tuple-element.64), channel_id=1, source_target_pairs={{0,64},{64,0},{128,192},{192,128},{256,320},{320,256},{384,448},{4... | collective-permute-start | bytes 55304 | tf_op jit(solution)/shard_map/ppermute | solution.py:281
  104.4 7.6 %collective-permute-start.8 = (bf16[32,72,128]{2,1,0:T(8,128)(2,1)S(1)}, bf16[32,72,128]{2,1,0:T(8,128)(2,1)S(1)}, u32[]{:S(2)}, u32[]{:S(2)}) collective-permute-start(bf16[32,72,128]{2,1,0:T(8,128)(2,1)S(1)} %all-to-all-done.3.mine_ref), channel_id=1, source_target_pairs={{0,64},{64,0},{1,65},{65,1},{2,66},{66,2},{3,67},{67,3},{4,68},{68... | collective-permute-start | bytes 1769480 | tf_op jit(solution)/shard_map/ppermute | solution.py:347

commit v8 on v5

--- a/solution.py
+++ b/solution.py
@@ -52,58 +52,65 @@
 
 
 def convolve(pad_ref, k_ref, out_ref, rows, cols, flip):
+    blocks = 4
     for t in range(2):
         ln = slice(t * LANES, (t + 1) * LANES)
 
         def step(n, carry, t=t, ln=ln):
-            at = pl.multiple_of(n * 8, 8)
-            acc = [jnp.zeros((8, LANES), F32) for _ in range(rows)]
+            at = pl.multiple_of(n * 8 * blocks, 8)
+            acc = [[jnp.zeros((8, LANES), F32) for _ in range(rows)] for _ in range(blocks)]
             for j in range(7):
-                window = [pad_ref[t, r, pl.ds(at + 5 + j, 8), :] for r in range(rows + 6)]
+                window = [
+                    [pad_ref[t, r, pl.ds(at + 8 * b + 5 + j, 8), :] for r in range(rows + 6)] for b in range(blocks)
+                ]
                 for i in range(7):
                     row, col = (6 - i, 6 - j) if flip else (i, j)
                     weight = k_ref[row, col : col + 1, ln]
-                    for p in range(rows):
-                        acc[p] = acc[p] + window[p + i] * weight
-            for p in range(rows):
-                out_ref[t, p, pl.ds(at, 8), :] = acc[p]
+                    for b in range(blocks):
+                        for p in range(rows):
+                            acc[b][p] = acc[b][p] + window[b][p + i] * weight
+            for b in range(blocks):
+                for p in range(rows):
+                    out_ref[t, p, pl.ds(at + 8 * b, 8), :] = acc[b][p]
             return carry
 
-        lax.fori_loop(0, cols // 8, step, 0)
-
-
-def kernel_sums(pad_ref, grad_ref, out_ref, rows, cols):
-    def step(n, carry):
-        t, j = n // 7, n % 7
-        acc = [jnp.zeros((8, LANES), F32) for _ in range(7)]
-        for b in range(cols // 8):
-            window = [pad_ref[t, r, pl.ds(b * 8 + 5 + j, 8), :] for r in range(rows + 6)]
-            grad = [grad_ref[t, p, b * 8 : b * 8 + 8, :] for p in range(rows)]
+        lax.fori_loop(0, cols // (8 * blocks), step, 0)
+
+
+def kernel_sums(pad_ref, grad_ref, small_ref, rows, cols):
+    for t in range(2):
+        for j in range(7):
+            acc = [jnp.zeros((8, LANES), F32) for _ in range(7)]
+            for b in range(cols // 8):
+                window = [pad_ref[t, r, b * 8 + 5 + j : b * 8 + 13 + j, :] for r in range(rows + 6)]
+                grad = [grad_ref[t, p, b * 8 : b * 8 + 8, :] for p in range(rows)]
+                for i in range(7):
+                    part = window[i] * grad[0]
+                    for p in range(1, rows):
+                        part = part + window[p + i] * grad[p]
+                    acc[i] = acc[i] + part
             for i in range(7):
-                for p in range(rows):
-                    acc[i] = acc[i] + window[p + i] * grad[p]
-        for i in range(7):
-            out_ref[t, j, i] = acc[i]
-        return carry
-
-    lax.fori_loop(0, 14, step, 0)
+                at = t * 64 + j * 7 + i
+                small_ref[at : at + 1, :] = jnp.sum(acc[i], axis=0, keepdims=True)
 
 
 def write_chunks(chunk_ref, base, part):
     for n in range(part.shape[0] // BIG_ROWS):
-        chunk_ref[base + n, 0:BIG_ROWS, :] = part[n * BIG_ROWS : (n + 1) * BIG_ROWS]
+        chunk_ref[base + n] = part[n * BIG_ROWS : (n + 1) * BIG_ROWS]
 
 
 def block_kernel(
     odd_ref, own_ref, near_rows_ref, far_rows_ref, near_cols_ref, far_cols_ref, mask_ref, masked_ref, k_ref, dw_bias_ref,
-    gain_ref, bias_ref, w_in_ref, b_in_ref, w_out_ref, b_out_ref, scale_ref,
-    out_ref, grad_ref, chunk_ref,
-    pad_ref, depth_ref, terms_ref, small_ref,
+    gain_ref, bias_ref, w_in_ref, b_in_ref, w_out_hbm_ref, b_out_ref, scale_ref,
+    out_ref, grad_ref, chunk_ref, singles_ref,
+    pad_ref, depth_ref, w_out_ref, w_out_sem,
 ):
     rows, cols, channels = own_ref.shape
     cells = rows * cols
     hidden = w_in_ref.shape[1]
     halves = channels // LANES
+    w_out_copy = pltpu.make_async_copy(w_out_hbm_ref, w_out_ref, w_out_sem)
+    w_out_copy.start()
     fill_padded(odd_ref, pad_ref, own_ref, near_rows_ref, far_rows_ref, near_cols_ref, far_cols_ref)
     convolve(pad_ref, k_ref, depth_ref, rows, cols, False)
     depth = jnp.concatenate([depth_ref[t].reshape(cells, LANES) for t in range(2)], axis=1)
@@ -117,6 +124,7 @@
     branch = jnp.zeros((cells, channels), F32)
     grad_norm = jnp.zeros((cells, channels), F32)
     root = math.sqrt(2.0 / math.pi)
+    w_out_copy.wait()
     b_in_sums = []
     width = channels
     for h in range(hidden // width):
@@ -151,9 +159,6 @@
     grad_depth = (inv_std * (scaled - mean_u - norm_hat * mean_un)).astype(BF16)
     grad_ref[...] = grad_depth.reshape(rows, cols, channels)
     grad_float = grad_depth.astype(F32)
-    for t in range(2):
-        depth_ref[t] = grad_float[:, t * LANES : (t + 1) * LANES].reshape(rows, cols, LANES)
-    kernel_sums(pad_ref, depth_ref, terms_ref, rows, cols)
     singles = b_in_sums + [
         jnp.sum(grad_float, axis=0, keepdims=True),
         jnp.sum(grad_norm * norm_hat, axis=0, keepdims=True),
@@ -161,20 +166,30 @@
         jnp.sum(grad_branch.astype(F32), axis=0, keepdims=True),
         jnp.sum(masked * branch, axis=0, keepdims=True),
     ]
+    for n, single in enumerate(singles):
+        singles_ref[n : n + 1, :] = single
+
+
+def sums_kernel(
+    odd_ref, own_ref, near_rows_ref, far_rows_ref, near_cols_ref, far_cols_ref, grad_ref, singles_ref, out_ref,
+    pad_ref, grad_float_ref, small_ref,
+):
+    rows, cols, _ = own_ref.shape
+    singles = singles_ref.shape[0]
+    fill_padded(odd_ref, pad_ref, own_ref, near_rows_ref, far_rows_ref, near_cols_ref, far_cols_ref)
     for t in range(2):
         ln = slice(t * LANES, (t + 1) * LANES)
-        small_ref[t, 0:49, :] = jnp.sum(terms_ref[t].reshape(49, 8, LANES), axis=1)
-        for n, single in enumerate(singles):
-            small_ref[t, 49 + n : 50 + n, :] = single[:, ln]
-        small_ref[t, 49 + len(singles) :, :] = jnp.zeros((64 - 49 - len(singles), LANES), F32)
-    chunks = chunk_ref.shape[0]
-    for c in range(chunks):
-        n = c % (chunks // 2)
-        if n < 16:
-            piece = small_ref[n // 8, (n % 8) * 8 : (n % 8) * 8 + 8, :].astype(BF16)
-        else:
-            piece = jnp.zeros((8, LANES), BF16)
-        chunk_ref[c, BIG_ROWS:, :] = piece
+        grad_float_ref[t] = grad_ref[:, :, ln].astype(F32)
+        small_ref[t * 64 + 49 : t * 64 + 49 + singles, :] = singles_ref[:, ln]
+        small_ref[t * 64 + 49 + singles : t * 64 + 64, :] = jnp.zeros((15 - singles, LANES), F32)
+    kernel_sums(pad_ref, grad_float_ref, small_ref, rows, cols)
+    out_ref[0:16] = small_ref[...].reshape(16, 8, LANES).astype(BF16)
+    out_ref[16:] = jnp.zeros((out_ref.shape[0] - 16, 8, LANES), BF16)
+
+
+def merge_kernel(pair_ref, small_ref, out_ref):
+    out_ref[:, 0:BIG_ROWS, :] = (pair_ref[0].astype(F32) + pair_ref[1].astype(F32)).astype(BF16)
+    out_ref[:, BIG_ROWS:, :] = small_ref[...]
 
 
 def state_kernel(
@@ -212,7 +227,8 @@
     def _():
         write(other_ref, mine_ref)
 
-    small_ref[...] = mine_ref[0:16, BIG_ROWS:, :].astype(F32).reshape(128, LANES) * factor
+    small = mine_ref[0:16, BIG_ROWS:, :].astype(F32) + other_ref[0:16, BIG_ROWS:, :].astype(F32)
+    small_ref[...] = small.reshape(128, LANES) * factor
     blocks = hidden // channels
     for t in range(2):
         ln = slice(t * LANES, (t + 1) * LANES)
@@ -303,30 +319,48 @@
     cells_scratch = pltpu.VMEM((2, rows, cols, LANES), F32)
     smem, vmem = pl.BlockSpec(memory_space=pltpu.SMEM), pl.BlockSpec(memory_space=pltpu.VMEM)
     params = pltpu.CompilerParams(vmem_limit_bytes=VMEM_BYTES)
-    output, grad_depth, chunks = pl.pallas_call(
+    blocks = hidden // channels
+    output, grad_depth, chunks, singles = pl.pallas_call(
         block_kernel,
         out_shape=(
             jax.ShapeDtypeStruct((rows, cols, channels), BF16),
             jax.ShapeDtypeStruct((rows, cols, channels), BF16),
-            jax.ShapeDtypeStruct((2 * plane, CHUNK_ROWS, LANES), BF16),
+            jax.ShapeDtypeStruct((2 * plane, BIG_ROWS, LANES), BF16),
+            jax.ShapeDtypeStruct((blocks + 5, channels), F32),
         ),
-        in_specs=[smem] + [vmem] * 16,
+        in_specs=[smem] + [vmem] * 13 + [pl.BlockSpec(memory_space=pltpu.HBM)] + [vmem] * 2,
         scratch_shapes=[
             pad,
             cells_scratch,
-            pltpu.VMEM((2, 7, 7, 8, LANES), F32),
-            pltpu.VMEM((2, 64, LANES), F32),
+            pltpu.VMEM(w_out.shape, BF16),
+            pltpu.SemaphoreType.DMA,
         ],
         compiler_params=params,
         cost_estimate=pl.CostEstimate(flops=1300000000, transcendentals=400000, bytes_accessed=6000000),
         name="block",
     )(
         odd, own, near_rows, far_rows, near_cols, far_cols, mask.reshape(cells, channels), masked.reshape(cells, channels), dw_kernel,
-        dw_bias[None], ln_gain[None], ln_bias[None], w_in, b_in[None], w_out, b_out[None], layer_scale[None],
+        dw_bias[None], ln_gain[None], ln_bias[None], w_in, b_in[None], pltpu.with_memory_space_constraint(w_out, pltpu.HBM), b_out[None], layer_scale[None],
     )
     rows_sent = swap_rows(grad_depth, odd_lat)
-    pair = lax.all_to_all(chunks.reshape(2, plane, CHUNK_ROWS, LANES), "core", 0, 0)
-    value = (pair[0].astype(F32) + pair[1].astype(F32)).astype(BF16)
+    small = pl.pallas_call(
+        sums_kernel,
+        out_shape=jax.ShapeDtypeStruct((plane, CHUNK_ROWS - BIG_ROWS, LANES), BF16),
+        in_specs=[smem] + [vmem] * 7,
+        scratch_shapes=[pad, cells_scratch, pltpu.VMEM((128, LANES), F32)],
+        compiler_params=params,
+        cost_estimate=pl.CostEstimate(flops=10000000, transcendentals=0, bytes_accessed=3000000),
+        name="sums",
+    )(odd, own, near_rows, far_rows, near_cols, far_cols, grad_depth, singles)
+    pair = lax.all_to_all(chunks.reshape(2, plane, BIG_ROWS, LANES), "core", 0, 0)
+    pair, small = lax.optimization_barrier((pair, small))
+    value = pl.pallas_call(
+        merge_kernel,
+        out_shape=jax.ShapeDtypeStruct((plane, CHUNK_ROWS, LANES), BF16),
+        compiler_params=params,
+        cost_estimate=pl.CostEstimate(flops=300000, transcendentals=0, bytes_accessed=2000000),
+        name="merge",
+    )(pair, small)
     value = exchange(value, PLANE)
     value = jnp.sum(value.astype(F32), axis=0).astype(BF16)
     value, rows_sent = lax.optimization_barrier((value, rows_sent))

time: 113 us -> 111 us (0.982)
  blocking collectives: 22.3 us -> 16.1 us
  starting transfers between devices: 54.7 us -> 60.3 us
  other arithmetic: 4.16 us -> 1.48 us
  waiting for transfers between devices: 14 us -> 15.6 us
    all_to_all x1 -> x0, blocking collectives: 6.16 us -> none  [local(): lax.all_to_all(chunks.reshape(2, plane, CHUNK_ROWS, LANES), 'core', 0, 0)]
    all_to_all x0 -> x1, starting transfers between devices: none -> 6.1 us  [local(): lax.all_to_all(chunks.reshape(2, plane, BIG_ROWS, LANES), 'core', 0, 0)]
    pallas_call x0 -> x2, Pallas kernels: none -> 2.9 us  [the longest x1 1.96 us: local(): pl.pallas_call(sums_kernel, out_shape=jax.ShapeDtypeStruct((plane, CHUNK_...]
    pallas_call x1, Pallas kernels: 7.76 us -> 5.78 us  [local(): pl.pallas_call(block_kernel, out_shape=(jax.ShapeDtypeStruct((rows, cols,...]
  transfers between devices with their start and end apart: 11 -> 12, of which waited for: 5 -> 6; matrix products, arithmetic and copies ran while one was open for 3% -> 0% of each run, Pallas kernels for 3% -> 4%
where the time goes in v8:
time: 111 us; the launch traced here: 110 us
  starting transfers between devices  60.3 us (54%)
  blocking collectives  16.1 us (15%)
  waiting for transfers between devices  15.6 us (14%)
  Pallas kernels  13 us (12%)
  local copies, waits for them, and re-layouts  2.63 us (2%)
  other arithmetic  1.48 us (1%)
    all_to_all x2, starting transfers between devices, exchange(): return lax.all_to_all(value, EVERY, 0, 0, axis_index_groups=groups)  23.1 us
    all_to_all x1, blocking collectives, exchange(): return lax.all_to_all(value, EVERY, 0, 0, axis_index_groups=groups)  16.1 us
    all_to_all x2, waiting for transfers between devices, exchange(): return lax.all_to_all(value, EVERY, 0, 0, axis_index_groups=groups)  11.5 us
    ppermute x2, starting transfers between devices, swap_rows(): near_rows = lax.ppermute(jnp.where(odd, first, last), LAT, near)  11.1 us
    ppermute x2, starting transfers between devices, swap_cols(): far_cols = lax.ppermute(jnp.where(odd_lon, last, first), LON, far)  8.18 us
    ppermute x2, starting transfers between devices, swap_cols(): near_cols = lax.ppermute(jnp.where(odd_lon, first, last), LON, near)  6.59 us
    all_to_all x1, starting transfers between devices, local(): lax.all_to_all(chunks.reshape(2, plane, BIG_ROWS, LANES), 'core', 0, 0)  6.1 us
    pallas_call x1, Pallas kernels, local(): pl.pallas_call(block_kernel, out_shape=(jax.ShapeDtypeStruct((rows, cols,...  5.78 us
  transfers between devices with their start and end apart: 12, of which 6 were waited for; matrix products, arithmetic and copies ran while one was open for 0% of the time, Pallas kernels for 4%

profile of v8, /device:TPU:1, one launch (start us, length us, event | category | flops | bytes accessed | tf_op | source)
XLA Modules:
  0.0 110.1 jit_solution(14133026312925391730)
XLA Ops:
  0.7 1.0 select_bitcast_fusion
  1.7 0.7 collective-permute-start.1
  2.3 8.2 %collective-permute-start = (bf16[3,64,256]{2,1,0:T(8,128)(2,1)S(1)}, bf16[3,64,256]{2,1,0:T(8,128)(2,1)S(1)}, u32[]{:S(2)}, u32[]{:S(2)}) collective-permute-start(bf16[3,64,256]{2,1,0:T(8,128)(2,1)S(1)} %get-tuple-element.66), channel_id=1, source_target_pairs={{0,1},{1,0},{2,3},{3,2},{4,5},{5,4},{6,7},{7,6},{8,9},{9,8},{10,11... | collective-permute-start | bytes 294920 | tf_op jit(solution)/shard_map/ppermute | solution.py:281
  10.6 0.1 convert_element_type.15
  10.6 0.1 bitcast_multiply_fusion.masked_ref
  10.8 0.8 copy-done
  11.6 0.9 collective-permute-done.near_rows_ref
  12.6 4.9 %collective-permute-start.3 = (bf16[12,3,256]{2,1,0:T(4,128)(2,1)S(1)}, bf16[12,3,256]{2,1,0:T(4,128)(2,1)S(1)}, u32[]{:S(2)}, u32[]{:S(2)}) collective-permute-start(bf16[12,3,256]{2,1,0:T(4,128)(2,1)S(1)} %get-tuple-element.69), channel_id=1, source_target_pairs={{64,128},{128,64},{192,256},{256,192},{320,384},{384,320},{448,0},... | collective-permute-start | bytes 55304 | tf_op jit(solution)/shard_map/ppermute | solution.py:296
  17.5 2.6 %collective-permute-start.2 = (bf16[12,3,256]{2,1,0:T(4,128)(2,1)S(1)}, bf16[12,3,256]{2,1,0:T(4,128)(2,1)S(1)}, u32[]{:S(2)}, u32[]{:S(2)}) collective-permute-start(bf16[12,3,256]{2,1,0:T(4,128)(2,1)S(1)} %get-tuple-element.70), channel_id=1, source_target_pairs={{0,64},{64,0},{128,192},{192,128},{256,320},{320,256},{384,448},{4... | collective-permute-start | bytes 55304 | tf_op jit(solution)/shard_map/ppermute | solution.py:297
  20.2 0.7 collective-permute-done.2.near_cols_ref
  21.0 0.1 broadcast_in_dim.42.mask_ref
  21.1 0.6 copy-done.2
  21.8 5.8 %block.1 = (bf16[6,64,256]{2,1,0:T(8,128)(2,1)}, bf16[6,64,256]{2,1,0:T(8,128)(2,1)S(1)}, bf16[64,64,128]{2,1,0:T(8,128)(2,1)}, f32[9,256]{1,0:T(8,128)S(1)}) custom-call(s32[2]{0:T(128)S(1)} %pad_add_fusion.odd_ref, bf16[6,64,256]{2,1,0:T(8,128)(2,1)S(1)} %bitcast.26, bf16[3,64,256]{2,1,0:T(8,128)(2,1)S(1)} %collective-permute-done.near_rows_ref, ...), custom_call_target="tpu_custom_call" | custom-call | flops 1300000000 | bytes 6000000 | tf_op jit(solution)/shard_map/block/pallas_call | solution.py:323
  27.6 6.1 %all-to-all-start = ((bf16[2,32,64,128]{3,2,1,0:T(8,128)(2,1)}), bf16[2,32,64,128]{3,2,1,0:T(8,128)(2,1)S(1)}, u32[]{:S(2)}, u32[]{:S(2)}) async-start(bf16[2,32,64,128]{3,2,1,0:T(8,128)(2,1)} %bitcast.13), calls=%async_computation | async-start | bytes 2097152 | tf_op jit(solution)/shard_map/all_to_all | solution.py:355
  33.7 2.0 %sums.1.small_ref = bf16[32,8,128]{2,1,0:T(8,128)(2,1)S(1)} custom-call(s32[2]{0:T(128)S(1)} %pad_add_fusion.odd_ref, bf16[6,64,256]{2,1,0:T(8,128)(2,1)S(1)} %bitcast.27, bf16[3,64,256]{2,1,0:T(8,128)(2,1)S(1)} %collective-permute-done.near_rows_ref, bf16[3,64,256]{2,1,0:T(8,128)(2,1)S(1)} %collective-permute-done.1.far_rows_ref, ...), custom_call_target="tpu_custom_call" | custom-call | flops 10000000 | bytes 3000000 | tf_op jit(solution)/shard_map/sums/pallas_call | solution.py:346
  35.7 0.9 merge.1
  36.6 14.9 %all-to-all-start.1 = ((bf16[32,72,128]{2,1,0:T(8,128)(2,1)}), bf16[32,72,128]{2,1,0:T(8,128)(2,1)S(1)}, u32[]{:S(2)}, u32[]{:S(2)}) async-start(bf16[32,72,128]{2,1,0:T(8,128)(2,1)} %merge.1), calls=%async_computation.1 | async-start | bytes 1179648 | tf_op jit(solution)/shard_map/all_to_all | solution.py:264
  51.6 0.7 collective-permute-start.5
  52.3 2.9 %collective-permute-start.4 = (bf16[3,64,256]{2,1,0:T(8,128)(2,1)S(1)}, bf16[3,64,256]{2,1,0:T(8,128)(2,1)S(1)}, u32[]{:S(2)}, u32[]{:S(2)}) collective-permute-start(bf16[3,64,256]{2,1,0:T(8,128)(2,1)S(1)} %get-tuple-element.58), channel_id=1, source_target_pairs={{0,1},{1,0},{2,3},{3,2},{4,5},{5,4},{6,7},{7,6},{8,9},{9,8},{10,11... | collective-permute-start | bytes 294920 | tf_op jit(solution)/shard_map/ppermute | solution.py:281
  55.2 9.4 %all-to-all-done.1 = bf16[32,72,128]{2,1,0:T(8,128)(2,1)S(1)} async-done(((bf16[32,72,128]{2,1,0:T(8,128)(2,1)}), bf16[32,72,128]{2,1,0:T(8,128)(2,1)S(1)}, u32[]{:S(2)}, u32[]{:S(2)}) %all-to-all-start.1) | async-done | bytes 589856 | tf_op jit(solution)/shard_map/all_to_all | solution.py:264
  64.6 0.1 reduce_sum.24
  64.7 16.1 %all_to_all.20 = bf16[8,72,128]{2,1,0:T(8,128)(2,1)S(1)} all-to-all(bf16[8,72,128]{2,1,0:T(8,128)(2,1)S(1)} %broadcast_in_dim.50), channel_id=1, replica_groups={{0,128,256,384,8,136,264,392},{1,129,257,385,9,137,265,393},{2,130,258,..., dimensions={0} | all-to-all | bytes 294912 | tf_op jit(solution)/shard_map/all_to_all | solution.py:264
  80.8 0.9 broadcast_in_dim.51
  81.7 8.2 %all-to-all-start.3 = ((bf16[32,72,128]{2,1,0:T(8,128)(2,1)}), bf16[32,72,128]{2,1,0:T(8,128)(2,1)S(1)}, u32[]{:S(2)}, u32[]{:S(2)}) async-start(bf16[32,72,128]{2,1,0:T(8,128)(2,1)} %broadcast_in_dim.51), calls=%async_computation.3 | async-start | bytes 1179648 | tf_op jit(solution)/shard_map/all_to_all | solution.py:264
  90.0 3.3 %collective-permute-start.7 = (bf16[12,3,256]{2,1,0:T(4,128)(2,1)S(1)}, bf16[12,3,256]{2,1,0:T(4,128)(2,1)S(1)}, u32[]{:S(2)}, u32[]{:S(2)}) collective-permute-start(bf16[12,3,256]{2,1,0:T(4,128)(2,1)S(1)} %get-tuple-element.67), channel_id=1, source_target_pairs={{64,128},{128,64},{192,256},{256,192},{320,384},{384,320},{448,0},... | collective-permute-start | bytes 55304 | tf_op jit(solution)/shard_map/ppermute | solution.py:296
  93.3 4.0 %collective-permute-start.6 = (bf16[12,3,256]{2,1,0:T(4,128)(2,1)S(1)}, bf16[12,3,256]{2,1,0:T(4,128)(2,1)S(1)}, u32[]{:S(2)}, u32[]{:S(2)}) collective-permute-start(bf16[12,3,256]{2,1,0:T(4,128)(2,1)S(1)} %get-tuple-element.68), channel_id=1, source_target_pairs={{0,64},{64,0},{128,192},{192,128},{256,320},{320,256},{384,448},{4... | collective-permute-start | bytes 55304 | tf_op jit(solution)/shard_map/ppermute | solution.py:297
  97.3 0.8 collective-permute-done.6.near_cols_ref
  98.1 2.8 %state.1 = bf16[6,64,256]{2,1,0:T(8,128)(2,1)} custom-call(s32[2]{0:T(128)S(1)} %pad_add_fusion.odd_ref, bf16[6,64,256]{2,1,0:T(8,128)(2,1)S(1)} %get-tuple-element.33.grad_ref.own_ref, bf16[3,64,256]{2,1,0:T(8,128)(2,1)S(1)} %collective-permute-done.4.near_rows_ref, bf16[3,64,256]{2,1,0:T(8,128)(2,1)S(1)} %collective-permute-done.5.far_rows_ref, ...), custom_call_target="tpu_custom_call" | custom-call | flops 10000000 | bytes 3000000 | tf_op jit(solution)/shard_map/state/pallas_call | solution.py:371
  100.9 2.1 %all-to-all-done.3.mine_ref = bf16[32,72,128]{2,1,0:T(8,128)(2,1)S(1)} async-done(((bf16[32,72,128]{2,1,0:T(8,128)(2,1)}), bf16[32,72,128]{2,1,0:T(8,128)(2,1)S(1)}, u32[]{:S(2)}, u32[]{:S(2)}) %all-to-all-start.3) | async-done | bytes 589856 | tf_op jit(solution)/shard_map/all_to_all | solution.py:264
  102.9 3.9 %collective-permute-start.8 = (bf16[32,72,128]{2,1,0:T(8,128)(2,1)S(1)}, bf16[32,72,128]{2,1,0:T(8,128)(2,1)S(1)}, u32[]{:S(2)}, u32[]{:S(2)}) collective-permute-start(bf16[32,72,128]{2,1,0:T(8,128)(2,1)S(1)} %all-to-all-done.3.mine_ref), channel_id=1, source_target_pairs={{0,64},{64,0},{1,65},{65,1},{2,66},{66,2},{3,67},{67,3},{4,68},{68... | collective-permute-start | bytes 1769480 | tf_op jit(solution)/shard_map/ppermute | solution.py:381
  106.9 1.6 %collective-permute-done.8.other_ref = bf16[32,72,128]{2,1,0:T(8,128)(2,1)S(1)} collective-permute-done((bf16[32,72,128]{2,1,0:T(8,128)(2,1)S(1)}, bf16[32,72,128]{2,1,0:T(8,128)(2,1)S(1)}, u32[]{:S(2)}, u32[]{:S(2)}) %collective-permute-start.8) | collective-permute-done | bytes 589856 | tf_op jit(solution)/shard_map/ppermute | solution.py:381
  108.5 1.6 %unpack.1 = (f32[7,7,256]{2,1,0:T(8,128)}, f32[1,256]{1,0:T(1,128)}, f32[1,256]{1,0:T(1,128)}, f32[1,256]{1,0:T(1,128)}, f32[256,1024]{1,0:T(8,128)}, /*index=5*...) custom-call(s32[1]{0:T(128)} %bitcast.1.core_ref, ...), custom_call_target="tpu_custom_call" | custom-call | tf_op jit(solution)/shard_map/unpack/pallas_call | solution.py:385
  (37 shorter events, 0.4 us)
Async XLA Ops:
  0.6 10.0 %copy-start.1 = (bf16[1,6,64,256]{3,2,1,0:T(8,128)(2,1)S(1)}, bf16[1,6,64,256]{3,2,1,0:T(8,128)(2,1)}, u32[]{:S(2)}) copy-start(bf16[1,6,64,256]{3,2,1,0:T(8,128)(2,1)} %param.14) | copy-start | bytes 589828
  1.7 8.9 %copy-start.10 = (s32[1,6,64]{2,0,1:T(1,128)S(1)}, s32[1,6,64]{2,0,1:T(1,128)}, u32[]{:S(2)}) copy-start(s32[1,6,64]{2,0,1:T(1,128)} %param.13) | copy-start | bytes 4612
  1.7 9.9 %collective-permute-start.1 = (bf16[3,64,256]{2,1,0:T(8,128)(2,1)S(1)}, bf16[3,64,256]{2,1,0:T(8,128)(2,1)S(1)}, u32[]{:S(2)}, u32[]{:S(2)}) collective-permute-start(bf16[3,64,256]{2,1,0:T(8,128)(2,1)S(1)} %get-tuple-element.65), channel_id=1, source_target_pairs={{1,2},{2,1},{3,4},{4,3},{5,6},{6,5},{7,8},{8,7},{9,10},{10,9},{11,... | collective-permute-start | bytes 294920 | tf_op jit(solution)/shard_map/ppermute | solution.py:280
  2.3 10.2 %collective-permute-start = (bf16[3,64,256]{2,1,0:T(8,128)(2,1)S(1)}, bf16[3,64,256]{2,1,0:T(8,128)(2,1)S(1)}, u32[]{:S(2)}, u32[]{:S(2)}) collective-permute-start(bf16[3,64,256]{2,1,0:T(8,128)(2,1)S(1)} %get-tuple-element.66), channel_id=1, source_target_pairs={{0,1},{1,0},{2,3},{3,2},{4,5},{5,4},{6,7},{7,6},{8,9},{9,8},{10,11... | collective-permute-start | bytes 294920 | tf_op jit(solution)/shard_map/ppermute | solution.py:281
  10.6 0.9 copy-start
  10.6 10.5 %copy-start.3 = (bf16[256,1024]{1,0:T(8,128)(2,1)S(1)}, bf16[256,1024]{1,0:T(8,128)(2,1)}, u32[]{:S(2)}) copy-start(bf16[256,1024]{1,0:T(8,128)(2,1)} %w_in_ref.1) | copy-start | bytes 1572868
  12.6 7.6 %collective-permute-start.3 = (bf16[12,3,256]{2,1,0:T(4,128)(2,1)S(1)}, bf16[12,3,256]{2,1,0:T(4,128)(2,1)S(1)}, u32[]{:S(2)}, u32[]{:S(2)}) collective-permute-start(bf16[12,3,256]{2,1,0:T(4,128)(2,1)S(1)} %get-tuple-element.69), channel_id=1, source_target_pairs={{64,128},{128,64},{192,256},{256,192},{320,384},{384,320},{448,0},... | collective-permute-start | bytes 55304 | tf_op jit(solution)/shard_map/ppermute | solution.py:296
  17.5 3.5 %collective-permute-start.2 = (bf16[12,3,256]{2,1,0:T(4,128)(2,1)S(1)}, bf16[12,3,256]{2,1,0:T(4,128)(2,1)S(1)}, u32[]{:S(2)}, u32[]{:S(2)}) collective-permute-start(bf16[12,3,256]{2,1,0:T(4,128)(2,1)S(1)} %get-tuple-element.70), channel_id=1, source_target_pairs={{0,64},{64,0},{128,192},{192,128},{256,320},{320,256},{384,448},{4... | collective-permute-start | bytes 55304 | tf_op jit(solution)/shard_map/ppermute | solution.py:297
  21.0 0.8 copy-start.2
  21.0 0.8 copy-start.4
  21.0 0.8 copy-start.5
  21.0 0.8 copy-start.6
  21.0 0.8 copy-start.7
  21.0 0.8 copy-start.8
  21.0 0.8 copy-start.9
  27.6 8.1 %all-to-all-start = ((bf16[2,32,64,128]{3,2,1,0:T(8,128)(2,1)}), bf16[2,32,64,128]{3,2,1,0:T(8,128)(2,1)S(1)}, u32[]{:S(2)}, u32[]{:S(2)}) async-start(bf16[2,32,64,128]{3,2,1,0:T(8,128)(2,1)} %bitcast.13), calls=%async_computation | async-start | bytes 2097152 | tf_op jit(solution)/shard_map/all_to_all | solution.py:355
  36.6 28.0 %all-to-all-start.1 = ((bf16[32,72,128]{2,1,0:T(8,128)(2,1)}), bf16[32,72,128]{2,1,0:T(8,128)(2,1)S(1)}, u32[]{:S(2)}, u32[]{:S(2)}) async-start(bf16[32,72,128]{2,1,0:T(8,128)(2,1)} %merge.1), calls=%async_computation.1 | async-start | bytes 1179648 | tf_op jit(solution)/shard_map/all_to_all | solution.py:264
  51.6 13.1 %collective-permute-start.5 = (bf16[3,64,256]{2,1,0:T(8,128)(2,1)S(1)}, bf16[3,64,256]{2,1,0:T(8,128)(2,1)S(1)}, u32[]{:S(2)}, u32[]{:S(2)}) collective-permute-start(bf16[3,64,256]{2,1,0:T(8,128)(2,1)S(1)} %get-tuple-element.57), channel_id=1, source_target_pairs={{1,2},{2,1},{3,4},{4,3},{5,6},{6,5},{7,8},{8,7},{9,10},{10,9},{11,... | collective-permute-start | bytes 294920 | tf_op jit(solution)/shard_map/ppermute | solution.py:280
  52.3 12.4 %collective-permute-start.4 = (bf16[3,64,256]{2,1,0:T(8,128)(2,1)S(1)}, bf16[3,64,256]{2,1,0:T(8,128)(2,1)S(1)}, u32[]{:S(2)}, u32[]{:S(2)}) collective-permute-start(bf16[3,64,256]{2,1,0:T(8,128)(2,1)S(1)} %get-tuple-element.58), channel_id=1, source_target_pairs={{0,1},{1,0},{2,3},{3,2},{4,5},{5,4},{6,7},{7,6},{8,9},{9,8},{10,11... | collective-permute-start | bytes 294920 | tf_op jit(solution)/shard_map/ppermute | solution.py:281
  81.7 21.2 %all-to-all-start.3 = ((bf16[32,72,128]{2,1,0:T(8,128)(2,1)}), bf16[32,72,128]{2,1,0:T(8,128)(2,1)S(1)}, u32[]{:S(2)}, u32[]{:S(2)}) async-start(bf16[32,72,128]{2,1,0:T(8,128)(2,1)} %broadcast_in_dim.51), calls=%async_computation.3 | async-start | bytes 1179648 | tf_op jit(solution)/shard_map/all_to_all | solution.py:264
  90.0 7.3 %collective-permute-start.7 = (bf16[12,3,256]{2,1,0:T(4,128)(2,1)S(1)}, bf16[12,3,256]{2,1,0:T(4,128)(2,1)S(1)}, u32[]{:S(2)}, u32[]{:S(2)}) collective-permute-start(bf16[12,3,256]{2,1,0:T(4,128)(2,1)S(1)} %get-tuple-element.67), channel_id=1, source_target_pairs={{64,128},{128,64},{192,256},{256,192},{320,384},{384,320},{448,0},... | collective-permute-start | bytes 55304 | tf_op jit(solution)/shard_map/ppermute | solution.py:296
  93.3 4.8 %collective-permute-start.6 = (bf16[12,3,256]{2,1,0:T(4,128)(2,1)S(1)}, bf16[12,3,256]{2,1,0:T(4,128)(2,1)S(1)}, u32[]{:S(2)}, u32[]{:S(2)}) collective-permute-start(bf16[12,3,256]{2,1,0:T(4,128)(2,1)S(1)} %get-tuple-element.68), channel_id=1, source_target_pairs={{0,64},{64,0},{128,192},{192,128},{256,320},{320,256},{384,448},{4... | collective-permute-start | bytes 55304 | tf_op jit(solution)/shard_map/ppermute | solution.py:297
  102.9 5.6 %collective-permute-start.8 = (bf16[32,72,128]{2,1,0:T(8,128)(2,1)S(1)}, bf16[32,72,128]{2,1,0:T(8,128)(2,1)S(1)}, u32[]{:S(2)}, u32[]{:S(2)}) collective-permute-start(bf16[32,72,128]{2,1,0:T(8,128)(2,1)S(1)} %all-to-all-done.3.mine_ref), channel_id=1, source_target_pairs={{0,64},{64,0},{1,65},{65,1},{2,66},{66,2},{3,67},{67,3},{4,68},{68... | collective-permute-start | bytes 1769480 | tf_op jit(solution)/shard_map/ppermute | solution.py:381

commit v9 on v8

--- a/solution.py
+++ b/solution.py
@@ -25,17 +25,20 @@
     return lax.dot_general(a, b, (((ca,), (cb,)), ((), ())), preferred_element_type=F32)
 
 
-def fill_padded(odd_ref, pad_ref, own_ref, near_rows_ref, far_rows_ref, near_cols_ref, far_cols_ref):
-    rows, cols, _ = own_ref.shape
+def fill_rows(odd_ref, pad_ref, own_ref, near_rows_ref, far_rows_ref, parts):
+    rows = own_ref.shape[0]
     low = rows + 3
     near_at = jnp.where(odd_ref[0] == 1, 0, low)
     far_at = low - near_at
     for t in range(2):
         ln = slice(t * LANES, (t + 1) * LANES)
-        pad_ref[t, 3 : 3 + rows, 8 : 8 + cols] = own_ref[:, :, ln].astype(F32)
-        pad_ref[t, pl.ds(near_at, 3), 8 : 8 + cols] = near_rows_ref[:, :, ln].astype(F32)
-        pad_ref[t, pl.ds(far_at, 3), 8 : 8 + cols] = far_rows_ref[:, :, ln].astype(F32)
-
+        for at, end in parts:
+            pad_ref[t, 3 : 3 + rows, 8 + at : 8 + end] = own_ref[:, at:end, ln].astype(F32)
+            pad_ref[t, pl.ds(near_at, 3), 8 + at : 8 + end] = near_rows_ref[:, at:end, ln].astype(F32)
+            pad_ref[t, pl.ds(far_at, 3), 8 + at : 8 + end] = far_rows_ref[:, at:end, ln].astype(F32)
+
+
+def fill_cols(odd_ref, pad_ref, cols, near_cols_ref, far_cols_ref):
     def place(left_ref, right_ref):
         for t in range(2):
             ln = slice(t * LANES, (t + 1) * LANES)
@@ -51,30 +54,42 @@
         place(near_cols_ref, far_cols_ref)
 
 
-def convolve(pad_ref, k_ref, out_ref, rows, cols, flip):
-    blocks = 4
+def fill_padded(odd_ref, pad_ref, own_ref, near_rows_ref, far_rows_ref, near_cols_ref, far_cols_ref):
+    cols = own_ref.shape[1]
+    fill_rows(odd_ref, pad_ref, own_ref, near_rows_ref, far_rows_ref, ((0, cols),))
+    fill_cols(odd_ref, pad_ref, cols, near_cols_ref, far_cols_ref)
+
+
+def convolve(pad_ref, k_ref, out_ref, rows, first, steps, offsets, flip):
+    stride = offsets[-1] + 8
     for t in range(2):
         ln = slice(t * LANES, (t + 1) * LANES)
 
         def step(n, carry, t=t, ln=ln):
-            at = pl.multiple_of(n * 8 * blocks, 8)
-            acc = [[jnp.zeros((8, LANES), F32) for _ in range(rows)] for _ in range(blocks)]
+            at = pl.multiple_of(n * stride, 8)
+            acc = [[jnp.zeros((8, LANES), F32) for _ in range(rows)] for _ in offsets]
             for j in range(7):
                 window = [
-                    [pad_ref[t, r, pl.ds(at + 8 * b + 5 + j, 8), :] for r in range(rows + 6)] for b in range(blocks)
+                    [pad_ref[t, r, pl.ds(at + first + off + 5 + j, 8), :] for r in range(rows + 6)] for off in offsets
                 ]
                 for i in range(7):
                     row, col = (6 - i, 6 - j) if flip else (i, j)
                     weight = k_ref[row, col : col + 1, ln]
-                    for b in range(blocks):
+                    for b in range(len(offsets)):
                         for p in range(rows):
                             acc[b][p] = acc[b][p] + window[b][p + i] * weight
-            for b in range(blocks):
+            for b, off in enumerate(offsets):
                 for p in range(rows):
-                    out_ref[t, p, pl.ds(at + 8 * b, 8), :] = acc[b][p]
+                    out_ref[t, p, pl.ds(at + off, 8), :] = acc[b][p]
             return carry
 
-        lax.fori_loop(0, cols // (8 * blocks), step, 0)
+        lax.fori_loop(0, steps, step, 0)
+
+
+def inner_kernel(odd_ref, own_ref, near_rows_ref, far_rows_ref, k_ref, out_ref, pad_ref):
+    rows, cols, _ = own_ref.shape
+    fill_rows(odd_ref, pad_ref, own_ref, near_rows_ref, far_rows_ref, ((0, cols),))
+    convolve(pad_ref, k_ref, out_ref, rows, 8, 2, (0, 8, 16), False)
 
 
 def kernel_sums(pad_ref, grad_ref, small_ref, rows, cols):
@@ -100,7 +115,7 @@
 
 
 def block_kernel(
-    odd_ref, own_ref, near_rows_ref, far_rows_ref, near_cols_ref, far_cols_ref, mask_ref, masked_ref, k_ref, dw_bias_ref,
+    odd_ref, own_ref, near_rows_ref, far_rows_ref, near_cols_ref, far_cols_ref, inner_ref, mask_ref, masked_ref, k_ref, dw_bias_ref,
     gain_ref, bias_ref, w_in_ref, b_in_ref, w_out_hbm_ref, b_out_ref, scale_ref,
     out_ref, grad_ref, chunk_ref, singles_ref,
     pad_ref, depth_ref, w_out_ref, w_out_sem,
@@ -111,8 +126,10 @@
     halves = channels // LANES
     w_out_copy = pltpu.make_async_copy(w_out_hbm_ref, w_out_ref, w_out_sem)
     w_out_copy.start()
-    fill_padded(odd_ref, pad_ref, own_ref, near_rows_ref, far_rows_ref, near_cols_ref, far_cols_ref)
-    convolve(pad_ref, k_ref, depth_ref, rows, cols, False)
+    fill_rows(odd_ref, pad_ref, own_ref, near_rows_ref, far_rows_ref, ((0, 16), (cols - 16, cols)))
+    fill_cols(odd_ref, pad_ref, cols, near_cols_ref, far_cols_ref)
+    convolve(pad_ref, k_ref, depth_ref, rows, 0, 1, (0, cols - 8), False)
+    depth_ref[:, :, 8 : cols - 8] = inner_ref[...]
     depth = jnp.concatenate([depth_ref[t].reshape(cells, LANES) for t in range(2)], axis=1)
     depth = depth + dw_bias_ref[...]
     center = depth - jnp.mean(depth, axis=-1, keepdims=True)
@@ -197,7 +214,7 @@
 ):
     rows, cols, _ = own_ref.shape
     fill_padded(odd_ref, pad_ref, own_ref, near_rows_ref, far_rows_ref, near_cols_ref, far_cols_ref)
-    convolve(pad_ref, k_ref, sum_ref, rows, cols, True)
+    convolve(pad_ref, k_ref, sum_ref, rows, 0, 2, (0, 8, 16, 24), True)
     for t in range(2):
         ln = slice(t * LANES, (t + 1) * LANES)
         out_ref[:, :, ln] = (cot_ref[:, :, ln].astype(F32) + sum_ref[t]).astype(BF16)
@@ -319,6 +336,15 @@
     cells_scratch = pltpu.VMEM((2, rows, cols, LANES), F32)
     smem, vmem = pl.BlockSpec(memory_space=pltpu.SMEM), pl.BlockSpec(memory_space=pltpu.VMEM)
     params = pltpu.CompilerParams(vmem_limit_bytes=VMEM_BYTES)
+    inner = pl.pallas_call(
+        inner_kernel,
+        out_shape=jax.ShapeDtypeStruct((2, rows, cols - 16, LANES), F32),
+        in_specs=[smem] + [vmem] * 4,
+        scratch_shapes=[pad],
+        compiler_params=params,
+        cost_estimate=pl.CostEstimate(flops=10000000, transcendentals=0, bytes_accessed=2000000),
+        name="inner",
+    )(odd, own, near_rows, far_rows, dw_kernel)
     blocks = hidden // channels
     output, grad_depth, chunks, singles = pl.pallas_call(
         block_kernel,
@@ -328,7 +354,7 @@
             jax.ShapeDtypeStruct((2 * plane, BIG_ROWS, LANES), BF16),
             jax.ShapeDtypeStruct((blocks + 5, channels), F32),
         ),
-        in_specs=[smem] + [vmem] * 13 + [pl.BlockSpec(memory_space=pltpu.HBM)] + [vmem] * 2,
+        in_specs=[smem] + [vmem] * 14 + [pl.BlockSpec(memory_space=pltpu.HBM)] + [vmem] * 2,
         scratch_shapes=[
             pad,
             cells_scratch,
@@ -339,7 +365,7 @@
         cost_estimate=pl.CostEstimate(flops=1300000000, transcendentals=400000, bytes_accessed=6000000),
         name="block",
     )(
-        odd, own, near_rows, far_rows, near_cols, far_cols, mask.reshape(cells, channels), masked.reshape(cells, channels), dw_kernel,
+        odd, own, near_rows, far_rows, near_cols, far_cols, inner, mask.reshape(cells, channels), masked.reshape(cells, channels), dw_kernel,
         dw_bias[None], ln_gain[None], ln_bias[None], w_in, b_in[None], pltpu.with_memory_space_constraint(w_out, pltpu.HBM), b_out[None], layer_scale[None],
     )
     rows_sent = swap_rows(grad_depth, odd_lat)

time: 111 us -> 111 us (level)
  blocking collectives: 16.1 us -> 14.8 us
    pallas_call x0 -> x1, Pallas kernels: none -> 1.81 us  [local(): pl.pallas_call(inner_kernel, out_shape=jax.ShapeDtypeStruct((2, rows, col...]
    all_to_all x1, blocking collectives: 16.1 us -> 14.8 us  [exchange(): return lax.all_to_all(value, EVERY, 0, 0, axis_index_groups=groups)]
    all_to_all x1, starting transfers between devices: 6.1 us -> 4.86 us  [local(): lax.all_to_all(chunks.reshape(2, plane, BIG_ROWS, LANES), 'core', 0, 0)]
    ppermute x2, starting transfers between devices: 8.18 us -> 9.38 us  [swap_cols(): far_cols = lax.ppermute(jnp.where(odd_lon, last, first), LON, far)]
  transfers between devices with their start and end apart: 12 -> 12, of which waited for: 6 -> 5; matrix products, arithmetic and copies ran while one was open for 0% -> 0% of each run, Pallas kernels for 4% -> 6%
where the time goes in v9:
time: 111 us; the launch traced here: 110 us
  starting transfers between devices  61.3 us (55%)
  waiting for transfers between devices  14.8 us (13%)
  blocking collectives  14.8 us (13%)
  Pallas kernels  14.1 us (13%)
  local copies, waits for them, and re-layouts  2.55 us (2%)
  other arithmetic  1.48 us (1%)
    all_to_all x2, starting transfers between devices, exchange(): return lax.all_to_all(value, EVERY, 0, 0, axis_index_groups=groups)  24.2 us
    all_to_all x1, blocking collectives, exchange(): return lax.all_to_all(value, EVERY, 0, 0, axis_index_groups=groups)  14.8 us
    all_to_all x2, waiting for transfers between devices, exchange(): return lax.all_to_all(value, EVERY, 0, 0, axis_index_groups=groups)  11.5 us
    ppermute x2, starting transfers between devices, swap_rows(): near_rows = lax.ppermute(jnp.where(odd, first, last), LAT, near)  11.1 us
    ppermute x2, starting transfers between devices, swap_cols(): far_cols = lax.ppermute(jnp.where(odd_lon, last, first), LON, far)  9.38 us
    ppermute x2, starting transfers between devices, swap_cols(): near_cols = lax.ppermute(jnp.where(odd_lon, first, last), LON, near)  5.52 us
    pallas_call x1, Pallas kernels, local(): pl.pallas_call(block_kernel, out_shape=(jax.ShapeDtypeStruct((rows, cols,...  5.05 us
    ppermute x1, starting transfers between devices, local(): other = lax.ppermute(value, 'core', [(0, 1), (1, 0)])  5.01 us
  transfers between devices with their start and end apart: 12, of which 5 were waited for; matrix products, arithmetic and copies ran while one was open for 0% of the time, Pallas kernels for 6%

profile of v9, /device:TPU:1, one launch (start us, length us, event | category | flops | bytes accessed | tf_op | source)
XLA Modules:
  0.0 110.0 jit_solution(7489355366751529491)
XLA Ops:
  0.7 1.0 select_bitcast_fusion
  1.7 0.7 collective-permute-start.1
  2.3 8.2 %collective-permute-start = (bf16[3,64,256]{2,1,0:T(8,128)(2,1)S(1)}, bf16[3,64,256]{2,1,0:T(8,128)(2,1)S(1)}, u32[]{:S(2)}, u32[]{:S(2)}) collective-permute-start(bf16[3,64,256]{2,1,0:T(8,128)(2,1)S(1)} %get-tuple-element.66), channel_id=1, source_target_pairs={{0,1},{1,0},{2,3},{3,2},{4,5},{5,4},{6,7},{7,6},{8,9},{9,8},{10,11... | collective-permute-start | bytes 294920 | tf_op jit(solution)/shard_map/ppermute | solution.py:298
  10.6 0.1 convert_element_type.15
  10.6 0.1 bitcast_multiply_fusion.masked_ref
  10.8 0.8 copy-done
  11.6 0.9 collective-permute-done.near_rows_ref
  12.6 5.0 %collective-permute-start.3 = (bf16[12,3,256]{2,1,0:T(4,128)(2,1)S(1)}, bf16[12,3,256]{2,1,0:T(4,128)(2,1)S(1)}, u32[]{:S(2)}, u32[]{:S(2)}) collective-permute-start(bf16[12,3,256]{2,1,0:T(4,128)(2,1)S(1)} %get-tuple-element.69), channel_id=1, source_target_pairs={{64,128},{128,64},{192,256},{256,192},{320,384},{384,320},{448,0},... | collective-permute-start | bytes 55304 | tf_op jit(solution)/shard_map/ppermute | solution.py:313
  17.7 2.6 %collective-permute-start.2 = (bf16[12,3,256]{2,1,0:T(4,128)(2,1)S(1)}, bf16[12,3,256]{2,1,0:T(4,128)(2,1)S(1)}, u32[]{:S(2)}, u32[]{:S(2)}) collective-permute-start(bf16[12,3,256]{2,1,0:T(4,128)(2,1)S(1)} %get-tuple-element.70), channel_id=1, source_target_pairs={{0,64},{64,0},{128,192},{192,128},{256,320},{320,256},{384,448},{4... | collective-permute-start | bytes 55304 | tf_op jit(solution)/shard_map/ppermute | solution.py:314
  20.4 1.8 %inner.1.inner_ref = f32[2,6,48,128]{3,2,1,0:T(8,128)S(1)} custom-call(s32[2]{0:T(128)S(1)} %pad_add_fusion.odd_ref, bf16[6,64,256]{2,1,0:T(8,128)(2,1)S(1)} %bitcast.26, bf16[3,64,256]{2,1,0:T(8,128)(2,1)S(1)} %collective-permute-done.near_rows_ref, bf16[3,64,256]{2,1,0:T(8,128)(2,1)S(1)} %collective-permute-done.1.far_rows_ref, f32[7,7,256]{2,1,0:T(8,128)S(1)} %copy-done.2), custom_call_target="tpu_custom_call" | custom-call | flops 10000000 | bytes 2000000 | tf_op jit(solution)/shard_map/inner/pallas_call | solution.py:339
  22.3 0.1 broadcast_in_dim.42.mask_ref
  22.4 0.5 copy-done.4
  23.0 5.0 %block.1 = (bf16[6,64,256]{2,1,0:T(8,128)(2,1)}, bf16[6,64,256]{2,1,0:T(8,128)(2,1)S(1)}, bf16[64,64,128]{2,1,0:T(8,128)(2,1)}, f32[9,256]{1,0:T(8,128)S(1)}) custom-call(s32[2]{0:T(128)S(1)} %pad_add_fusion.odd_ref, bf16[6,64,256]{2,1,0:T(8,128)(2,1)S(1)} %bitcast.27, bf16[3,64,256]{2,1,0:T(8,128)(2,1)S(1)} %collective-permute-done.near_rows_ref, ...), custom_call_target="tpu_custom_call" | custom-call | flops 1300000000 | bytes 6000000 | tf_op jit(solution)/shard_map/block/pallas_call | solution.py:349
  28.0 4.9 %all-to-all-start = ((bf16[2,32,64,128]{3,2,1,0:T(8,128)(2,1)}), bf16[2,32,64,128]{3,2,1,0:T(8,128)(2,1)S(1)}, u32[]{:S(2)}, u32[]{:S(2)}) async-start(bf16[2,32,64,128]{3,2,1,0:T(8,128)(2,1)} %bitcast.13), calls=%async_computation | async-start | bytes 2097152 | tf_op jit(solution)/shard_map/all_to_all | solution.py:381
  32.9 2.0 %sums.1.small_ref = bf16[32,8,128]{2,1,0:T(8,128)(2,1)S(1)} custom-call(s32[2]{0:T(128)S(1)} %pad_add_fusion.odd_ref, bf16[6,64,256]{2,1,0:T(8,128)(2,1)S(1)} %bitcast.28, bf16[3,64,256]{2,1,0:T(8,128)(2,1)S(1)} %collective-permute-done.near_rows_ref, bf16[3,64,256]{2,1,0:T(8,128)(2,1)S(1)} %collective-permute-done.1.far_rows_ref, ...), custom_call_target="tpu_custom_call" | custom-call | flops 10000000 | bytes 3000000 | tf_op jit(solution)/shard_map/sums/pallas_call | solution.py:372
  34.8 0.9 merge.1
  35.8 16.2 %all-to-all-start.1 = ((bf16[32,72,128]{2,1,0:T(8,128)(2,1)}), bf16[32,72,128]{2,1,0:T(8,128)(2,1)S(1)}, u32[]{:S(2)}, u32[]{:S(2)}) async-start(bf16[32,72,128]{2,1,0:T(8,128)(2,1)} %merge.1), calls=%async_computation.1 | async-start | bytes 1179648 | tf_op jit(solution)/shard_map/all_to_all | solution.py:281
  52.0 0.7 collective-permute-start.5
  52.7 2.9 %collective-permute-start.4 = (bf16[3,64,256]{2,1,0:T(8,128)(2,1)S(1)}, bf16[3,64,256]{2,1,0:T(8,128)(2,1)S(1)}, u32[]{:S(2)}, u32[]{:S(2)}) collective-permute-start(bf16[3,64,256]{2,1,0:T(8,128)(2,1)S(1)} %get-tuple-element.58), channel_id=1, source_target_pairs={{0,1},{1,0},{2,3},{3,2},{4,5},{5,4},{6,7},{7,6},{8,9},{9,8},{10,11... | collective-permute-start | bytes 294920 | tf_op jit(solution)/shard_map/ppermute | solution.py:298
  55.6 9.4 %all-to-all-done.1 = bf16[32,72,128]{2,1,0:T(8,128)(2,1)S(1)} async-done(((bf16[32,72,128]{2,1,0:T(8,128)(2,1)}), bf16[32,72,128]{2,1,0:T(8,128)(2,1)S(1)}, u32[]{:S(2)}, u32[]{:S(2)}) %all-to-all-start.1) | async-done | bytes 589856 | tf_op jit(solution)/shard_map/all_to_all | solution.py:281
  65.0 0.1 reduce_sum.24
  65.1 14.8 %all_to_all.20 = bf16[8,72,128]{2,1,0:T(8,128)(2,1)S(1)} all-to-all(bf16[8,72,128]{2,1,0:T(8,128)(2,1)S(1)} %broadcast_in_dim.50), channel_id=1, replica_groups={{0,128,256,384,8,136,264,392},{1,129,257,385,9,137,265,393},{2,130,258,..., dimensions={0} | all-to-all | bytes 294912 | tf_op jit(solution)/shard_map/all_to_all | solution.py:281
  80.0 0.9 broadcast_in_dim.51
  80.8 8.0 %all-to-all-start.3 = ((bf16[32,72,128]{2,1,0:T(8,128)(2,1)}), bf16[32,72,128]{2,1,0:T(8,128)(2,1)S(1)}, u32[]{:S(2)}, u32[]{:S(2)}) async-start(bf16[32,72,128]{2,1,0:T(8,128)(2,1)} %broadcast_in_dim.51), calls=%async_computation.3 | async-start | bytes 1179648 | tf_op jit(solution)/shard_map/all_to_all | solution.py:281
  88.9 4.3 %collective-permute-start.7 = (bf16[12,3,256]{2,1,0:T(4,128)(2,1)S(1)}, bf16[12,3,256]{2,1,0:T(4,128)(2,1)S(1)}, u32[]{:S(2)}, u32[]{:S(2)}) collective-permute-start(bf16[12,3,256]{2,1,0:T(4,128)(2,1)S(1)} %get-tuple-element.67), channel_id=1, source_target_pairs={{64,128},{128,64},{192,256},{256,192},{320,384},{384,320},{448,0},... | collective-permute-start | bytes 55304 | tf_op jit(solution)/shard_map/ppermute | solution.py:313
  93.3 2.9 %collective-permute-start.6 = (bf16[12,3,256]{2,1,0:T(4,128)(2,1)S(1)}, bf16[12,3,256]{2,1,0:T(4,128)(2,1)S(1)}, u32[]{:S(2)}, u32[]{:S(2)}) collective-permute-start(bf16[12,3,256]{2,1,0:T(4,128)(2,1)S(1)} %get-tuple-element.68), channel_id=1, source_target_pairs={{0,64},{64,0},{128,192},{192,128},{256,320},{320,256},{384,448},{4... | collective-permute-start | bytes 55304 | tf_op jit(solution)/shard_map/ppermute | solution.py:314
  96.2 0.8 collective-permute-done.6.near_cols_ref
  97.0 2.8 %state.1 = bf16[6,64,256]{2,1,0:T(8,128)(2,1)} custom-call(s32[2]{0:T(128)S(1)} %pad_add_fusion.odd_ref, bf16[6,64,256]{2,1,0:T(8,128)(2,1)S(1)} %get-tuple-element.33.grad_ref.own_ref, bf16[3,64,256]{2,1,0:T(8,128)(2,1)S(1)} %collective-permute-done.4.near_rows_ref, bf16[3,64,256]{2,1,0:T(8,128)(2,1)S(1)} %collective-permute-done.5.far_rows_ref, ...), custom_call_target="tpu_custom_call" | custom-call | flops 10000000 | bytes 3000000 | tf_op jit(solution)/shard_map/state/pallas_call | solution.py:397
  99.8 2.1 %all-to-all-done.3.mine_ref = bf16[32,72,128]{2,1,0:T(8,128)(2,1)S(1)} async-done(((bf16[32,72,128]{2,1,0:T(8,128)(2,1)}), bf16[32,72,128]{2,1,0:T(8,128)(2,1)S(1)}, u32[]{:S(2)}, u32[]{:S(2)}) %all-to-all-start.3) | async-done | bytes 589856 | tf_op jit(solution)/shard_map/all_to_all | solution.py:281
  101.8 5.0 %collective-permute-start.8 = (bf16[32,72,128]{2,1,0:T(8,128)(2,1)S(1)}, bf16[32,72,128]{2,1,0:T(8,128)(2,1)S(1)}, u32[]{:S(2)}, u32[]{:S(2)}) collective-permute-start(bf16[32,72,128]{2,1,0:T(8,128)(2,1)S(1)} %all-to-all-done.3.mine_ref), channel_id=1, source_target_pairs={{0,64},{64,0},{1,65},{65,1},{2,66},{66,2},{3,67},{67,3},{4,68},{68... | collective-permute-start | bytes 1769480 | tf_op jit(solution)/shard_map/ppermute | solution.py:407
  106.8 1.6 %collective-permute-done.8.other_ref = bf16[32,72,128]{2,1,0:T(8,128)(2,1)S(1)} collective-permute-done((bf16[32,72,128]{2,1,0:T(8,128)(2,1)S(1)}, bf16[32,72,128]{2,1,0:T(8,128)(2,1)S(1)}, u32[]{:S(2)}, u32[]{:S(2)}) %collective-permute-start.8) | collective-permute-done | bytes 589856 | tf_op jit(solution)/shard_map/ppermute | solution.py:407
  108.5 1.6 %unpack.1 = (f32[7,7,256]{2,1,0:T(8,128)}, f32[1,256]{1,0:T(1,128)}, f32[1,256]{1,0:T(1,128)}, f32[1,256]{1,0:T(1,128)}, f32[256,1024]{1,0:T(8,128)}, /*index=5*...) custom-call(s32[1]{0:T(128)} %bitcast.1.core_ref, ...), custom_call_target="tpu_custom_call" | custom-call | tf_op jit(solution)/shard_map/unpack/pallas_call | solution.py:411
  (38 shorter events, 0.5 us)
Async XLA Ops:
  0.6 10.0 %copy-start.1 = (bf16[1,6,64,256]{3,2,1,0:T(8,128)(2,1)S(1)}, bf16[1,6,64,256]{3,2,1,0:T(8,128)(2,1)}, u32[]{:S(2)}) copy-start(bf16[1,6,64,256]{3,2,1,0:T(8,128)(2,1)} %param.14) | copy-start | bytes 589828
  1.7 8.9 %copy-start.10 = (s32[1,6,64]{2,0,1:T(1,128)S(1)}, s32[1,6,64]{2,0,1:T(1,128)}, u32[]{:S(2)}) copy-start(s32[1,6,64]{2,0,1:T(1,128)} %param.13) | copy-start | bytes 4612
  1.7 9.9 %collective-permute-start.1 = (bf16[3,64,256]{2,1,0:T(8,128)(2,1)S(1)}, bf16[3,64,256]{2,1,0:T(8,128)(2,1)S(1)}, u32[]{:S(2)}, u32[]{:S(2)}) collective-permute-start(bf16[3,64,256]{2,1,0:T(8,128)(2,1)S(1)} %get-tuple-element.65), channel_id=1, source_target_pairs={{1,2},{2,1},{3,4},{4,3},{5,6},{6,5},{7,8},{8,7},{9,10},{10,9},{11,... | collective-permute-start | bytes 294920 | tf_op jit(solution)/shard_map/ppermute | solution.py:297
  2.3 10.2 %collective-permute-start = (bf16[3,64,256]{2,1,0:T(8,128)(2,1)S(1)}, bf16[3,64,256]{2,1,0:T(8,128)(2,1)S(1)}, u32[]{:S(2)}, u32[]{:S(2)}) collective-permute-start(bf16[3,64,256]{2,1,0:T(8,128)(2,1)S(1)} %get-tuple-element.66), channel_id=1, source_target_pairs={{0,1},{1,0},{2,3},{3,2},{4,5},{5,4},{6,7},{7,6},{8,9},{9,8},{10,11... | collective-permute-start | bytes 294920 | tf_op jit(solution)/shard_map/ppermute | solution.py:298
  10.6 0.9 copy-start
  12.5 7.8 %copy-start.2 = (f32[7,7,256]{2,1,0:T(8,128)S(1)}, f32[7,7,256]{2,1,0:T(8,128)}, u32[]{:S(2)}) copy-start(f32[7,7,256]{2,1,0:T(8,128)} %k_ref.5) | copy-start | bytes 150532
  12.5 9.8 %copy-start.3 = (bf16[256,1024]{1,0:T(8,128)(2,1)S(1)}, bf16[256,1024]{1,0:T(8,128)(2,1)}, u32[]{:S(2)}) copy-start(bf16[256,1024]{1,0:T(8,128)(2,1)} %w_in_ref.1) | copy-start | bytes 1572868
  12.6 9.6 %collective-permute-start.3 = (bf16[12,3,256]{2,1,0:T(4,128)(2,1)S(1)}, bf16[12,3,256]{2,1,0:T(4,128)(2,1)S(1)}, u32[]{:S(2)}, u32[]{:S(2)}) collective-permute-start(bf16[12,3,256]{2,1,0:T(4,128)(2,1)S(1)} %get-tuple-element.69), channel_id=1, source_target_pairs={{64,128},{128,64},{192,256},{256,192},{320,384},{384,320},{448,0},... | collective-permute-start | bytes 55304 | tf_op jit(solution)/shard_map/ppermute | solution.py:313
  17.7 4.5 %collective-permute-start.2 = (bf16[12,3,256]{2,1,0:T(4,128)(2,1)S(1)}, bf16[12,3,256]{2,1,0:T(4,128)(2,1)S(1)}, u32[]{:S(2)}, u32[]{:S(2)}) collective-permute-start(bf16[12,3,256]{2,1,0:T(4,128)(2,1)S(1)} %get-tuple-element.70), channel_id=1, source_target_pairs={{0,64},{64,0},{128,192},{192,128},{256,320},{320,256},{384,448},{4... | collective-permute-start | bytes 55304 | tf_op jit(solution)/shard_map/ppermute | solution.py:314
  22.2 0.7 copy-start.4
  22.2 0.7 copy-start.5
  22.2 0.7 copy-start.6
  22.2 0.7 copy-start.7
  22.2 0.7 copy-start.8
  22.3 0.7 copy-start.9
  28.0 6.8 %all-to-all-start = ((bf16[2,32,64,128]{3,2,1,0:T(8,128)(2,1)}), bf16[2,32,64,128]{3,2,1,0:T(8,128)(2,1)S(1)}, u32[]{:S(2)}, u32[]{:S(2)}) async-start(bf16[2,32,64,128]{3,2,1,0:T(8,128)(2,1)} %bitcast.13), calls=%async_computation | async-start | bytes 2097152 | tf_op jit(solution)/shard_map/all_to_all | solution.py:381
  35.8 29.2 %all-to-all-start.1 = ((bf16[32,72,128]{2,1,0:T(8,128)(2,1)}), bf16[32,72,128]{2,1,0:T(8,128)(2,1)S(1)}, u32[]{:S(2)}, u32[]{:S(2)}) async-start(bf16[32,72,128]{2,1,0:T(8,128)(2,1)} %merge.1), calls=%async_computation.1 | async-start | bytes 1179648 | tf_op jit(solution)/shard_map/all_to_all | solution.py:281
  52.0 13.1 %collective-permute-start.5 = (bf16[3,64,256]{2,1,0:T(8,128)(2,1)S(1)}, bf16[3,64,256]{2,1,0:T(8,128)(2,1)S(1)}, u32[]{:S(2)}, u32[]{:S(2)}) collective-permute-start(bf16[3,64,256]{2,1,0:T(8,128)(2,1)S(1)} %get-tuple-element.57), channel_id=1, source_target_pairs={{1,2},{2,1},{3,4},{4,3},{5,6},{6,5},{7,8},{8,7},{9,10},{10,9},{11,... | collective-permute-start | bytes 294920 | tf_op jit(solution)/shard_map/ppermute | solution.py:297
  52.7 12.4 %collective-permute-start.4 = (bf16[3,64,256]{2,1,0:T(8,128)(2,1)S(1)}, bf16[3,64,256]{2,1,0:T(8,128)(2,1)S(1)}, u32[]{:S(2)}, u32[]{:S(2)}) collective-permute-start(bf16[3,64,256]{2,1,0:T(8,128)(2,1)S(1)} %get-tuple-element.58), channel_id=1, source_target_pairs={{0,1},{1,0},{2,3},{3,2},{4,5},{5,4},{6,7},{7,6},{8,9},{9,8},{10,11... | collective-permute-start | bytes 294920 | tf_op jit(solution)/shard_map/ppermute | solution.py:298
  80.8 21.0 %all-to-all-start.3 = ((bf16[32,72,128]{2,1,0:T(8,128)(2,1)}), bf16[32,72,128]{2,1,0:T(8,128)(2,1)S(1)}, u32[]{:S(2)}, u32[]{:S(2)}) async-start(bf16[32,72,128]{2,1,0:T(8,128)(2,1)} %broadcast_in_dim.51), calls=%async_computation.3 | async-start | bytes 1179648 | tf_op jit(solution)/shard_map/all_to_all | solution.py:281
  88.9 7.3 %collective-permute-start.7 = (bf16[12,3,256]{2,1,0:T(4,128)(2,1)S(1)}, bf16[12,3,256]{2,1,0:T(4,128)(2,1)S(1)}, u32[]{:S(2)}, u32[]{:S(2)}) collective-permute-start(bf16[12,3,256]{2,1,0:T(4,128)(2,1)S(1)} %get-tuple-element.67), channel_id=1, source_target_pairs={{64,128},{128,64},{192,256},{256,192},{320,384},{384,320},{448,0},... | collective-permute-start | bytes 55304 | tf_op jit(solution)/shard_map/ppermute | solution.py:313
  93.3 3.7 %collective-permute-start.6 = (bf16[12,3,256]{2,1,0:T(4,128)(2,1)S(1)}, bf16[12,3,256]{2,1,0:T(4,128)(2,1)S(1)}, u32[]{:S(2)}, u32[]{:S(2)}) collective-permute-start(bf16[12,3,256]{2,1,0:T(4,128)(2,1)S(1)} %get-tuple-element.68), channel_id=1, source_target_pairs={{0,64},{64,0},{128,192},{192,128},{256,320},{320,256},{384,448},{4... | collective-permute-start | bytes 55304 | tf_op jit(solution)/shard_map/ppermute | solution.py:314
  101.8 6.6 %collective-permute-start.8 = (bf16[32,72,128]{2,1,0:T(8,128)(2,1)S(1)}, bf16[32,72,128]{2,1,0:T(8,128)(2,1)S(1)}, u32[]{:S(2)}, u32[]{:S(2)}) collective-permute-start(bf16[32,72,128]{2,1,0:T(8,128)(2,1)S(1)} %all-to-all-done.3.mine_ref), channel_id=1, source_target_pairs={{0,64},{64,0},{1,65},{65,1},{2,66},{66,2},{3,67},{67,3},{4,68},{68... | collective-permute-start | bytes 1769480 | tf_op jit(solution)/shard_map/ppermute | solution.py:407

commit v10 on v8

--- a/solution.py
+++ b/solution.py
@@ -25,7 +25,7 @@
     return lax.dot_general(a, b, (((ca,), (cb,)), ((), ())), preferred_element_type=F32)
 
 
-def fill_padded(odd_ref, pad_ref, own_ref, near_rows_ref, far_rows_ref, near_cols_ref, far_cols_ref):
+def fill_padded(odd_ref, pad_ref, own_ref, near_rows_ref, far_rows_ref, far_cols_ref, near_cols_ref):
     rows, cols, _ = own_ref.shape
     low = rows + 3
     near_at = jnp.where(odd_ref[0] == 1, 0, low)
@@ -100,7 +100,7 @@
 
 
 def block_kernel(
-    odd_ref, own_ref, near_rows_ref, far_rows_ref, near_cols_ref, far_cols_ref, mask_ref, masked_ref, k_ref, dw_bias_ref,
+    odd_ref, own_ref, near_rows_ref, far_rows_ref, far_cols_ref, near_cols_ref, mask_ref, masked_ref, k_ref, dw_bias_ref,
     gain_ref, bias_ref, w_in_ref, b_in_ref, w_out_hbm_ref, b_out_ref, scale_ref,
     out_ref, grad_ref, chunk_ref, singles_ref,
     pad_ref, depth_ref, w_out_ref, w_out_sem,
@@ -111,7 +111,7 @@
     halves = channels // LANES
     w_out_copy = pltpu.make_async_copy(w_out_hbm_ref, w_out_ref, w_out_sem)
     w_out_copy.start()
-    fill_padded(odd_ref, pad_ref, own_ref, near_rows_ref, far_rows_ref, near_cols_ref, far_cols_ref)
+    fill_padded(odd_ref, pad_ref, own_ref, near_rows_ref, far_rows_ref, far_cols_ref, near_cols_ref)
     convolve(pad_ref, k_ref, depth_ref, rows, cols, False)
     depth = jnp.concatenate([depth_ref[t].reshape(cells, LANES) for t in range(2)], axis=1)
     depth = depth + dw_bias_ref[...]
@@ -171,12 +171,12 @@
 
 
 def sums_kernel(
-    odd_ref, own_ref, near_rows_ref, far_rows_ref, near_cols_ref, far_cols_ref, grad_ref, singles_ref, out_ref,
+    odd_ref, own_ref, near_rows_ref, far_rows_ref, far_cols_ref, near_cols_ref, grad_ref, singles_ref, out_ref,
     pad_ref, grad_float_ref, small_ref,
 ):
     rows, cols, _ = own_ref.shape
     singles = singles_ref.shape[0]
-    fill_padded(odd_ref, pad_ref, own_ref, near_rows_ref, far_rows_ref, near_cols_ref, far_cols_ref)
+    fill_padded(odd_ref, pad_ref, own_ref, near_rows_ref, far_rows_ref, far_cols_ref, near_cols_ref)
     for t in range(2):
         ln = slice(t * LANES, (t + 1) * LANES)
         grad_float_ref[t] = grad_ref[:, :, ln].astype(F32)
@@ -193,10 +193,10 @@
 
 
 def state_kernel(
-    odd_ref, own_ref, near_rows_ref, far_rows_ref, near_cols_ref, far_cols_ref, cot_ref, k_ref, out_ref, pad_ref, sum_ref
+    odd_ref, own_ref, near_rows_ref, far_rows_ref, far_cols_ref, near_cols_ref, cot_ref, k_ref, out_ref, pad_ref, sum_ref
 ):
     rows, cols, _ = own_ref.shape
-    fill_padded(odd_ref, pad_ref, own_ref, near_rows_ref, far_rows_ref, near_cols_ref, far_cols_ref)
+    fill_padded(odd_ref, pad_ref, own_ref, near_rows_ref, far_rows_ref, far_cols_ref, near_cols_ref)
     convolve(pad_ref, k_ref, sum_ref, rows, cols, True)
     for t in range(2):
         ln = slice(t * LANES, (t + 1) * LANES)
@@ -295,7 +295,7 @@
     first, last = strip(0), strip(cols - 3)
     far_cols = lax.ppermute(jnp.where(odd_lon, last, first), LON, far)
     near_cols = lax.ppermute(jnp.where(odd_lon, first, last), LON, near)
-    return near_cols, far_cols
+    return far_cols, near_cols
 
 
 def local(
@@ -312,7 +312,7 @@
     odd = jnp.stack([odd_lat, core]).astype(jnp.int32)
     odd_lat, odd_lon = odd_lat == 1, core == 1
     near_rows, far_rows = swap_rows(own, odd_lat)
-    near_cols, far_cols = swap_cols(own, near_rows, far_rows, odd_lat, odd_lon)
+    far_cols, near_cols = swap_cols(own, near_rows, far_rows, odd_lat, odd_lon)
     mask = jnp.broadcast_to(land_sea[0].astype(BF16)[..., None], cot.shape)
     masked = mask * cot
     pad = pltpu.VMEM((2, rows + 6, cols + 16, LANES), F32)
@@ -339,7 +339,7 @@
         cost_estimate=pl.CostEstimate(flops=1300000000, transcendentals=400000, bytes_accessed=6000000),
         name="block",
     )(
-        odd, own, near_rows, far_rows, near_cols, far_cols, mask.reshape(cells, channels), masked.reshape(cells, channels), dw_kernel,
+        odd, own, near_rows, far_rows, far_cols, near_cols, mask.reshape(cells, channels), masked.reshape(cells, channels), dw_kernel,
         dw_bias[None], ln_gain[None], ln_bias[None], w_in, b_in[None], pltpu.with_memory_space_constraint(w_out, pltpu.HBM), b_out[None], layer_scale[None],
     )
     rows_sent = swap_rows(grad_depth, odd_lat)
@@ -351,7 +351,7 @@
         compiler_params=params,
         cost_estimate=pl.CostEstimate(flops=10000000, transcendentals=0, bytes_accessed=3000000),
         name="sums",
-    )(odd, own, near_rows, far_rows, near_cols, far_cols, grad_depth, singles)
+    )(odd, own, near_rows, far_rows, far_cols, near_cols, grad_depth, singles)
     pair = lax.all_to_all(chunks.reshape(2, plane, BIG_ROWS, LANES), "core", 0, 0)
     pair, small = lax.optimization_barrier((pair, small))
     value = pl.pallas_call(

time: 111 us -> 111 us (level)
  starting transfers between devices: 60.3 us -> 55.9 us
  waiting for transfers between devices: 15.6 us -> 19.6 us
    ppermute x2, waiting for transfers between devices: 0.01 us -> 6.81 us  [swap_cols(): far_cols = lax.ppermute(jnp.where(odd_lon, last, first), LON, far)]
    ppermute x2, starting transfers between devices: 8.18 us -> 5.07 us  [swap_cols(): far_cols = lax.ppermute(jnp.where(odd_lon, last, first), LON, far)]
    ppermute x2, waiting for transfers between devices: 1.56 us -> 0.01 us  [swap_cols(): near_cols = lax.ppermute(jnp.where(odd_lon, first, last), LON, near)]
    all_to_all x2, waiting for transfers between devices: 11.5 us -> 10.3 us  [exchange(): return lax.all_to_all(value, EVERY, 0, 0, axis_index_groups=groups)]
where the time goes in v10:
time: 111 us
  starting transfers between devices  55.9 us (50%)
  waiting for transfers between devices  19.6 us (18%)
  blocking collectives  17.1 us (15%)
  Pallas kernels  13 us (12%)
  local copies, waits for them, and re-layouts  2.63 us (2%)
  other arithmetic  1.48 us (1%)
    all_to_all x2, starting transfers between devices, exchange(): return lax.all_to_all(value, EVERY, 0, 0, axis_index_groups=groups)  22.5 us
    all_to_all x1, blocking collectives, exchange(): return lax.all_to_all(value, EVERY, 0, 0, axis_index_groups=groups)  17.1 us
    ppermute x2, starting transfers between devices, swap_rows(): near_rows = lax.ppermute(jnp.where(odd, first, last), LAT, near)  11.1 us
    all_to_all x2, waiting for transfers between devices, exchange(): return lax.all_to_all(value, EVERY, 0, 0, axis_index_groups=groups)  10.3 us
    ppermute x2, starting transfers between devices, swap_cols(): near_cols = lax.ppermute(jnp.where(odd_lon, first, last), LON, near)  7.42 us
    ppermute x2, waiting for transfers between devices, swap_cols(): far_cols = lax.ppermute(jnp.where(odd_lon, last, first), LON, far)  6.81 us
    pallas_call x1, Pallas kernels, local(): pl.pallas_call(block_kernel, out_shape=(jax.ShapeDtypeStruct((rows, cols,...  5.78 us
    all_to_all x1, starting transfers between devices, local(): lax.all_to_all(chunks.reshape(2, plane, BIG_ROWS, LANES), 'core', 0, 0)  5.4 us
  transfers between devices with their start and end apart: 12, of which 6 were waited for; matrix products, arithmetic and copies ran while one was open for 0% of the time, Pallas kernels for 4%

profile of v10, /device:TPU:1, one launch (start us, length us, event | category | flops | bytes accessed | tf_op | source)
XLA Modules:
  0.0 110.8 jit_solution(2547188835787244898)
XLA Ops:
  0.7 1.0 select_bitcast_fusion
  1.7 0.7 collective-permute-start.1
  2.3 8.2 %collective-permute-start = (bf16[3,64,256]{2,1,0:T(8,128)(2,1)S(1)}, bf16[3,64,256]{2,1,0:T(8,128)(2,1)S(1)}, u32[]{:S(2)}, u32[]{:S(2)}) collective-permute-start(bf16[3,64,256]{2,1,0:T(8,128)(2,1)S(1)} %get-tuple-element.66), channel_id=1, source_target_pairs={{0,1},{1,0},{2,3},{3,2},{4,5},{5,4},{6,7},{7,6},{8,9},{9,8},{10,11... | collective-permute-start | bytes 294920 | tf_op jit(solution)/shard_map/ppermute | solution.py:281
  10.6 0.1 convert_element_type.15
  10.6 0.1 bitcast_multiply_fusion.masked_ref
  10.8 0.8 copy-done
  11.6 0.9 collective-permute-done.near_rows_ref
  12.6 5.1 %collective-permute-start.3 = (bf16[12,3,256]{2,1,0:T(4,128)(2,1)S(1)}, bf16[12,3,256]{2,1,0:T(4,128)(2,1)S(1)}, u32[]{:S(2)}, u32[]{:S(2)}) collective-permute-start(bf16[12,3,256]{2,1,0:T(4,128)(2,1)S(1)} %get-tuple-element.69), channel_id=1, source_target_pairs={{0,64},{64,0},{128,192},{192,128},{256,320},{320,256},{384,448},{4... | collective-permute-start | bytes 55304 | tf_op jit(solution)/shard_map/ppermute | solution.py:297
  17.7 1.9 %collective-permute-start.2 = (bf16[12,3,256]{2,1,0:T(4,128)(2,1)S(1)}, bf16[12,3,256]{2,1,0:T(4,128)(2,1)S(1)}, u32[]{:S(2)}, u32[]{:S(2)}) collective-permute-start(bf16[12,3,256]{2,1,0:T(4,128)(2,1)S(1)} %get-tuple-element.70), channel_id=1, source_target_pairs={{64,128},{128,64},{192,256},{256,192},{320,384},{384,320},{448,0},... | collective-permute-start | bytes 55304 | tf_op jit(solution)/shard_map/ppermute | solution.py:296
  19.7 3.1 %collective-permute-done.2.far_cols_ref = bf16[12,3,256]{2,1,0:T(4,128)(2,1)S(1)} collective-permute-done((bf16[12,3,256]{2,1,0:T(4,128)(2,1)S(1)}, bf16[12,3,256]{2,1,0:T(4,128)(2,1)S(1)}, u32[]{:S(2)}, u32[]{:S(2)}) %collective-permute-start.2) | collective-permute-done | bytes 18464 | tf_op jit(solution)/shard_map/ppermute | solution.py:296
  22.9 0.1 broadcast_in_dim.42.mask_ref
  23.1 0.6 copy-done.2
  23.7 5.8 %block.1 = (bf16[6,64,256]{2,1,0:T(8,128)(2,1)}, bf16[6,64,256]{2,1,0:T(8,128)(2,1)S(1)}, bf16[64,64,128]{2,1,0:T(8,128)(2,1)}, f32[9,256]{1,0:T(8,128)S(1)}) custom-call(s32[2]{0:T(128)S(1)} %pad_add_fusion.odd_ref, bf16[6,64,256]{2,1,0:T(8,128)(2,1)S(1)} %bitcast.26, bf16[3,64,256]{2,1,0:T(8,128)(2,1)S(1)} %collective-permute-done.near_rows_ref, ...), custom_call_target="tpu_custom_call" | custom-call | flops 1300000000 | bytes 6000000 | tf_op jit(solution)/shard_map/block/pallas_call | solution.py:323
  29.5 5.4 %all-to-all-start = ((bf16[2,32,64,128]{3,2,1,0:T(8,128)(2,1)}), bf16[2,32,64,128]{3,2,1,0:T(8,128)(2,1)S(1)}, u32[]{:S(2)}, u32[]{:S(2)}) async-start(bf16[2,32,64,128]{3,2,1,0:T(8,128)(2,1)} %bitcast.13), calls=%async_computation | async-start | bytes 2097152 | tf_op jit(solution)/shard_map/all_to_all | solution.py:355
  34.9 2.0 %sums.1.small_ref = bf16[32,8,128]{2,1,0:T(8,128)(2,1)S(1)} custom-call(s32[2]{0:T(128)S(1)} %pad_add_fusion.odd_ref, bf16[6,64,256]{2,1,0:T(8,128)(2,1)S(1)} %bitcast.27, bf16[3,64,256]{2,1,0:T(8,128)(2,1)S(1)} %collective-permute-done.near_rows_ref, bf16[3,64,256]{2,1,0:T(8,128)(2,1)S(1)} %collective-permute-done.1.far_rows_ref, ...), custom_call_target="tpu_custom_call" | custom-call | flops 10000000 | bytes 3000000 | tf_op jit(solution)/shard_map/sums/pallas_call | solution.py:346
  36.9 0.9 merge.1
  37.8 14.9 %all-to-all-start.1 = ((bf16[32,72,128]{2,1,0:T(8,128)(2,1)}), bf16[32,72,128]{2,1,0:T(8,128)(2,1)S(1)}, u32[]{:S(2)}, u32[]{:S(2)}) async-start(bf16[32,72,128]{2,1,0:T(8,128)(2,1)} %merge.1), calls=%async_computation.1 | async-start | bytes 1179648 | tf_op jit(solution)/shard_map/all_to_all | solution.py:264
  52.8 0.7 collective-permute-start.5
  53.5 2.9 %collective-permute-start.4 = (bf16[3,64,256]{2,1,0:T(8,128)(2,1)S(1)}, bf16[3,64,256]{2,1,0:T(8,128)(2,1)S(1)}, u32[]{:S(2)}, u32[]{:S(2)}) collective-permute-start(bf16[3,64,256]{2,1,0:T(8,128)(2,1)S(1)} %get-tuple-element.58), channel_id=1, source_target_pairs={{0,1},{1,0},{2,3},{3,2},{4,5},{5,4},{6,7},{7,6},{8,9},{9,8},{10,11... | collective-permute-start | bytes 294920 | tf_op jit(solution)/shard_map/ppermute | solution.py:281
  56.4 9.3 %all-to-all-done.1 = bf16[32,72,128]{2,1,0:T(8,128)(2,1)S(1)} async-done(((bf16[32,72,128]{2,1,0:T(8,128)(2,1)}), bf16[32,72,128]{2,1,0:T(8,128)(2,1)S(1)}, u32[]{:S(2)}, u32[]{:S(2)}) %all-to-all-start.1) | async-done | bytes 589856 | tf_op jit(solution)/shard_map/all_to_all | solution.py:264
  65.7 0.1 reduce_sum.24
  65.8 17.1 %all_to_all.20 = bf16[8,72,128]{2,1,0:T(8,128)(2,1)S(1)} all-to-all(bf16[8,72,128]{2,1,0:T(8,128)(2,1)S(1)} %broadcast_in_dim.50), channel_id=1, replica_groups={{0,128,256,384,8,136,264,392},{1,129,257,385,9,137,265,393},{2,130,258,..., dimensions={0} | all-to-all | bytes 294912 | tf_op jit(solution)/shard_map/all_to_all | solution.py:264
  82.9 0.9 broadcast_in_dim.51
  83.8 7.6 %all-to-all-start.3 = ((bf16[32,72,128]{2,1,0:T(8,128)(2,1)}), bf16[32,72,128]{2,1,0:T(8,128)(2,1)S(1)}, u32[]{:S(2)}, u32[]{:S(2)}) async-start(bf16[32,72,128]{2,1,0:T(8,128)(2,1)} %broadcast_in_dim.51), calls=%async_computation.3 | async-start | bytes 1179648 | tf_op jit(solution)/shard_map/all_to_all | solution.py:264
  91.5 2.3 %collective-permute-start.7 = (bf16[12,3,256]{2,1,0:T(4,128)(2,1)S(1)}, bf16[12,3,256]{2,1,0:T(4,128)(2,1)S(1)}, u32[]{:S(2)}, u32[]{:S(2)}) collective-permute-start(bf16[12,3,256]{2,1,0:T(4,128)(2,1)S(1)} %get-tuple-element.67), channel_id=1, source_target_pairs={{0,64},{64,0},{128,192},{192,128},{256,320},{320,256},{384,448},{4... | collective-permute-start | bytes 55304 | tf_op jit(solution)/shard_map/ppermute | solution.py:297
  93.8 3.2 %collective-permute-start.6 = (bf16[12,3,256]{2,1,0:T(4,128)(2,1)S(1)}, bf16[12,3,256]{2,1,0:T(4,128)(2,1)S(1)}, u32[]{:S(2)}, u32[]{:S(2)}) collective-permute-start(bf16[12,3,256]{2,1,0:T(4,128)(2,1)S(1)} %get-tuple-element.68), channel_id=1, source_target_pairs={{64,128},{128,64},{192,256},{256,192},{320,384},{384,320},{448,0},... | collective-permute-start | bytes 55304 | tf_op jit(solution)/shard_map/ppermute | solution.py:296
  97.0 3.7 %collective-permute-done.6.far_cols_ref = bf16[12,3,256]{2,1,0:T(4,128)(2,1)S(1)} collective-permute-done((bf16[12,3,256]{2,1,0:T(4,128)(2,1)S(1)}, bf16[12,3,256]{2,1,0:T(4,128)(2,1)S(1)}, u32[]{:S(2)}, u32[]{:S(2)}) %collective-permute-start.6) | collective-permute-done | bytes 18464 | tf_op jit(solution)/shard_map/ppermute | solution.py:296
  100.7 2.8 %state.1 = bf16[6,64,256]{2,1,0:T(8,128)(2,1)} custom-call(s32[2]{0:T(128)S(1)} %pad_add_fusion.odd_ref, bf16[6,64,256]{2,1,0:T(8,128)(2,1)S(1)} %get-tuple-element.33.grad_ref.own_ref, bf16[3,64,256]{2,1,0:T(8,128)(2,1)S(1)} %collective-permute-done.4.near_rows_ref, bf16[3,64,256]{2,1,0:T(8,128)(2,1)S(1)} %collective-permute-done.5.far_rows_ref, ...), custom_call_target="tpu_custom_call" | custom-call | flops 10000000 | bytes 3000000 | tf_op jit(solution)/shard_map/state/pallas_call | solution.py:371
  103.4 1.0 all-to-all-done.3.mine_ref
  104.4 3.1 %collective-permute-start.8 = (bf16[32,72,128]{2,1,0:T(8,128)(2,1)S(1)}, bf16[32,72,128]{2,1,0:T(8,128)(2,1)S(1)}, u32[]{:S(2)}, u32[]{:S(2)}) collective-permute-start(bf16[32,72,128]{2,1,0:T(8,128)(2,1)S(1)} %all-to-all-done.3.mine_ref), channel_id=1, source_target_pairs={{0,64},{64,0},{1,65},{65,1},{2,66},{66,2},{3,67},{67,3},{4,68},{68... | collective-permute-start | bytes 1769480 | tf_op jit(solution)/shard_map/ppermute | solution.py:381
  107.6 1.6 %collective-permute-done.8.other_ref = bf16[32,72,128]{2,1,0:T(8,128)(2,1)S(1)} collective-permute-done((bf16[32,72,128]{2,1,0:T(8,128)(2,1)S(1)}, bf16[32,72,128]{2,1,0:T(8,128)(2,1)S(1)}, u32[]{:S(2)}, u32[]{:S(2)}) %collective-permute-start.8) | collective-permute-done | bytes 589856 | tf_op jit(solution)/shard_map/ppermute | solution.py:381
  109.2 1.6 %unpack.1 = (f32[7,7,256]{2,1,0:T(8,128)}, f32[1,256]{1,0:T(1,128)}, f32[1,256]{1,0:T(1,128)}, f32[1,256]{1,0:T(1,128)}, f32[256,1024]{1,0:T(8,128)}, /*index=5*...) custom-call(s32[1]{0:T(128)} %bitcast.1.core_ref, ...), custom_call_target="tpu_custom_call" | custom-call | tf_op jit(solution)/shard_map/unpack/pallas_call | solution.py:385
  (37 shorter events, 0.4 us)
Async XLA Ops:
  0.6 10.0 %copy-start.1 = (bf16[1,6,64,256]{3,2,1,0:T(8,128)(2,1)S(1)}, bf16[1,6,64,256]{3,2,1,0:T(8,128)(2,1)}, u32[]{:S(2)}) copy-start(bf16[1,6,64,256]{3,2,1,0:T(8,128)(2,1)} %param.14) | copy-start | bytes 589828
  1.7 8.9 %copy-start.10 = (s32[1,6,64]{2,0,1:T(1,128)S(1)}, s32[1,6,64]{2,0,1:T(1,128)}, u32[]{:S(2)}) copy-start(s32[1,6,64]{2,0,1:T(1,128)} %param.13) | copy-start | bytes 4612
  1.7 9.9 %collective-permute-start.1 = (bf16[3,64,256]{2,1,0:T(8,128)(2,1)S(1)}, bf16[3,64,256]{2,1,0:T(8,128)(2,1)S(1)}, u32[]{:S(2)}, u32[]{:S(2)}) collective-permute-start(bf16[3,64,256]{2,1,0:T(8,128)(2,1)S(1)} %get-tuple-element.65), channel_id=1, source_target_pairs={{1,2},{2,1},{3,4},{4,3},{5,6},{6,5},{7,8},{8,7},{9,10},{10,9},{11,... | collective-permute-start | bytes 294920 | tf_op jit(solution)/shard_map/ppermute | solution.py:280
  2.3 10.2 %collective-permute-start = (bf16[3,64,256]{2,1,0:T(8,128)(2,1)S(1)}, bf16[3,64,256]{2,1,0:T(8,128)(2,1)S(1)}, u32[]{:S(2)}, u32[]{:S(2)}) collective-permute-start(bf16[3,64,256]{2,1,0:T(8,128)(2,1)S(1)} %get-tuple-element.66), channel_id=1, source_target_pairs={{0,1},{1,0},{2,3},{3,2},{4,5},{5,4},{6,7},{7,6},{8,9},{9,8},{10,11... | collective-permute-start | bytes 294920 | tf_op jit(solution)/shard_map/ppermute | solution.py:281
  10.6 0.9 copy-start
  10.6 12.4 %copy-start.3 = (bf16[256,1024]{1,0:T(8,128)(2,1)S(1)}, bf16[256,1024]{1,0:T(8,128)(2,1)}, u32[]{:S(2)}) copy-start(bf16[256,1024]{1,0:T(8,128)(2,1)} %w_in_ref.1) | copy-start | bytes 1572868
  12.6 7.2 %collective-permute-start.3 = (bf16[12,3,256]{2,1,0:T(4,128)(2,1)S(1)}, bf16[12,3,256]{2,1,0:T(4,128)(2,1)S(1)}, u32[]{:S(2)}, u32[]{:S(2)}) collective-permute-start(bf16[12,3,256]{2,1,0:T(4,128)(2,1)S(1)} %get-tuple-element.69), channel_id=1, source_target_pairs={{0,64},{64,0},{128,192},{192,128},{256,320},{320,256},{384,448},{4... | collective-permute-start | bytes 55304 | tf_op jit(solution)/shard_map/ppermute | solution.py:297
  17.7 5.1 %collective-permute-start.2 = (bf16[12,3,256]{2,1,0:T(4,128)(2,1)S(1)}, bf16[12,3,256]{2,1,0:T(4,128)(2,1)S(1)}, u32[]{:S(2)}, u32[]{:S(2)}) collective-permute-start(bf16[12,3,256]{2,1,0:T(4,128)(2,1)S(1)} %get-tuple-element.70), channel_id=1, source_target_pairs={{64,128},{128,64},{192,256},{256,192},{320,384},{384,320},{448,0},... | collective-permute-start | bytes 55304 | tf_op jit(solution)/shard_map/ppermute | solution.py:296
  22.9 0.8 copy-start.2
  22.9 0.8 copy-start.4
  22.9 0.8 copy-start.5
  22.9 0.8 copy-start.6
  22.9 0.8 copy-start.7
  22.9 0.8 copy-start.8
  22.9 0.8 copy-start.9
  29.5 7.4 %all-to-all-start = ((bf16[2,32,64,128]{3,2,1,0:T(8,128)(2,1)}), bf16[2,32,64,128]{3,2,1,0:T(8,128)(2,1)S(1)}, u32[]{:S(2)}, u32[]{:S(2)}) async-start(bf16[2,32,64,128]{3,2,1,0:T(8,128)(2,1)} %bitcast.13), calls=%async_computation | async-start | bytes 2097152 | tf_op jit(solution)/shard_map/all_to_all | solution.py:355
  37.8 27.8 %all-to-all-start.1 = ((bf16[32,72,128]{2,1,0:T(8,128)(2,1)}), bf16[32,72,128]{2,1,0:T(8,128)(2,1)S(1)}, u32[]{:S(2)}, u32[]{:S(2)}) async-start(bf16[32,72,128]{2,1,0:T(8,128)(2,1)} %merge.1), calls=%async_computation.1 | async-start | bytes 1179648 | tf_op jit(solution)/shard_map/all_to_all | solution.py:264
  52.8 13.0 %collective-permute-start.5 = (bf16[3,64,256]{2,1,0:T(8,128)(2,1)S(1)}, bf16[3,64,256]{2,1,0:T(8,128)(2,1)S(1)}, u32[]{:S(2)}, u32[]{:S(2)}) collective-permute-start(bf16[3,64,256]{2,1,0:T(8,128)(2,1)S(1)} %get-tuple-element.57), channel_id=1, source_target_pairs={{1,2},{2,1},{3,4},{4,3},{5,6},{6,5},{7,8},{8,7},{9,10},{10,9},{11,... | collective-permute-start | bytes 294920 | tf_op jit(solution)/shard_map/ppermute | solution.py:280
  53.5 12.3 %collective-permute-start.4 = (bf16[3,64,256]{2,1,0:T(8,128)(2,1)S(1)}, bf16[3,64,256]{2,1,0:T(8,128)(2,1)S(1)}, u32[]{:S(2)}, u32[]{:S(2)}) collective-permute-start(bf16[3,64,256]{2,1,0:T(8,128)(2,1)S(1)} %get-tuple-element.58), channel_id=1, source_target_pairs={{0,1},{1,0},{2,3},{3,2},{4,5},{5,4},{6,7},{7,6},{8,9},{9,8},{10,11... | collective-permute-start | bytes 294920 | tf_op jit(solution)/shard_map/ppermute | solution.py:281
  83.8 20.6 %all-to-all-start.3 = ((bf16[32,72,128]{2,1,0:T(8,128)(2,1)}), bf16[32,72,128]{2,1,0:T(8,128)(2,1)S(1)}, u32[]{:S(2)}, u32[]{:S(2)}) async-start(bf16[32,72,128]{2,1,0:T(8,128)(2,1)} %broadcast_in_dim.51), calls=%async_computation.3 | async-start | bytes 1179648 | tf_op jit(solution)/shard_map/all_to_all | solution.py:264
  91.5 5.5 %collective-permute-start.7 = (bf16[12,3,256]{2,1,0:T(4,128)(2,1)S(1)}, bf16[12,3,256]{2,1,0:T(4,128)(2,1)S(1)}, u32[]{:S(2)}, u32[]{:S(2)}) collective-permute-start(bf16[12,3,256]{2,1,0:T(4,128)(2,1)S(1)} %get-tuple-element.67), channel_id=1, source_target_pairs={{0,64},{64,0},{128,192},{192,128},{256,320},{320,256},{384,448},{4... | collective-permute-start | bytes 55304 | tf_op jit(solution)/shard_map/ppermute | solution.py:297
  93.8 6.8 %collective-permute-start.6 = (bf16[12,3,256]{2,1,0:T(4,128)(2,1)S(1)}, bf16[12,3,256]{2,1,0:T(4,128)(2,1)S(1)}, u32[]{:S(2)}, u32[]{:S(2)}) collective-permute-start(bf16[12,3,256]{2,1,0:T(4,128)(2,1)S(1)} %get-tuple-element.68), channel_id=1, source_target_pairs={{64,128},{128,64},{192,256},{256,192},{320,384},{384,320},{448,0},... | collective-permute-start | bytes 55304 | tf_op jit(solution)/shard_map/ppermute | solution.py:296
  104.4 4.7 %collective-permute-start.8 = (bf16[32,72,128]{2,1,0:T(8,128)(2,1)S(1)}, bf16[32,72,128]{2,1,0:T(8,128)(2,1)S(1)}, u32[]{:S(2)}, u32[]{:S(2)}) collective-permute-start(bf16[32,72,128]{2,1,0:T(8,128)(2,1)S(1)} %all-to-all-done.3.mine_ref), channel_id=1, source_target_pairs={{0,64},{64,0},{1,65},{65,1},{2,66},{66,2},{3,67},{67,3},{4,68},{68... | collective-permute-start | bytes 1769480 | tf_op jit(solution)/shard_map/ppermute | solution.py:381
